TPU v7x, 128 devices: a whole 4x4x4 slice. The times are simulated.
128 devices in a mesh: sample: 2 (over core), sx: 8 (over z_hi, y), sy: 8 (over x, z_lo).
Axes of the slice: x: 4, y: 4, z: 4 (z_hi: 2, z_lo: 2; z = z_hi * 2 + z_lo), core: 2. Of those that a mesh axis runs over, the one named last changes fastest.
Arguments:
- features: bfloat16 [32, 4, 32, 32, 256], P('sx', 'sample', 'sy'), may hold values from -6 to 6
- kernel: bfloat16 [3, 3, 3, 256, 256], P(None, None, None, 'sx', 'sy'), may hold values from -0.078125 to 0.078125
- filter_bias: bfloat16 [256], P('sy'), may hold values from -3 to 3
- cotangent: bfloat16 [32, 4, 32, 32, 256], P('sx', 'sample', None, None, 'sy'), may hold values from -6 to 6
Outputs:
- output: bfloat16 [32, 4, 32, 32, 256], P('sx', 'sample', None, None, 'sy')
- input_grad: bfloat16 [32, 4, 32, 32, 256], P('sx', 'sample', 'sy')
- kernel_grad: float32 [3, 3, 3, 256, 256], P(None, None, None, 'sx', 'sy')
All inputs are finite; a program needn't handle non-finite values.
Results may differ from a plain program's by a relative error of at most 0.014.
Values may be sent and summed in bfloat16 or wider, within the bound.
No kernel may reach another device: no remote copies, remote signals or barrier semaphores. Data moves between devices by JAX's collectives and lax.ppermute only.
A program may use at most 128 MiB of HBM per device.

v0:
```python
import jax
import jax.numpy as jnp
from jax import lax
from jax.sharding import PartitionSpec as P


def padded_2(array, sides, width):
    for axis, dim in sides:
        size, length = (lax.axis_size(axis), array.shape[dim])
        up = [(i, (i + 1) % size) for i in range(size - 1)]
        down = [(j, i) for i, j in up]
        last = lax.slice_in_dim(array, length - width, length, axis=dim)
        leading = lax.slice_in_dim(array, 0, width, axis=dim)
        before = lax.ppermute(last, axis, up)
        after = lax.ppermute(leading, axis, down)
        array = jnp.concatenate([before, array, after], axis=dim)
    return array


def slope_of(hidden):
    gate = jax.nn.sigmoid(hidden)
    return gate * (1.0 + hidden * (1.0 - gate))


def convolve(inputs, weights, pads, layout):
    return lax.conv_general_dilated(
        inputs,
        weights,
        (1, 1, 1),
        pads,
        dimension_numbers=layout,
        preferred_element_type=jnp.float32,
    )


def forward_conv(inputs, weights):
    return convolve(inputs, weights, ((0, 0), (0, 0), (0, 0)), ("DNHWC", "DHWIO", "DNHWC"))


def kernel_grad_of(window, grad_pre):
    return convolve(window, grad_pre, ((0, 0), (0, 0), (0, 0)), ("DCHWN", "DIHWO", "DHWNC"))


def local(features, kernel, filter_bias, cotangent):
    kernel_full = lax.all_gather(kernel, "sx", axis=3, tiled=True)
    edged = padded_2(features, (("sx", 0),), 1)
    band = lax.all_gather(edged, "sy", axis=2, tiled=True)
    padded = jnp.pad(band, ((0, 0), (0, 0), (1, 1), (1, 1), (0, 0)))
    hidden = forward_conv(padded, kernel_full) + filter_bias.astype(jnp.float32)
    output = jax.nn.silu(hidden).astype(jnp.bfloat16)
    grad_pre = (cotangent.astype(jnp.float32) * slope_of(hidden)).astype(jnp.bfloat16)
    grad_band = padded_2(grad_pre, (("sx", 0),), 1)
    grad_padded = jnp.pad(grad_band, ((0, 0), (0, 0), (1, 1), (1, 1), (0, 0)))
    flipped = kernel_full[::-1, ::-1, ::-1]
    partial_grad = convolve(
        grad_padded, flipped, ((0, 0), (0, 0), (0, 0)), ("DNHWC", "DHWOI", "DNHWC")
    )
    input_grad = lax.psum_scatter(
        partial_grad.astype(jnp.bfloat16), "sy", scatter_dimension=2, tiled=True
    )
    local_grad = kernel_grad_of(padded, grad_pre)
    weight_sum = lax.psum_scatter(
        local_grad.astype(jnp.bfloat16), "sx", scatter_dimension=3, tiled=True
    )
    kernel_grad = lax.psum(weight_sum, "sample").astype(jnp.float32)
    return (output, input_grad, kernel_grad)


def solution(mesh):
    return jax.shard_map(
        local,
        mesh=mesh,
        in_specs=(
            P("sx", "sample", "sy", None, None),
            P(None, None, None, "sx", "sy"),
            P("sy"),
            P("sx", "sample", None, None, "sy"),
        ),
        out_specs=(
            P("sx", "sample", None, None, "sy"),
            P("sx", "sample", "sy", None, None),
            P(None, None, None, "sx", "sy"),
        ),
        check_vma=False,
    )
```

profile of v0, /device:TPU:3, one launch (start us, length us, event | category | flops | bytes accessed | tf_op | source)
XLA Modules:
  0.0 489.5 jit_solution(8424084960163487004)
XLA Ops:
  7.2 1.6 copy.28
  9.0 3.2 collective-permute-start
  12.2 1.3 collective-permute-start.1
  14.3 3.6 collective-permute-done.1
  17.9 2.1 pad_maximum_fusion
  20.7 37.3 %all_gather.7 = bf16[3,3,3,256,32]{4,3,2,1,0:T(8,128)(2,1)S(1)} all-gather(bf16[3,3,3,32,32]{4,3,2,1,0:T(8,128)(2,1)} %param.5), channel_id=1, replica_groups=mesh['sample'=2,'sx'=8,'sy'=8] {'sx'}, dimensions={3}, use_global_device_ids=true | all-gather | bytes 497664 | tf_op jit(solution)/shard_map/all_gather | solution.py:45
  58.1 111.8 %all-gather.2.cloned.1.call-done = bf16[6,2,32,32,256]{4,1,3,2,0:T(2,128)(2,1)} async-done(((bf16[6,2,4,32,256]{4,1,3,2,0:T(2,128)(2,1)}), bf16[6,2,32,32,256]{4,1,3,2,0:T(2,128)(2,1)}) %all-gather.2.cloned.1.call-update) | async-done | bytes 6291472 | tf_op jit(solution)/shard_map/all_gather | solution.py:47
  169.9 9.7 %pad.4 = bf16[6,32,2,40,256]{4,2,3,1,0:T(2,128)(2,1)S(1)} pad(bf16[6,32,2,32,256]{4,2,3,1,0:T(2,128)(2,1)} %bitcast.37, bf16[]{:T(256)} %constant.8), padding=0_0x0_0x0_0x1_7x0_0 | pad | bytes 14155778 | tf_op jit(solution)/shard_map/all_gather | solution.py:47
  179.6 4.7 copy.32
  184.3 2.8 slice.23
  187.2 42.3 %add_multiply_fusion = (f32[4,32,16,5,32]{4,2,3,1,0:T(8,128)S(1)}, bf16[4,32,16,5,32]{4,2,3,1,0:T(8,128)(2,1)}) fusion(f32[32]{0:T(128)S(1)} %convert_element_type.25, pred[16,5]{0,1:T(8,128)(4,1)S(1)} %copy-done.4, bf16[3,3,3,256,32]{4,3,2,1,0:T(8,128)(2,1)S(1)} %all_gather.7, bf16[6,32,2,7,2,256]{5,3,2,4,1,0:T(8,128)(2,1)S(1)} %slice.23, ...), kind=kOutput, calls=%fused_computation.16 | convolution fusion | flops 4472111104 | bytes 13025488 | tf_op jit(solution)/shard_map/conv_general_dilated | solution.py:26
  229.5 1.6 copy.35
  233.3 2.1 collective-permute-start.2
  235.4 1.3 collective-permute-start.3
  236.7 75.1 %fusion.20 = bf16[3,3,3,256,32]{4,3,2,1,0:T(8,128)(2,1)} fusion(bf16[6,2,32,32,256]{4,1,3,2,0:T(2,128)(2,1)S(1)} %bitcast.39, bf16[4,2,32,32,32]{4,2,3,1,0:T(8,128)(2,1)S(1)} %fusion.15), kind=kOutput, calls=%fused_computation.28 | convolution fusion | flops 3474677760 | bytes 7258112 | tf_op jit(solution)/shard_map/conv_general_dilated | solution.py:26
  312.0 1.9 maximum_bitcast_fusion
  316.7 10.1 %select_convert_fusion = bf16[4,32,16,5,256]{4,2,3,1,0:T(8,128)(2,1)S(1)} fusion(pred[16,5]{0,1:T(8,128)(4,1)S(1)} %copy-done.5, bf16[3,3,3,256,32]{4,3,2,1,0:T(8,128)(2,1)S(1)} %copy-done.3, bf16[6,32,2,8,7,32]{5,1,4,3,2,0:T(8,128)(2,1)S(1)} %fusion.9), kind=kOutput, calls=%fused_computation.10 | convolution fusion | flops 4440719360 | bytes 7061584 | tf_op jit(solution)/shard_map/conv_general_dilated | solution.py:26
  326.8 2.0 copy.37
  329.3 4.4 copy.38
  334.8 2.1 copy.40
  336.9 50.9 %reduce-scatter.5.cloned.1.call-done = bf16[3,3,3,32,32]{4,3,2,1,0:T(8,128)(2,1)} async-done(((bf16[3,3,3,256,32]{4,3,2,1,0:T(8,128)(2,1)}), bf16[3,3,3,32,32]{4,3,2,1,0:T(8,128)(2,1)}) %reduce-scatter.5.cloned.1.call-update) | async-done | bytes 55312 | tf_op jit(solution)/shard_map/reduce_scatter | solution.py:62
  387.8 6.7 %psum.7 = bf16[3,3,3,32,32]{4,3,2,1,0:T(8,128)(2,1)S(1)} all-reduce(bf16[3,3,3,32,32]{4,3,2,1,0:T(8,128)(2,1)} %reduce-scatter.5.cloned.1.call-done), channel_id=1, replica_groups=mesh['sample'=2,'sx'=8,'sy'=8] {'sample'}, use_global_device_ids=true, to_apply=%region_2.3 | all-reduce | flops 27648 | bytes 110592 | tf_op jit(solution)/shard_map/psum | solution.py:65
  395.3 85.6 %reduce-scatter.3.cloned.1.call-done = bf16[4,2,4,32,256]{4,3,1,0,2:T(8,128)(2,1)} async-done(((bf16[4,2,32,32,256]{4,3,1,0,2:T(8,128)(2,1)}), bf16[4,2,4,32,256]{4,3,1,0,2:T(8,128)(2,1)}) %reduce-scatter.3.cloned.1.call-update) | async-done | bytes 524304 | tf_op jit(solution)/shard_map/reduce_scatter | solution.py:58
  481.0 1.9 copy.41
  (37 shorter events, 9.1 us)
Async XLA Ops:
  7.2 162.7 %all-gather.2.cloned.1.call-start = ((), (), s32[]{:S(2)}) async-start(), calls=%async_computation.2 | async-start | bytes 7077888 | tf_op jit(solution)/shard_map/all_gather | solution.py:47
  9.0 5.4 %collective-permute-start = (bf16[1,2,4,32,256]{4,1,3,2,0:T(2,128)(2,1)S(1)}, bf16[1,2,4,32,256]{4,1,3,2,0:T(2,128)(2,1)S(1)}, u32[]{:S(2)}, u32[]{:S(2)}) collective-permute-start(bf16[1,2,4,32,256]{4,1,3,2,0:T(2,128)(2,1)S(1)} %get-tuple-element.13), channel_id=1, source_target_pairs={{0,8},{8,16},{16,24},{24,32},{32,40},{40,48},{48,56},{1,9},{9,17},... | collective-permute-start | bytes 393224 | tf_op jit(solution)/shard_map/ppermute | solution.py:14
  12.2 5.7 %collective-permute-start.1 = (bf16[1,2,4,32,256]{4,1,3,2,0:T(2,128)(2,1)S(1)}, bf16[1,2,4,32,256]{4,1,3,2,0:T(2,128)(2,1)S(1)}, u32[]{:S(2)}, u32[]{:S(2)}) collective-permute-start(bf16[1,2,4,32,256]{4,1,3,2,0:T(2,128)(2,1)S(1)} %get-tuple-element.14), channel_id=1, source_target_pairs={{8,0},{16,8},{24,16},{32,24},{40,32},{48,40},{56,48},{9,1},{17,9},... | collective-permute-start | bytes 393224 | tf_op jit(solution)/shard_map/ppermute | solution.py:15
  20.0 367.8 %reduce-scatter.5.cloned.1.call-start = ((), (), s32[]{:S(2)}) async-start(), calls=%async_computation.4 | async-start | bytes 1990656 | tf_op jit(solution)/shard_map/reduce_scatter | solution.py:62
  58.0 129.1 %copy-start.2 = (bf16[3,3,3,256,32]{4,3,2,1,0:T(8,128)(2,1)}, bf16[3,3,3,256,32]{4,3,2,1,0:T(8,128)(2,1)S(1)}, u32[]{:S(2)}) copy-start(bf16[3,3,3,256,32]{4,3,2,1,0:T(8,128)(2,1)S(1)} %all_gather.7) | copy-start | bytes 1327108
  184.3 2.9 copy-start.4
  229.5 1.6 copy-start.1
  229.5 7.2 %slice-start = ((s8[6291456]{0:T(1024)(128)(4,1)}), s8[4194304]{0:T(1024)(128)(4,1)S(1)}, s32[]{:S(2)}) async-start(s8[6291456]{0:T(1024)(128)(4,1)} %bitcast.38), calls=%async_computation.5 | async-start | bytes 8388608
  231.1 5.6 %slice-start.1 = ((s8[6291456]{0:T(1024)(128)(4,1)}), s8[2097152]{0:T(1024)(128)(4,1)S(1)}, s32[]{:S(2)}) async-start(s8[6291456]{0:T(1024)(128)(4,1)} %bitcast.38), calls=%async_computation.6 | async-start | bytes 4194304
  233.3 78.6 %collective-permute-start.2 = (bf16[1,2,32,32,32]{4,2,3,1,0:T(8,128)(2,1)}, bf16[1,2,32,32,32]{4,2,3,1,0:T(8,128)(2,1)}, u32[]{:S(2)}, u32[]{:S(2)}) collective-permute-start(bf16[1,2,32,32,32]{4,2,3,1,0:T(8,128)(2,1)} %get-tuple-element.11), channel_id=1, source_target_pairs={{0,8},{8,16},{16,24},{24,32},{32,40},{40,48},{48,56},{1,9},{9,17},... | collective-permute-start | bytes 393224 | tf_op jit(solution)/shard_map/ppermute | solution.py:14
  235.4 76.5 %collective-permute-start.3 = (bf16[1,2,32,32,32]{4,2,3,1,0:T(8,128)(2,1)}, bf16[1,2,32,32,32]{4,2,3,1,0:T(8,128)(2,1)}, u32[]{:S(2)}, u32[]{:S(2)}) collective-permute-start(bf16[1,2,32,32,32]{4,2,3,1,0:T(8,128)(2,1)} %get-tuple-element.12), channel_id=1, source_target_pairs={{8,0},{16,8},{24,16},{32,24},{40,32},{48,40},{56,48},{9,1},{17,9},... | collective-permute-start | bytes 393224 | tf_op jit(solution)/shard_map/ppermute | solution.py:15
  311.9 169.1 %reduce-scatter.3.cloned.1.call-start = ((), (), s32[]{:S(2)}) async-start(), calls=%async_computation.3 | async-start | bytes 4718592 | tf_op jit(solution)/shard_map/reduce_scatter | solution.py:58
  315.2 1.5 copy-start.3
  315.2 1.5 copy-start.5
  329.3 4.4 copy-start
Sparse Core Ops, SparseCore 0:
  20.2 149.6 all-gather.1
  312.0 75.7 reduce-scatter.4
  390.2 90.6 reduce-scatter.2
where the time goes:
time: 495 us; the launch traced here: 490 us
  waiting for transfers between devices  253 us (51%)
  matrix products  128 us (26%)
  blocking collectives  44 us (9%)
  local copies, waits for them, and re-layouts  35.1 us (7%)
  between operations  14.2 us (3%)
  starting transfers between devices  7.99 us (2%)
  other arithmetic  7.82 us (2%)
    conv_general_dilated x3, matrix products, convolve(): lax.conv_general_dilated(inputs, weights, (1, 1, 1), pads, dimension_numb...  128 us
    all_gather x1, waiting for transfers between devices, local(): band = lax.all_gather(edged, 'sy', axis=2, tiled=True)  112 us
    reduce_scatter x1, waiting for transfers between devices, local(): lax.psum_scatter(partial_grad.astype(jnp.bfloat16), 'sy', scatter_dimensi...  85.6 us
    reduce_scatter x1, waiting for transfers between devices, local(): lax.psum_scatter(local_grad.astype(jnp.bfloat16), 'sx', scatter_dimension...  50.9 us
    all_gather x1, blocking collectives, local(): kernel_full = lax.all_gather(kernel, 'sx', axis=3, tiled=True)  37.3 us
  transfers between devices with their start and end apart: 7, of which 5 were waited for; matrix products, arithmetic and copies ran while one was open for 21% of the time, Pallas kernels for 0%

commit v1 on v0

v1 whole, which is shorter than its diff:
```python
import jax
import jax.numpy as jnp
from jax import lax
from jax.experimental import pallas as pl
from jax.experimental.pallas import tpu as pltpu
from jax.sharding import PartitionSpec as P

HALF = 14
GRID = ("sx", "sy")
BF16 = jnp.bfloat16
F32 = jnp.float32


def halo(array, axis, dim):
    size, length = (lax.axis_size(axis), array.shape[dim])
    up = [(i, i + 1) for i in range(size - 1)]
    down = [(j, i) for i, j in up]
    last = lax.slice_in_dim(array, length - 1, length, axis=dim)
    leading = lax.slice_in_dim(array, 0, 1, axis=dim)
    return lax.ppermute(last, axis, up), lax.ppermute(leading, axis, down)


def padded(array, axis, dim):
    before, after = halo(array, axis, dim)
    return jnp.concatenate([before, array, after], axis=dim)


def swap_cores(array):
    return lax.ppermute(array, "sample", [(0, 1), (1, 0)])


def call(body, out, grid=None, ins=None, outs=None, scratch=(), limit=48):
    extra = {}
    if grid is not None:
        extra = {"grid": grid, "in_specs": ins, "out_specs": outs}
    elif ins is not None:
        extra = {"in_specs": ins}
    return pl.pallas_call(
        body,
        out_shape=out,
        scratch_shapes=list(scratch),
        compiler_params=pltpu.CompilerParams(vmem_limit_bytes=limit << 20),
        **extra,
    )


def shape(dims, dtype=BF16):
    return jax.ShapeDtypeStruct(dims, dtype)


def turn(parts):
    a = parts
    lane = lax.broadcasted_iota(jnp.int32, a[0].shape, 1)
    low = lane < 64
    even = (lane // 32) % 2 == 0

    def pair(x, y, mask, step):
        first = jnp.where(mask, x, pltpu.roll(y, step, 1))
        second = jnp.where(mask, pltpu.roll(x, 128 - step, 1), y)
        return first, second

    a0, a2 = pair(a[0], a[2], low, 64)
    a1, a3 = pair(a[1], a[3], low, 64)
    b0, b1 = pair(a0, a1, even, 32)
    b2, b3 = pair(a2, a3, even, 32)
    return [b0, b1, b2, b3]


def pack_kernel_body(core, taps, out):
    rows = []
    for t in range(HALF // 2):
        one = taps[core[0] * HALF + 2 * t].astype(F32)
        two = taps[core[0] * HALF + 2 * t + 1].astype(F32)
        rows.append(jnp.concatenate([one[:16], one[16:], two[:16], two[16:]], axis=1))
    block = jnp.concatenate(rows, axis=0).astype(BF16)
    out[...] = jnp.broadcast_to(block[None], out.shape)


def unpack_kernel_body(mine, out):
    for t in range(HALF // 2):
        for high in range(2):
            parts = [mine[high * 4 + s, 16 * t : 16 * t + 16, :] for s in range(4)]
            for g, part in enumerate(turn(parts)):
                rows = pl.ds(16 * (g % 2), 16)
                out[2 * t + g // 2, rows, 128 * high : 128 * high + 128] = part


def pack_grad_body(core, own, received, out):
    start = core[0] * 13
    for t in range(HALF // 2):
        for high in range(2):
            parts = []
            for g in range(4):
                slot, rows = 2 * t + g // 2, pl.ds(16 * (g % 2), 16)
                lanes = pl.ds(128 * high, 128)
                total = own[start + slot, rows, lanes].astype(F32) + received[slot, rows, lanes].astype(F32)
                parts.append(total.astype(BF16))
            for s, part in enumerate(turn(parts)):
                out[high * 4 + s, 0, 16 * t : 16 * t + 16, :] = part


def sum_grad_body(blocks, out):
    total = blocks[0].astype(F32)
    for n in range(1, 64):
        total = total + blocks[n].astype(F32)
    out[...] = total


def unpack_grad_body(core, mine, other, out):
    zero = core[0] == 0
    first = jnp.where(zero, mine[...], other[...])
    second = jnp.where(zero, other[...], mine[...])
    for start, source in ((0, first), (13, second)):
        for t in range(HALF // 2):
            rows = source[16 * t : 16 * t + 16]
            for u in range(2):
                piece = jnp.concatenate([rows[:, 64 * u : 64 * u + 32], rows[:, 64 * u + 32 : 64 * u + 64]], axis=0)
                out[start + 2 * t + u] = piece.T


def pack_cotangent_body(cot, out):
    for s in range(2):
        parts = [cot[p, s].reshape(1024, 32).astype(F32) for p in range(4)]
        block = jnp.concatenate(parts, axis=1).astype(BF16)
        out[:, 128 * s : 128 * s + 128, :] = block.reshape(8, 128, 128)


def unpack_output_body(block, out):
    for s in range(2):
        rows = block[:, 128 * s : 128 * s + 128, :].reshape(1024, 128).astype(F32)
        for p in range(4):
            out[p, s] = rows[:, 32 * p : 32 * p + 32].reshape(32, 32, 32).astype(BF16)


def fill_shifts(source, target):
    row = lax.broadcasted_iota(jnp.int32, (192, 256), 0) % 32

    def plane(n, carry):
        a, s = n // 2, n % 2
        x = source[a, s]
        wide = x.astype(F32)
        before = jnp.where(row == 0, 0.0, pltpu.roll(wide, 1, 0))
        after = jnp.where(row == 31, 0.0, pltpu.roll(wide, 191, 0))
        target[a, s, :, 0:256] = before.astype(BF16)
        target[a, s, :, 256:512] = x
        target[a, s, :, 512:768] = after.astype(BF16)
        return carry

    lax.fori_loop(0, 12, plane, 0)


def by_core(core, run, mine, other):
    @pl.when(core[0] == 0)
    def _():
        run(mine, other)

    @pl.when(core[0] == 1)
    def _():
        run(other, mine)


def forward_body(core, window, mine, other, cot, shifts, grad_pre, packed, cots, outs):
    fill_shifts(window, shifts)
    for high in range(2):
        parts = turn([cot[high * 4 + s] for s in range(4)])
        for p in range(4):
            cots[p, :, 128 * high : 128 * high + 128] = parts[p]

    def run(first, second):
        bias = second[13, 0:1, :].astype(F32)

        def plane(p, carry):
            total = jnp.zeros((256, 256), F32)
            for i in range(3):
                for j in range(3):
                    start = 9 * i + 3 * j
                    source = first if start < HALF else second
                    at = start % HALF
                    count = min(3, HALF - at)
                    lhs = shifts[p + i, :, 32 * j : 32 * j + 128, 0 : 256 * count].reshape(256, 256 * count)
                    rhs = source[at : at + count].reshape(256 * count, 256)
                    total = total + jnp.dot(lhs, rhs, preferred_element_type=F32)
                    if count < 3:
                        lhs = shifts[p + i, :, 32 * j : 32 * j + 128, 256 * count : 768].reshape(256, 768 - 256 * count)
                        rhs = second[0 : 3 - count].reshape(768 - 256 * count, 256)
                        total = total + jnp.dot(lhs, rhs, preferred_element_type=F32)
            hidden = total + bias
            gate = 1.0 / (1.0 + jnp.exp(-hidden))
            outs[p] = (hidden * gate).astype(BF16)
            slope = gate * (1.0 + hidden * (1.0 - gate))
            grad_pre[p] = (cots[p].astype(F32) * slope).astype(BF16).reshape(2, 128, 256)
            return carry

        lax.fori_loop(0, 4, plane, 0)

    by_core(core, run, mine, other)
    for high in range(2):
        parts = turn([outs[p, :, 128 * high : 128 * high + 128] for p in range(4)])
        for s in range(4):
            packed[high * 4 + s] = parts[s]


def kernel_grad_body(shifts, grad_pre, out, turned):
    for p in range(4):
        turned[:, 256 * p : 256 * p + 256] = grad_pre[p].reshape(256, 256).astype(F32).T.astype(BF16)
    lhs = turned[...]
    for i in range(3):
        for j in range(3):
            rhs = shifts[i : i + 4, :, 32 * j : 32 * j + 128, :].reshape(1024, 768)
            res = jnp.dot(lhs, rhs, preferred_element_type=F32).astype(BF16)
            for k in range(3):
                out[9 * i + 3 * j + k] = res[:, 256 * k : 256 * k + 256]


def input_grad_body(core, window, mine, other, out, shifts):
    fill_shifts(window, shifts)

    def run(first, second):
        def plane(p, carry):
            total = jnp.zeros((256, 256), F32)
            for i in range(3):
                for j in range(3):
                    for k in range(3):
                        tap = 9 * i + 3 * j + k
                        rhs = first[tap] if tap < HALF else second[tap - HALF]
                        lanes = pl.ds(256 * (2 - k), 256)
                        lhs = shifts[p + 2 - i, :, 32 * (2 - j) : 32 * (2 - j) + 128, lanes].reshape(256, 256)
                        total = total + lax.dot_general(
                            lhs, rhs, (((1,), (1,)), ((), ())), preferred_element_type=F32
                        )
            out[p] = total.astype(BF16).reshape(2, 128, 256)
            return carry

        lax.fori_loop(0, 4, plane, 0)

    by_core(core, run, mine, other)


SMEM = pl.BlockSpec(memory_space=pltpu.SMEM)
FULL = pl.BlockSpec(memory_space=pltpu.VMEM)


def local(features, kernel, filter_bias, cotangent):
    core = lax.axis_index("sample").astype(jnp.int32)
    index = core[None]
    bias = jnp.broadcast_to(filter_bias[None, None, :], (1, 32, 32))
    taps = jnp.concatenate([kernel.reshape(27, 32, 32), bias], axis=0)
    blocks = call(pack_kernel_body, shape((64, 112, 128)), ins=[SMEM, FULL])(index, taps)
    blocks = lax.all_to_all(blocks, GRID, 0, 0, tiled=True)
    before, after = halo(features, "sx", 0)
    cot = call(pack_cotangent_body, shape((8, 256, 128)))(cotangent)
    before, after, blocks, cot = lax.optimization_barrier((before, after, blocks, cot))
    window = jnp.concatenate([before, features, after], axis=0)
    cot = lax.all_to_all(cot, "sy", 0, 0, tiled=True)
    window = padded(window, "sy", 2).reshape(6, 2, 192, 256)
    mine = call(
        unpack_kernel_body,
        shape((HALF, 256, 256)),
        (8,),
        [pl.BlockSpec((8, 112, 128), lambda n: (n, 0, 0))],
        pl.BlockSpec((HALF, 32, 256), lambda n: (0, n, 0)),
    )(blocks)
    other = swap_cores(mine)
    shifts, grad_pre, packed = call(
        forward_body,
        (shape((6, 2, 192, 768)), shape((4, 2, 128, 256)), shape((8, 256, 128))),
        ins=[SMEM, FULL, FULL, FULL, FULL],
        scratch=[pltpu.VMEM((4, 256, 256), BF16), pltpu.VMEM((4, 256, 256), BF16)],
    )(index, window, mine, other, cot)
    packed = lax.all_to_all(packed, "sy", 0, 0, tiled=True)
    grad_window = padded(grad_pre.reshape(4, 2, 4, 32, 256), "sx", 0)
    local_grad = call(kernel_grad_body, shape((27, 256, 256)), scratch=[pltpu.VMEM((256, 1024), BF16)])(
        shifts, grad_pre
    )
    received = swap_cores(lax.dynamic_slice_in_dim(local_grad, (1 - core) * 13, HALF, axis=0))
    grad_window = padded(grad_window, "sy", 2).reshape(6, 2, 192, 256)
    blocks = call(
        pack_grad_body,
        shape((8, 8, 112, 128)),
        (8,),
        [
            SMEM,
            pl.BlockSpec((27, 32, 256), lambda n: (0, n, 0)),
            pl.BlockSpec((HALF, 32, 256), lambda n: (0, n, 0)),
        ],
        pl.BlockSpec((8, 1, 112, 128), lambda n: (0, n, 0, 0)),
    )(index, local_grad, received)
    blocks, packed = lax.optimization_barrier((blocks, packed))
    blocks = lax.all_to_all(blocks.reshape(64, 112, 128), GRID, 0, 0, tiled=True)
    input_grad = call(
        input_grad_body,
        shape((4, 2, 128, 256)),
        ins=[SMEM, FULL, FULL, FULL],
        scratch=[pltpu.VMEM((6, 2, 192, 768), BF16)],
    )(index, grad_window, mine, other)
    output = call(unpack_output_body, shape((4, 2, 32, 32, 32)))(packed)
    blocks, input_grad, output = lax.optimization_barrier((blocks, input_grad, output))
    rows = call(sum_grad_body, shape((112, 128), F32))(blocks)
    kernel_grad = call(unpack_grad_body, shape((27, 32, 32), F32), ins=[SMEM, FULL, FULL])(
        index, rows, swap_cores(rows)
    )
    return (output, input_grad.reshape(4, 2, 4, 32, 256), kernel_grad.reshape(3, 3, 3, 32, 32))


def solution(mesh):
    return jax.shard_map(
        local,
        mesh=mesh,
        in_specs=(
            P("sx", "sample", "sy", None, None),
            P(None, None, None, "sx", "sy"),
            P("sy"),
            P("sx", "sample", None, None, "sy"),
        ),
        out_specs=(
            P("sx", "sample", None, None, "sy"),
            P("sx", "sample", "sy", None, None),
            P(None, None, None, "sx", "sy"),
        ),
        check_vma=False,
    )
```

time: 495 us -> 163 us (0.33)
  waiting for transfers between devices: 253 us -> 55.8 us
  matrix products: 128 us -> 0 us
  starting transfers between devices: 7.99 us -> 52.1 us
  blocking collectives: 44 us -> 0 us
  Pallas kernels: 0 us -> 37.2 us
  local copies, waits for them, and re-layouts: 35.1 us -> 11.4 us
  between operations: 14.2 us -> 0.89 us
  other arithmetic: 7.82 us -> 2.63 us
    reduce_scatter x2 -> x0, waiting for transfers between devices: 137 us -> none  [the longest x1 85.6 us: local(): lax.psum_scatter(partial_grad.astype(jnp.bfloat16), 'sy', scatter_dimensi...]
    conv_general_dilated x3 -> x0, matrix products: 128 us -> none  [convolve(): lax.conv_general_dilated(inputs, weights, (1, 1, 1), pads, dimension_numb...]
    all_gather x1 -> x0, waiting for transfers between devices: 112 us -> none  [local(): band = lax.all_gather(edged, 'sy', axis=2, tiled=True)]
    ppermute x4 -> x11, waiting for transfers between devices: 4.42 us -> 53.7 us  [the longest x8 52.8 us: halo(): return (lax.ppermute(last, axis, up), lax.ppermute(leading, axis, down))]
    all_gather x1 -> x0, blocking collectives: 37.3 us -> none  [local(): kernel_full = lax.all_gather(kernel, 'sx', axis=3, tiled=True)]
    pallas_call x0 -> x10, Pallas kernels: none -> 37.2 us  [the longest x1 9.54 us: local(): call(forward_body, (shape((6, 2, 192, 768)), shape((4, 2, 128, 256)), sha...]
    all_to_all x0 -> x4, starting transfers between devices: none -> 27.3 us  [the longest x1 11.1 us: local(): blocks = lax.all_to_all(blocks, GRID, 0, 0, tiled=True)]
    ppermute x4 -> x11, starting transfers between devices: 7.86 us -> 24.8 us  [the longest x8 21.3 us: halo(): return (lax.ppermute(last, axis, up), lax.ppermute(leading, axis, down))]
  transfers between devices with their start and end apart: 7 -> 15, of which waited for: 5 -> 11; matrix products, arithmetic and copies ran while one was open for 21% -> 1% of each run, Pallas kernels for 0% -> 11%
where the time goes in v1:
time: 163 us; the launch traced here: 160 us
  waiting for transfers between devices  55.8 us (34%)
  starting transfers between devices  52.1 us (32%)
  Pallas kernels  37.2 us (23%)
  local copies, waits for them, and re-layouts  11.4 us (7%)
  other arithmetic  2.63 us (2%)
    ppermute x8, waiting for transfers between devices, halo(): return (lax.ppermute(last, axis, up), lax.ppermute(leading, axis, down))  52.8 us
    ppermute x8, starting transfers between devices, halo(): return (lax.ppermute(last, axis, up), lax.ppermute(leading, axis, down))  21.3 us
    all_to_all x1, starting transfers between devices, local(): blocks = lax.all_to_all(blocks, GRID, 0, 0, tiled=True)  11.1 us
    pallas_call x1, Pallas kernels, local(): call(forward_body, (shape((6, 2, 192, 768)), shape((4, 2, 128, 256)), sha...  9.54 us
    unnamed x24, local copies, waits for them, and re-layouts  9.11 us
    all_to_all x1, starting transfers between devices, local(): lax.all_to_all(blocks.reshape(64, 112, 128), GRID, 0, 0, tiled=True)  7.73 us
    pallas_call x1, Pallas kernels, local(): call(input_grad_body, shape((4, 2, 128, 256)), ins=[SMEM, FULL, FULL, FUL...  7.46 us
    pallas_call x1, Pallas kernels, local(): call(pack_grad_body, shape((8, 8, 112, 128)), (8,), [SMEM, pl.BlockSpec((...  6.75 us
  transfers between devices with their start and end apart: 15, of which 11 were waited for; matrix products, arithmetic and copies ran while one was open for 1% of the time, Pallas kernels for 11%

profile of v1, /device:TPU:3, one launch (start us, length us, event | category | flops | bytes accessed | tf_op | source)
XLA Modules:
  0.0 160.0 jit_solution(11359435921986958739)
XLA Ops:
  3.7 11.1 %all-to-all-start = ((bf16[64,112,128]{2,1,0:T(8,128)(2,1)}), bf16[64,112,128]{2,1,0:T(8,128)(2,1)S(1)}, u32[]{:S(2)}, u32[]{:S(2)}) async-start(bf16[64,112,128]{2,1,0:T(8,128)(2,1)} %copy-done.5), calls=%async_computation | async-start | bytes 3670016 | tf_op jit(solution)/shard_map/all_to_all | solution.py:249
  14.8 3.1 %collective-permute-start = (bf16[1,2,4,32,256]{4,3,2,1,0:T(8,128)(2,1)S(1)}, bf16[1,2,4,32,256]{4,3,2,1,0:T(8,128)(2,1)S(1)}, u32[]{:S(2)}, u32[]{:S(2)}) collective-permute-start(bf16[1,2,4,32,256]{4,3,2,1,0:T(8,128)(2,1)S(1)} %get-tuple-element.34), channel_id=1, source_target_pairs={{0,8},{8,16},{16,24},{24,32},{32,40},{40,48},{48,56},{1,9},{9,17},... | collective-permute-start | bytes 393224 | tf_op jit(solution)/shard_map/ppermute | solution.py:20
  22.1 14.0 %collective-permute-done = bf16[1,2,4,32,256]{4,3,2,1,0:T(8,128)(2,1)S(1)} collective-permute-done((bf16[1,2,4,32,256]{4,3,2,1,0:T(8,128)(2,1)S(1)}, bf16[1,2,4,32,256]{4,3,2,1,0:T(8,128)(2,1)S(1)}, u32[]{:S(2)}, u32[]{:S(2)}) %collective-permute-start) | collective-permute-done | bytes 131104 | tf_op jit(solution)/shard_map/ppermute | solution.py:20
  36.2 2.4 %collective-permute-done.1 = bf16[1,2,4,32,256]{4,3,2,1,0:T(8,128)(2,1)S(1)} collective-permute-done((bf16[1,2,4,32,256]{4,3,2,1,0:T(8,128)(2,1)S(1)}, bf16[1,2,4,32,256]{4,3,2,1,0:T(8,128)(2,1)S(1)}, u32[]{:S(2)}, u32[]{:S(2)}) %collective-permute-start.1) | collective-permute-done | bytes 131104 | tf_op jit(solution)/shard_map/ppermute | solution.py:20
  42.2 2.0 %shard_map.69.mine = bf16[14,256,256]{2,1,0:T(8,128)(2,1)S(1)} custom-call(bf16[64,112,128]{2,1,0:T(8,128)(2,1)S(1)} %copy-done.4), custom_call_target="tpu_custom_call" | custom-call | tf_op jit(solution)/shard_map/pallas_call | solution.py:256
  44.2 2.3 %collective-permute-start.4 = (bf16[14,256,256]{2,1,0:T(8,128)(2,1)S(1)}, bf16[14,256,256]{2,1,0:T(8,128)(2,1)}, u32[]{:S(2)}, u32[]{:S(2)}) collective-permute-start(bf16[14,256,256]{2,1,0:T(8,128)(2,1)S(1)} %shard_map.69.mine), channel_id=1, source_target_pairs={{0,64},{64,0},{1,65},{65,1},{2,66},{66,2},{3,67},{67,3},{4,68},{68... | collective-permute-start | bytes 5505032 | tf_op jit(solution)/shard_map/ppermute | solution.py:29
  46.5 4.4 %all-to-all-start.1 = ((bf16[8,256,128]{2,1,0:T(8,128)(2,1)}), bf16[8,256,128]{2,1,0:T(8,128)(2,1)S(1)}, u32[]{:S(2)}, u32[]{:S(2)}) async-start(bf16[8,256,128]{2,1,0:T(8,128)(2,1)} %shard_map.68), calls=%async_computation.1 | async-start | bytes 1048576 | tf_op jit(solution)/shard_map/all_to_all | solution.py:254
  52.0 3.1 %collective-permute-start.2 = (bf16[6,2,1,32,256]{4,3,2,1,0:T(8,128)(2,1)S(1)}, bf16[6,2,1,32,256]{4,3,2,1,0:T(8,128)(2,1)}, u32[]{:S(2)}, u32[]{:S(2)}) collective-permute-start(bf16[6,2,1,32,256]{4,3,2,1,0:T(8,128)(2,1)S(1)} %get-tuple-element.29), channel_id=1, source_target_pairs={{0,1},{1,2},{2,3},{3,4},{4,5},{5,6},{6,7},{8,9},{9,10},{10,11},{11... | collective-permute-start | bytes 589832 | tf_op jit(solution)/shard_map/ppermute | solution.py:20
  55.1 3.1 %collective-permute-start.3 = (bf16[6,2,1,32,256]{4,3,2,1,0:T(8,128)(2,1)S(1)}, bf16[6,2,1,32,256]{4,3,2,1,0:T(8,128)(2,1)}, u32[]{:S(2)}, u32[]{:S(2)}) collective-permute-start(bf16[6,2,1,32,256]{4,3,2,1,0:T(8,128)(2,1)S(1)} %get-tuple-element.30), channel_id=1, source_target_pairs={{1,0},{2,1},{3,2},{4,3},{5,4},{6,5},{7,6},{9,8},{10,9},{11,10},{12... | collective-permute-start | bytes 589832 | tf_op jit(solution)/shard_map/ppermute | solution.py:20
  58.2 6.9 %collective-permute-done.2 = bf16[6,2,1,32,256]{4,3,2,1,0:T(8,128)(2,1)} collective-permute-done((bf16[6,2,1,32,256]{4,3,2,1,0:T(8,128)(2,1)S(1)}, bf16[6,2,1,32,256]{4,3,2,1,0:T(8,128)(2,1)}, u32[]{:S(2)}, u32[]{:S(2)}) %collective-permute-start.2) | collective-permute-done | bytes 196640 | tf_op jit(solution)/shard_map/ppermute | solution.py:20
  65.1 2.8 %collective-permute-done.3 = bf16[6,2,1,32,256]{4,3,2,1,0:T(8,128)(2,1)} collective-permute-done((bf16[6,2,1,32,256]{4,3,2,1,0:T(8,128)(2,1)S(1)}, bf16[6,2,1,32,256]{4,3,2,1,0:T(8,128)(2,1)}, u32[]{:S(2)}, u32[]{:S(2)}) %collective-permute-start.3) | collective-permute-done | bytes 196640 | tf_op jit(solution)/shard_map/ppermute | solution.py:20
  71.1 9.5 %shard_map.70 = (bf16[6,2,192,768]{3,2,1,0:T(8,128)(2,1)}, bf16[4,2,128,256]{3,2,1,0:T(8,128)(2,1)S(1)}, bf16[8,256,128]{2,1,0:T(8,128)(2,1)}) custom-call(s32[1]{0:T(128)} %bitcast.core, bf16[6,2,192,256]{3,2,1,0:T(8,128)(2,1)S(1)} %bitcast.12, bf16[14,256,256]{2,1,0:T(8,128)(2,1)S(1)} %shard_map.69.mine, ...), custom_call_target="tpu_custom_call" | custom-call | tf_op jit(solution)/shard_map/pallas_call | solution.py:264
  80.7 5.9 %shard_map.71.own = bf16[27,256,256]{2,1,0:T(8,128)(2,1)S(1)} custom-call(bf16[6,2,192,768]{3,2,1,0:T(8,128)(2,1)} %get-tuple-element.19.shifts, bf16[4,2,128,256]{3,2,1,0:T(8,128)(2,1)S(1)} %get-tuple-element.20.grad_pre), custom_call_target="tpu_custom_call" | custom-call | tf_op jit(solution)/shard_map/pallas_call | solution.py:272
  89.3 4.1 %all-to-all-start.2 = ((bf16[8,256,128]{2,1,0:T(8,128)(2,1)}), bf16[8,256,128]{2,1,0:T(8,128)(2,1)S(1)}, u32[]{:S(2)}, u32[]{:S(2)}) async-start(bf16[8,256,128]{2,1,0:T(8,128)(2,1)} %get-tuple-element.21), calls=%async_computation.2 | async-start | bytes 1048576 | tf_op jit(solution)/shard_map/all_to_all | solution.py:270
  93.4 6.8 %shard_map.72 = bf16[8,8,112,128]{3,2,1,0:T(8,128)(2,1)} custom-call(s32[1]{0:T(128)} %bitcast.core, bf16[27,256,256]{2,1,0:T(8,128)(2,1)} %copy-done, bf16[14,256,256]{2,1,0:T(8,128)(2,1)S(1)} %collective-permute-done.5.received), custom_call_target="tpu_custom_call" | custom-call | tf_op jit(solution)/shard_map/pallas_call | solution.py:277
  101.3 7.7 %all-to-all-start.3 = ((bf16[64,112,128]{2,1,0:T(8,128)(2,1)}), bf16[64,112,128]{2,1,0:T(8,128)(2,1)S(1)}, u32[]{:S(2)}, u32[]{:S(2)}) async-start(bf16[64,112,128]{2,1,0:T(8,128)(2,1)} %bitcast.3), calls=%async_computation.3 | async-start | bytes 3670016 | tf_op jit(solution)/shard_map/all_to_all | solution.py:289
  109.1 3.1 %collective-permute-start.6 = (bf16[1,2,4,32,256]{4,3,2,1,0:T(8,128)(2,1)S(1)}, bf16[1,2,4,32,256]{4,3,2,1,0:T(8,128)(2,1)S(1)}, u32[]{:S(2)}, u32[]{:S(2)}) collective-permute-start(bf16[1,2,4,32,256]{4,3,2,1,0:T(8,128)(2,1)S(1)} %bitcast.18), channel_id=1, source_target_pairs={{0,8},{8,16},{16,24},{24,32},{32,40},{40,48},{48,56},{1,9},{9,17},... | collective-permute-start | bytes 393224 | tf_op jit(solution)/shard_map/ppermute | solution.py:20
  113.5 16.9 %collective-permute-done.6 = bf16[1,2,4,32,256]{4,3,2,1,0:T(8,128)(2,1)S(1)} collective-permute-done((bf16[1,2,4,32,256]{4,3,2,1,0:T(8,128)(2,1)S(1)}, bf16[1,2,4,32,256]{4,3,2,1,0:T(8,128)(2,1)S(1)}, u32[]{:S(2)}, u32[]{:S(2)}) %collective-permute-start.6) | collective-permute-done | bytes 131104 | tf_op jit(solution)/shard_map/ppermute | solution.py:20
  130.4 2.4 %collective-permute-done.7 = bf16[1,2,4,32,256]{4,3,2,1,0:T(8,128)(2,1)S(1)} collective-permute-done((bf16[1,2,4,32,256]{4,3,2,1,0:T(8,128)(2,1)S(1)}, bf16[1,2,4,32,256]{4,3,2,1,0:T(8,128)(2,1)S(1)}, u32[]{:S(2)}, u32[]{:S(2)}) %collective-permute-start.7) | collective-permute-done | bytes 131104 | tf_op jit(solution)/shard_map/ppermute | solution.py:20
  132.9 3.4 %collective-permute-start.8 = (bf16[6,2,1,32,256]{4,3,2,1,0:T(8,128)(2,1)S(1)}, bf16[6,2,1,32,256]{4,3,2,1,0:T(8,128)(2,1)S(1)}, u32[]{:S(2)}, u32[]{:S(2)}) collective-permute-start(bf16[6,2,1,32,256]{4,3,2,1,0:T(8,128)(2,1)S(1)} %get-tuple-element.27), channel_id=1, source_target_pairs={{0,1},{1,2},{2,3},{3,4},{4,5},{5,6},{6,7},{8,9},{9,10},{10,11},{11... | collective-permute-start | bytes 589832 | tf_op jit(solution)/shard_map/ppermute | solution.py:20
  136.3 2.9 %collective-permute-start.9 = (bf16[6,2,1,32,256]{4,3,2,1,0:T(8,128)(2,1)S(1)}, bf16[6,2,1,32,256]{4,3,2,1,0:T(8,128)(2,1)S(1)}, u32[]{:S(2)}, u32[]{:S(2)}) collective-permute-start(bf16[6,2,1,32,256]{4,3,2,1,0:T(8,128)(2,1)S(1)} %get-tuple-element.28), channel_id=1, source_target_pairs={{1,0},{2,1},{3,2},{4,3},{5,4},{6,5},{7,6},{9,8},{10,9},{11,10},{12... | collective-permute-start | bytes 589832 | tf_op jit(solution)/shard_map/ppermute | solution.py:20
  140.7 5.9 %collective-permute-done.9 = bf16[6,2,1,32,256]{4,3,2,1,0:T(8,128)(2,1)S(1)} collective-permute-done((bf16[6,2,1,32,256]{4,3,2,1,0:T(8,128)(2,1)S(1)}, bf16[6,2,1,32,256]{4,3,2,1,0:T(8,128)(2,1)S(1)}, u32[]{:S(2)}, u32[]{:S(2)}) %collective-permute-start.9) | collective-permute-done | bytes 196640 | tf_op jit(solution)/shard_map/ppermute | solution.py:20
  146.8 7.5 %shard_map.73 = bf16[4,2,128,256]{3,2,1,0:T(8,128)(2,1)} custom-call(s32[1]{0:T(128)} %bitcast.core, bf16[6,2,192,256]{3,2,1,0:T(8,128)(2,1)S(1)} %bitcast.13, bf16[14,256,256]{2,1,0:T(8,128)(2,1)S(1)} %copy-done.2, bf16[14,256,256]{2,1,0:T(8,128)(2,1)} %collective-permute-done.4.other), custom_call_target="tpu_custom_call" | custom-call | tf_op jit(solution)/shard_map/pallas_call | solution.py:290
  154.2 2.2 %shard_map.74 = bf16[4,2,32,32,32]{4,3,2,1,0:T(8,128)(2,1)} custom-call(bf16[8,256,128]{2,1,0:T(8,128)(2,1)S(1)} %all-to-all-done.2.block), custom_call_target="tpu_custom_call" | custom-call | tf_op jit(solution)/shard_map/pallas_call | solution.py:296
  (50 shorter events, 25.6 us)
Async XLA Ops:
  2.5 1.2 copy-start.5
  3.7 11.1 %copy-start.10 = (bf16[4,2,4,32,256]{4,3,2,1,0:T(8,128)(2,1)S(1)}, bf16[4,2,4,32,256]{4,3,2,1,0:T(8,128)(2,1)}, u32[]{:S(2)}) copy-start(bf16[4,2,4,32,256]{4,3,2,1,0:T(8,128)(2,1)} %param.4) | copy-start | bytes 1572868
  3.7 35.8 %all-to-all-start = ((bf16[64,112,128]{2,1,0:T(8,128)(2,1)}), bf16[64,112,128]{2,1,0:T(8,128)(2,1)S(1)}, u32[]{:S(2)}, u32[]{:S(2)}) async-start(bf16[64,112,128]{2,1,0:T(8,128)(2,1)} %copy-done.5), calls=%async_computation | async-start | bytes 3670016 | tf_op jit(solution)/shard_map/all_to_all | solution.py:249
  14.8 21.3 %collective-permute-start = (bf16[1,2,4,32,256]{4,3,2,1,0:T(8,128)(2,1)S(1)}, bf16[1,2,4,32,256]{4,3,2,1,0:T(8,128)(2,1)S(1)}, u32[]{:S(2)}, u32[]{:S(2)}) collective-permute-start(bf16[1,2,4,32,256]{4,3,2,1,0:T(8,128)(2,1)S(1)} %get-tuple-element.34), channel_id=1, source_target_pairs={{0,8},{8,16},{16,24},{24,32},{32,40},{40,48},{48,56},{1,9},{9,17},... | collective-permute-start | bytes 393224 | tf_op jit(solution)/shard_map/ppermute | solution.py:20
  17.9 20.7 %collective-permute-start.1 = (bf16[1,2,4,32,256]{4,3,2,1,0:T(8,128)(2,1)S(1)}, bf16[1,2,4,32,256]{4,3,2,1,0:T(8,128)(2,1)S(1)}, u32[]{:S(2)}, u32[]{:S(2)}) collective-permute-start(bf16[1,2,4,32,256]{4,3,2,1,0:T(8,128)(2,1)S(1)} %get-tuple-element.33), channel_id=1, source_target_pairs={{8,0},{16,8},{24,16},{32,24},{40,32},{48,40},{56,48},{9,1},{17,9},... | collective-permute-start | bytes 393224 | tf_op jit(solution)/shard_map/ppermute | solution.py:20
  19.2 1.6 copy-start.6
  39.5 1.2 copy-start.3
  40.7 1.5 copy-start.4
  44.2 25.9 %copy-start.1 = (bf16[14,256,256]{2,1,0:T(8,128)(2,1)}, bf16[14,256,256]{2,1,0:T(8,128)(2,1)S(1)}, u32[]{:S(2)}) copy-start(bf16[14,256,256]{2,1,0:T(8,128)(2,1)S(1)} %shard_map.69.mine) | copy-start | bytes 5505028
  44.2 25.9 %collective-permute-start.4 = (bf16[14,256,256]{2,1,0:T(8,128)(2,1)S(1)}, bf16[14,256,256]{2,1,0:T(8,128)(2,1)}, u32[]{:S(2)}, u32[]{:S(2)}) collective-permute-start(bf16[14,256,256]{2,1,0:T(8,128)(2,1)S(1)} %shard_map.69.mine), channel_id=1, source_target_pairs={{0,64},{64,0},{1,65},{65,1},{2,66},{66,2},{3,67},{67,3},{4,68},{68... | collective-permute-start | bytes 5505032 | tf_op jit(solution)/shard_map/ppermute | solution.py:29
  46.5 22.7 %all-to-all-start.1 = ((bf16[8,256,128]{2,1,0:T(8,128)(2,1)}), bf16[8,256,128]{2,1,0:T(8,128)(2,1)S(1)}, u32[]{:S(2)}, u32[]{:S(2)}) async-start(bf16[8,256,128]{2,1,0:T(8,128)(2,1)} %shard_map.68), calls=%async_computation.1 | async-start | bytes 1048576 | tf_op jit(solution)/shard_map/all_to_all | solution.py:254
  52.0 13.1 %collective-permute-start.2 = (bf16[6,2,1,32,256]{4,3,2,1,0:T(8,128)(2,1)S(1)}, bf16[6,2,1,32,256]{4,3,2,1,0:T(8,128)(2,1)}, u32[]{:S(2)}, u32[]{:S(2)}) collective-permute-start(bf16[6,2,1,32,256]{4,3,2,1,0:T(8,128)(2,1)S(1)} %get-tuple-element.29), channel_id=1, source_target_pairs={{0,1},{1,2},{2,3},{3,4},{4,5},{5,6},{6,7},{8,9},{9,10},{10,11},{11... | collective-permute-start | bytes 589832 | tf_op jit(solution)/shard_map/ppermute | solution.py:20
  55.1 12.8 %collective-permute-start.3 = (bf16[6,2,1,32,256]{4,3,2,1,0:T(8,128)(2,1)S(1)}, bf16[6,2,1,32,256]{4,3,2,1,0:T(8,128)(2,1)}, u32[]{:S(2)}, u32[]{:S(2)}) collective-permute-start(bf16[6,2,1,32,256]{4,3,2,1,0:T(8,128)(2,1)S(1)} %get-tuple-element.30), channel_id=1, source_target_pairs={{1,0},{2,1},{3,2},{4,3},{5,4},{6,5},{7,6},{9,8},{10,9},{11,10},{12... | collective-permute-start | bytes 589832 | tf_op jit(solution)/shard_map/ppermute | solution.py:20
  70.1 1.0 copy-start.8
  86.5 2.3 %copy-start = (bf16[27,256,256]{2,1,0:T(8,128)(2,1)}, bf16[27,256,256]{2,1,0:T(8,128)(2,1)S(1)}, u32[]{:S(2)}) copy-start(bf16[27,256,256]{2,1,0:T(8,128)(2,1)S(1)} %shard_map.71.own) | copy-start | bytes 10616836
  88.9 4.5 %collective-permute-start.5 = (bf16[14,256,256]{2,1,0:T(8,128)(2,1)}, bf16[14,256,256]{2,1,0:T(8,128)(2,1)S(1)}, u32[]{:S(2)}, u32[]{:S(2)}) collective-permute-start(bf16[14,256,256]{2,1,0:T(8,128)(2,1)} %constant_dynamic-slice_fusion), channel_id=1, source_target_pairs={{0,64},{64,0},{1,65},{65,1},{2,66},{66,2},{3,67},{67,3},{4,68},{68... | collective-permute-start | bytes 5505032 | tf_op jit(solution)/shard_map/ppermute | solution.py:29
  89.3 11.9 %all-to-all-start.2 = ((bf16[8,256,128]{2,1,0:T(8,128)(2,1)}), bf16[8,256,128]{2,1,0:T(8,128)(2,1)S(1)}, u32[]{:S(2)}, u32[]{:S(2)}) async-start(bf16[8,256,128]{2,1,0:T(8,128)(2,1)} %get-tuple-element.21), calls=%async_computation.2 | async-start | bytes 1048576 | tf_op jit(solution)/shard_map/all_to_all | solution.py:270
  101.3 55.1 %all-to-all-start.3 = ((bf16[64,112,128]{2,1,0:T(8,128)(2,1)}), bf16[64,112,128]{2,1,0:T(8,128)(2,1)S(1)}, u32[]{:S(2)}, u32[]{:S(2)}) async-start(bf16[64,112,128]{2,1,0:T(8,128)(2,1)} %bitcast.3), calls=%async_computation.3 | async-start | bytes 3670016 | tf_op jit(solution)/shard_map/all_to_all | solution.py:289
  109.1 21.3 %collective-permute-start.6 = (bf16[1,2,4,32,256]{4,3,2,1,0:T(8,128)(2,1)S(1)}, bf16[1,2,4,32,256]{4,3,2,1,0:T(8,128)(2,1)S(1)}, u32[]{:S(2)}, u32[]{:S(2)}) collective-permute-start(bf16[1,2,4,32,256]{4,3,2,1,0:T(8,128)(2,1)S(1)} %bitcast.18), channel_id=1, source_target_pairs={{0,8},{8,16},{16,24},{24,32},{32,40},{40,48},{48,56},{1,9},{9,17},... | collective-permute-start | bytes 393224 | tf_op jit(solution)/shard_map/ppermute | solution.py:20
  112.2 20.7 %collective-permute-start.7 = (bf16[1,2,4,32,256]{4,3,2,1,0:T(8,128)(2,1)S(1)}, bf16[1,2,4,32,256]{4,3,2,1,0:T(8,128)(2,1)S(1)}, u32[]{:S(2)}, u32[]{:S(2)}) collective-permute-start(bf16[1,2,4,32,256]{4,3,2,1,0:T(8,128)(2,1)S(1)} %bitcast.17), channel_id=1, source_target_pairs={{8,0},{16,8},{24,16},{32,24},{40,32},{48,40},{56,48},{9,1},{17,9},... | collective-permute-start | bytes 393224 | tf_op jit(solution)/shard_map/ppermute | solution.py:20
  132.9 7.8 %collective-permute-start.8 = (bf16[6,2,1,32,256]{4,3,2,1,0:T(8,128)(2,1)S(1)}, bf16[6,2,1,32,256]{4,3,2,1,0:T(8,128)(2,1)S(1)}, u32[]{:S(2)}, u32[]{:S(2)}) collective-permute-start(bf16[6,2,1,32,256]{4,3,2,1,0:T(8,128)(2,1)S(1)} %get-tuple-element.27), channel_id=1, source_target_pairs={{0,1},{1,2},{2,3},{3,4},{4,5},{5,6},{6,7},{8,9},{9,10},{10,11},{11... | collective-permute-start | bytes 589832 | tf_op jit(solution)/shard_map/ppermute | solution.py:20
  136.3 10.5 %copy-start.2 = (bf16[14,256,256]{2,1,0:T(8,128)(2,1)S(1)}, bf16[14,256,256]{2,1,0:T(8,128)(2,1)}, u32[]{:S(2)}) copy-start(bf16[14,256,256]{2,1,0:T(8,128)(2,1)} %copy-done.1) | copy-start | bytes 5505028
  136.3 10.3 %collective-permute-start.9 = (bf16[6,2,1,32,256]{4,3,2,1,0:T(8,128)(2,1)S(1)}, bf16[6,2,1,32,256]{4,3,2,1,0:T(8,128)(2,1)S(1)}, u32[]{:S(2)}, u32[]{:S(2)}) collective-permute-start(bf16[6,2,1,32,256]{4,3,2,1,0:T(8,128)(2,1)S(1)} %get-tuple-element.28), channel_id=1, source_target_pairs={{1,0},{2,1},{3,2},{4,3},{5,4},{6,5},{7,6},{9,8},{10,9},{11,10},{12... | collective-permute-start | bytes 589832 | tf_op jit(solution)/shard_map/ppermute | solution.py:20
  156.7 1.6 collective-permute-start.10
  (2 other events, 1.7 us)

commit v2 on v1

v2 whole, which is shorter than its diff:
```python
import jax
import jax.numpy as jnp
from jax import lax
from jax.experimental import pallas as pl
from jax.experimental.pallas import tpu as pltpu
from jax.sharding import PartitionSpec as P

HALF = 14
GRID = ("sx", "sy")
BF16 = jnp.bfloat16
F32 = jnp.float32


def halo(array, axis, dim):
    size, length = (lax.axis_size(axis), array.shape[dim])
    up = [(i, i + 1) for i in range(size - 1)]
    down = [(j, i) for i, j in up]
    last = lax.slice_in_dim(array, length - 1, length, axis=dim)
    leading = lax.slice_in_dim(array, 0, 1, axis=dim)
    return lax.ppermute(last, axis, up), lax.ppermute(leading, axis, down)


def corners(before, array, after):
    edge = shape((6, 2, 1, 32, 256))
    leading, last = call(edges_body, (edge, edge))(before, array, after)
    up = [(i, i + 1) for i in range(7)]
    down = [(j, i) for i, j in up]
    return lax.ppermute(last, "sy", up), lax.ppermute(leading, "sy", down)


def swap_cores(array):
    return lax.ppermute(array, "sample", [(0, 1), (1, 0)])


def swap_sides(array):
    return lax.ppermute(array, "sy", [(i, i + 1 - 2 * (i % 2)) for i in range(8)])


def spread(own, got):
    pieces = call(join_body, tuple(shape((2, 256, 128)) for _ in range(4)))(own, got)
    moved = [
        lax.ppermute(pieces[d], "sy", [(i, (i // 2 + d) % 4 * 2 + i % 2) for i in range(8)]) for d in range(1, 4)
    ]
    return [pieces[0], *moved]


def padded_bytes(x):
    dims = [1, *x.shape]
    lanes, rows = -(-dims[-1] // 128) * 128, -(-dims[-2] // 16) * 16
    size = lanes * rows * jnp.dtype(x.dtype).itemsize
    for dim in dims[:-2]:
        size *= dim
    return size


def call(body, out, scratch=(), far=(), far_out=()):
    outs = list(out) if isinstance(out, tuple) else [out]

    def run(*args):
        scalars = [x.dtype == jnp.int32 for x in args]
        held = list(far)
        written = list(far_out)

        def kernel(*refs):
            count = len(args) + len(outs)
            near = list(refs[:count])
            extra = refs[count:]
            sems = extra[-1]
            copies = []
            for at, n in enumerate(held):
                near[n] = extra[at]
                copies.append(pltpu.make_async_copy(refs[n], near[n], sems.at[at]))
            for copy in copies:
                copy.start()
            for at, n in enumerate(written):
                near[len(args) + n] = extra[len(held) + at]
            for copy in copies:
                copy.wait()
            body(*near, *extra[len(held) + len(written) : -1])
            copies = []
            for at, n in enumerate(written):
                to = refs[len(args) + n]
                copies.append(pltpu.make_async_copy(near[len(args) + n], to, sems.at[len(held) + at]))
            for copy in copies:
                copy.start()
            for copy in copies:
                copy.wait()

        rooms = [pltpu.VMEM(args[n].shape, args[n].dtype) for n in held]
        rooms += [pltpu.VMEM(outs[n].shape, outs[n].dtype) for n in written]
        rooms += list(scratch)
        total = sum(padded_bytes(x) for x in rooms)
        total += sum(padded_bytes(x) for n, x in enumerate(args) if n not in far)
        total += sum(padded_bytes(x) for n, x in enumerate(outs) if n not in far_out)
        specs = [SMEM if scalars[n] else FAR if n in far else FULL for n in range(len(args))]
        result = pl.pallas_call(
            kernel,
            out_shape=[pltpu.HBM(x.shape, x.dtype) if n in far_out else x for n, x in enumerate(outs)],
            in_specs=specs,
            out_specs=[FAR if n in far_out else FULL for n in range(len(outs))],
            scratch_shapes=[*rooms, pltpu.SemaphoreType.DMA((len(held) + len(written) + 1,))],
            compiler_params=pltpu.CompilerParams(vmem_limit_bytes=total + (3 << 20)),
        )(*[pltpu.with_memory_space_constraint(x, pltpu.HBM) if n in held else x for n, x in enumerate(args)])
        return result if isinstance(out, tuple) else result[0]

    return run


def shape(dims, dtype=BF16):
    return jax.ShapeDtypeStruct(dims, dtype)


def turn(parts):
    a = parts
    lane = lax.broadcasted_iota(jnp.int32, a[0].shape, 1)
    low = lane < 64
    even = (lane // 32) % 2 == 0

    def pair(x, y, mask, step):
        first = jnp.where(mask, x, pltpu.roll(y, step, 1))
        second = jnp.where(mask, pltpu.roll(x, 128 - step, 1), y)
        return first, second

    a0, a2 = pair(a[0], a[2], low, 64)
    a1, a3 = pair(a[1], a[3], low, 64)
    b0, b1 = pair(a0, a1, even, 32)
    b2, b3 = pair(a2, a3, even, 32)
    return [b0, b1, b2, b3]


def pack_kernel_body(core, taps, out):
    rows = []
    for t in range(HALF // 2):
        one = taps[core[0] * HALF + 2 * t].astype(F32)
        two = taps[core[0] * HALF + 2 * t + 1].astype(F32)
        rows.append(jnp.concatenate([one[:16], one[16:], two[:16], two[16:]], axis=1))
    block = jnp.concatenate(rows, axis=0).astype(BF16)
    out[...] = jnp.broadcast_to(block[None], out.shape)


def unpack_kernel_body(mine, out):
    def step(n, carry):
        for t in range(HALF // 2):
            for high in range(2):
                parts = [mine[8 * n + high * 4 + s, 16 * t : 16 * t + 16, :] for s in range(4)]
                for g, part in enumerate(turn(parts)):
                    rows = pl.ds(32 * n + 16 * (g % 2), 16)
                    out[2 * t + g // 2, rows, 128 * high : 128 * high + 128] = part
        return carry

    lax.fori_loop(0, 8, step, 0)


def pack_grad_body(kept, received, out):
    def step(n, carry):
        for t in range(HALF // 2):
            for high in range(2):
                parts = []
                for g in range(4):
                    slot, rows = 2 * t + g // 2, pl.ds(32 * n + 16 * (g % 2), 16)
                    lanes = pl.ds(128 * high, 128)
                    total = kept[slot, rows, lanes].astype(F32) + received[slot, rows, lanes].astype(F32)
                    parts.append(total.astype(BF16))
                for s, part in enumerate(turn(parts)):
                    out[8 * (high * 4 + s) + n, 16 * t : 16 * t + 16, :] = part
        return carry

    lax.fori_loop(0, 8, step, 0)


def sum_grad_body(blocks, out):
    total = blocks[0].astype(F32)
    for n in range(1, 64):
        total = total + blocks[n].astype(F32)
    out[...] = total


def unpack_grad_body(core, mine, other, out):
    zero = core[0] == 0
    first = jnp.where(zero, mine[...], other[...])
    second = jnp.where(zero, other[...], mine[...])
    for start, source in ((0, first), (13, second)):
        for t in range(HALF // 2):
            rows = source[16 * t : 16 * t + 16]
            for u in range(2):
                piece = jnp.concatenate([rows[:, 64 * u : 64 * u + 32], rows[:, 64 * u + 32 : 64 * u + 64]], axis=0)
                out[start + 2 * t + u] = piece.T


def blocks_of(place, turn_by, d):
    x, z = place[0] // 2, place[0] % 2
    column = (x + 4 + turn_by * d) % 4 * 2
    return column + z, column + 1 - z


def pack_cotangent_body(place, cot, keep, send):
    for d in range(4):
        for out, at in zip((keep, send), blocks_of(place, 1, d)):
            for s in range(2):
                parts = [cot[p, s, pl.ds(at * 4, 4)].reshape(128, 32).astype(F32) for p in range(4)]
                out[d, 128 * s : 128 * s + 128, :] = jnp.concatenate(parts, axis=1).astype(BF16)


def join_body(own, got, *outs):
    for d in range(4):
        outs[d][0] = own[d]
        outs[d][1] = got[d]


def unpack_output_body(place, *refs):
    out = refs[4]
    for d in range(4):
        for n, at in enumerate(blocks_of(place, -1, d)):
            for s in range(2):
                rows = refs[d][n, 128 * s : 128 * s + 128, :].astype(F32)
                for p in range(4):
                    out[p, s, pl.ds(at * 4, 4)] = rows[:, 32 * p : 32 * p + 32].reshape(4, 32, 32).astype(BF16)


def fill_shifts(pieces, target, window):
    middle, before, after, left, right = pieces
    window[0, :, 32:160, :] = before[0].reshape(2, 128, 256)
    window[1:5, :, 32:160, :] = middle[...].reshape(4, 2, 128, 256)
    window[5, :, 32:160, :] = after[0].reshape(2, 128, 256)
    window[:, :, 0:32, :] = left[...].reshape(6, 2, 32, 256)
    window[:, :, 160:192, :] = right[...].reshape(6, 2, 32, 256)
    row = lax.broadcasted_iota(jnp.int32, (192, 256), 0) % 32

    def plane(n, carry):
        a, s = n // 2, n % 2
        x = window[a, s]
        wide = x.astype(F32)
        up = jnp.where(row == 0, 0.0, pltpu.roll(wide, 1, 0))
        down = jnp.where(row == 31, 0.0, pltpu.roll(wide, 191, 0))
        target[a, s, :, 0:256] = up.astype(BF16)
        target[a, s, :, 256:512] = x
        target[a, s, :, 512:768] = down.astype(BF16)
        return carry

    lax.fori_loop(0, 12, plane, 0)


def by_core(core, run, swap=0):
    @pl.when(core[0] == swap)
    def _():
        run(0)

    @pl.when(core[0] == 1 - swap)
    def _():
        run(1)


def edges_body(before, array, after, leading, last):
    for out, at in ((leading, 0), (last, 3)):
        out[0, :, 0] = before[0, :, at]
        out[1:5, :, 0] = array[:, :, at]
        out[5, :, 0] = after[0, :, at]


def prepare_body(middle, before, after, left, right, shifts, window):
    fill_shifts((middle, before, after, left, right), shifts, window)


def groups_of(half):
    groups = []
    for tap in range(HALF * half, min(27, HALF * half + HALF)):
        i, j, k = tap // 9, tap // 3 % 3, tap % 3
        if groups and groups[-1][:2] == (i, j):
            groups[-1] = (i, j, groups[-1][2], groups[-1][3] + 1, groups[-1][4])
        else:
            groups.append((i, j, k, 1, tap - HALF * half))
    return groups


def conv_rows(shifts, weights, p, half):
    total = None
    for i, j, k, count, slot in groups_of(half):
        lanes = pl.ds(256 * k, 256 * count)
        lhs = shifts[p + i, :, 32 * j : 32 * j + 128, lanes].reshape(256, 256 * count)
        rhs = weights[slot : slot + count].reshape(256 * count, 256)
        term = jnp.dot(lhs, rhs, preferred_element_type=F32)
        total = term if total is None else total + term
    if half:
        total = total + weights[13, 0:1, :].astype(F32)
    return total


def forward_first_body(core, shifts, mine, partial):
    def run(half):
        def plane(p, carry):
            partial[p] = conv_rows(shifts, mine, p, half)
            return carry

        lax.fori_loop(0, 4, plane, 0)

    by_core(core, run)


def forward_second_body(core, place, shifts, other, partial, r0, r1, r2, r3, grad_pre, keep, send, blocks, cots, outs):
    for d, block in enumerate((r0, r1, r2, r3)):
        for n, at in enumerate(blocks_of(place, -1, d)):
            blocks[at] = block[n]
    for high in range(2):
        parts = turn([blocks[high * 4 + n] for n in range(4)])
        for p in range(4):
            cots[p, :, 128 * high : 128 * high + 128] = parts[p]

    def run(half):
        def plane(p, carry):
            hidden = partial[p] + conv_rows(shifts, other, p, half)
            gate = 1.0 / (1.0 + jnp.exp(-hidden))
            outs[p] = (hidden * gate).astype(BF16)
            slope = gate * (1.0 + hidden * (1.0 - gate))
            grad_pre[p] = (cots[p].astype(F32) * slope).astype(BF16).reshape(2, 4, 32, 256)
            return carry

        lax.fori_loop(0, 4, plane, 0)

    by_core(core, run, 1)
    for high in range(2):
        parts = turn([outs[p, :, 128 * high : 128 * high + 128] for p in range(4)])
        for n in range(4):
            blocks[high * 4 + n] = parts[n]
    for d in range(4):
        for out, at in zip((keep, send), blocks_of(place, 1, d)):
            out[d] = blocks[at]


def tap_grads(shifts, turned, out, half):
    for i in range(3):
        for j in range(3):
            taps = [k for k in range(3) if 13 * half <= 9 * i + 3 * j + k < 13 * half + HALF]
            if taps:
                lanes = pl.ds(256 * taps[0], 256 * len(taps))
                rhs = shifts[i : i + 4, :, 32 * j : 32 * j + 128, lanes].reshape(1024, 256 * len(taps))
                res = jnp.dot(turned[...], rhs, preferred_element_type=F32).astype(BF16)
                for n, k in enumerate(taps):
                    out[9 * i + 3 * j + k - 13 * half] = res[:, 256 * n : 256 * n + 256]


def give_grads_body(core, shifts, grad_pre, out, turned):
    for p in range(4):
        turned[:, 256 * p : 256 * p + 256] = grad_pre[p].reshape(256, 256).astype(F32).T.astype(BF16)
    by_core(core, lambda half: tap_grads(shifts, turned, out, half), 1)


def keep_grads_body(core, shifts, turned, out):
    by_core(core, lambda half: tap_grads(shifts, turned, out, half))


def input_grad_body(core, middle, before, after, left, right, mine, other, out, shifts, window):
    fill_shifts((middle, before, after, left, right), shifts, window)

    def run(half):
        first, second = (other, mine) if half else (mine, other)

        def plane(p, carry):
            total = jnp.zeros((256, 256), F32)
            for i in range(3):
                for j in range(3):
                    for k in range(3):
                        tap = 9 * i + 3 * j + k
                        rhs = first[tap] if tap < HALF else second[tap - HALF]
                        lanes = pl.ds(256 * (2 - k), 256)
                        lhs = shifts[p + 2 - i, :, 32 * (2 - j) : 32 * (2 - j) + 128, lanes].reshape(256, 256)
                        total = total + lax.dot_general(
                            lhs, rhs, (((1,), (1,)), ((), ())), preferred_element_type=F32
                        )
            out[p] = total.astype(BF16).reshape(2, 128, 256)
            return carry

        lax.fori_loop(0, 4, plane, 0)

    by_core(core, run)


SMEM = pl.BlockSpec(memory_space=pltpu.SMEM)
FULL = pl.BlockSpec(memory_space=pltpu.VMEM)
FAR = pl.BlockSpec(memory_space=pltpu.HBM)


def local(features, kernel, filter_bias, cotangent):
    core = lax.axis_index("sample").astype(jnp.int32)
    index = core[None]
    bias = jnp.broadcast_to(filter_bias[None, None, :], (1, 32, 32))
    taps = jnp.concatenate([kernel.reshape(27, 32, 32), bias], axis=0)
    place = lax.axis_index("sy").astype(jnp.int32)[None]
    four = shape((4, 256, 128))
    blocks = call(pack_kernel_body, shape((64, 112, 128)), far_out=(0,))(index, taps)
    keep, send = call(pack_cotangent_body, (four, four))(place, cotangent)
    before, after = halo(features, "sx", 0)
    got = swap_sides(send)
    blocks = lax.all_to_all(blocks, GRID, 0, 0, tiled=True)
    before, after, blocks, got = lax.optimization_barrier((before, after, blocks, got))
    left, right = corners(before, features, after)
    cot = spread(keep, got)
    mine = call(unpack_kernel_body, shape((HALF, 256, 256)), far=(0,))(blocks)
    other = swap_cores(mine)
    shifts = call(prepare_body, shape((6, 2, 192, 768)), [pltpu.VMEM((6, 2, 192, 256), BF16)])(
        features, before, after, left, right
    )
    planes = shape((4, 256, 256), F32)
    partial = call(forward_first_body, planes)(index, shifts, mine)
    grad_pre, keep, send = call(
        forward_second_body,
        (shape((4, 2, 4, 32, 256)), four, four),
        [pltpu.VMEM((8, 256, 128), BF16), pltpu.VMEM((4, 256, 256), BF16), pltpu.VMEM((4, 256, 256), BF16)],
    )(index, place, shifts, other, partial, *cot)
    before, after = halo(grad_pre, "sx", 0)
    got = swap_sides(send)
    given, turned = call(give_grads_body, (shape((HALF, 256, 256)), shape((256, 1024))))(index, shifts, grad_pre)
    given, before, after, got = lax.optimization_barrier((given, before, after, got))
    received = swap_cores(given)
    left, right = corners(before, grad_pre, after)
    kept = call(keep_grads_body, shape((HALF, 256, 256)))(index, shifts, turned)
    blocks = call(pack_grad_body, shape((64, 112, 128)), far_out=(0,))(kept, received)
    blocks, left, right, keep, got = lax.optimization_barrier((blocks, left, right, keep, got))
    blocks = lax.all_to_all(blocks, GRID, 0, 0, tiled=True)
    pieces = spread(keep, got)
    input_grad = call(
        input_grad_body,
        shape((4, 2, 128, 256)),
        [pltpu.VMEM((6, 2, 192, 768), BF16), pltpu.VMEM((6, 2, 192, 256), BF16)],
        far=(1, 2, 3, 4, 5, 6, 7),
    )(index, grad_pre, before, after, left, right, mine, other)
    blocks, input_grad = lax.optimization_barrier((blocks, input_grad))
    rows = call(sum_grad_body, shape((112, 128), F32))(blocks)
    kernel_grad = call(unpack_grad_body, shape((27, 32, 32), F32))(index, rows, swap_cores(rows))
    output = call(unpack_output_body, shape((4, 2, 32, 32, 32)))(place, *pieces)
    return (output, input_grad.reshape(4, 2, 4, 32, 256), kernel_grad.reshape(3, 3, 3, 32, 32))


def solution(mesh):
    return jax.shard_map(
        local,
        mesh=mesh,
        in_specs=(
            P("sx", "sample", "sy", None, None),
            P(None, None, None, "sx", "sy"),
            P("sy"),
            P("sx", "sample", None, None, "sy"),
        ),
        out_specs=(
            P("sx", "sample", None, None, "sy"),
            P("sx", "sample", "sy", None, None),
            P(None, None, None, "sx", "sy"),
        ),
        check_vma=False,
    )
```

time: 163 us -> 142 us (0.87); the launches traced: 160 us -> 141 us
  waiting for transfers between devices: 55.8 us -> 47.2 us
  local copies, waits for them, and re-layouts: 11.4 us -> 3.07 us
  Pallas kernels: 37.2 us -> 32.9 us
  starting transfers between devices: 52.1 us -> 55.6 us
  other arithmetic: 2.63 us -> 0.98 us
    ppermute x8 -> x4, waiting for transfers between devices: 52.8 us -> 18.2 us  [halo(): return (lax.ppermute(last, axis, up), lax.ppermute(leading, axis, down))]
    ppermute x0 -> x12, starting transfers between devices: none -> 20.4 us  [the longest x4 12.4 us: corners(): return (lax.ppermute(last, 'sy', up), lax.ppermute(leading, 'sy', down))]
    ppermute x0 -> x12, waiting for transfers between devices: none -> 16.8 us  [the longest x2 9.54 us: swap_sides(): lax.ppermute(array, 'sy', [(i, i + 1 - 2 * (i % 2)) for i in range(8)])]
    all_to_all x3 -> x0, starting transfers between devices: 16.2 us -> none  [the longest x1 7.73 us: local(): lax.all_to_all(blocks.reshape(64, 112, 128), GRID, 0, 0, tiled=True)]
    ppermute x8 -> x4, starting transfers between devices: 21.3 us -> 6.98 us  [halo(): return (lax.ppermute(last, axis, up), lax.ppermute(leading, axis, down))]
    all_to_all x1 -> x2, waiting for transfers between devices: 0.88 us -> 12.1 us  [local(): blocks = lax.all_to_all(blocks, GRID, 0, 0, tiled=True)]
    all_to_all x1 -> x2, starting transfers between devices: 11.1 us -> 19.8 us  [local(): blocks = lax.all_to_all(blocks, GRID, 0, 0, tiled=True)]
    unnamed x24 -> x18, local copies, waits for them, and re-layouts: 9.11 us -> 2.38 us
  transfers between devices with their start and end apart: 15 -> 21, of which waited for: 11 -> 10; matrix products, arithmetic and copies ran while one was open for 1% -> 0% of each run, Pallas kernels for 11% -> 16%
where the time goes in v2:
time: 142 us; the launch traced here: 141 us
  starting transfers between devices  55.6 us (39%)
  waiting for transfers between devices  47.2 us (33%)
  Pallas kernels  32.9 us (23%)
  local copies, waits for them, and re-layouts  3.07 us (2%)
    pallas_call x17, Pallas kernels, run(): pl.pallas_call(kernel, out_shape=[pltpu.HBM(x.shape, x.dtype) if n in far...  32.9 us
    all_to_all x2, starting transfers between devices, local(): blocks = lax.all_to_all(blocks, GRID, 0, 0, tiled=True)  19.8 us
    ppermute x4, waiting for transfers between devices, halo(): return (lax.ppermute(last, axis, up), lax.ppermute(leading, axis, down))  18.2 us
    ppermute x4, starting transfers between devices, corners(): return (lax.ppermute(last, 'sy', up), lax.ppermute(leading, 'sy', down))  12.4 us
    all_to_all x2, waiting for transfers between devices, local(): blocks = lax.all_to_all(blocks, GRID, 0, 0, tiled=True)  12.1 us
    ppermute x2, waiting for transfers between devices, swap_sides(): lax.ppermute(array, 'sy', [(i, i + 1 - 2 * (i % 2)) for i in range(8)])  9.54 us
    ppermute x3, starting transfers between devices, swap_cores(): return lax.ppermute(array, 'sample', [(0, 1), (1, 0)])  8.47 us
    ppermute x4, waiting for transfers between devices, corners(): return (lax.ppermute(last, 'sy', up), lax.ppermute(leading, 'sy', down))  6.99 us
  transfers between devices with their start and end apart: 21, of which 10 were waited for; matrix products, arithmetic and copies ran while one was open for 0% of the time, Pallas kernels for 16%

profile of v2, /device:TPU:3, one launch (start us, length us, event | category | flops | bytes accessed | tf_op | source)
XLA Modules:
  0.0 140.9 jit_solution(13944102639571173579)
XLA Ops:
  3.7 11.1 %all-to-all-start = ((bf16[64,112,128]{2,1,0:T(8,128)(2,1)}), bf16[64,112,128]{2,1,0:T(8,128)(2,1)}, u32[]{:S(2)}, u32[]{:S(2)}) async-start(bf16[64,112,128]{2,1,0:T(8,128)(2,1)} %shard_map.67), calls=%async_computation | async-start | bytes 3670016 | tf_op jit(solution)/shard_map/all_to_all | solution.py:393
  18.3 3.1 %collective-permute-start = (bf16[1,2,4,32,256]{4,3,2,1,0:T(8,128)(2,1)S(1)}, bf16[1,2,4,32,256]{4,3,2,1,0:T(8,128)(2,1)S(1)}, u32[]{:S(2)}, u32[]{:S(2)}) collective-permute-start(bf16[1,2,4,32,256]{4,3,2,1,0:T(8,128)(2,1)S(1)} %get-tuple-element.74), channel_id=1, source_target_pairs={{0,8},{8,16},{16,24},{24,32},{32,40},{40,48},{48,56},{1,9},{9,17},... | collective-permute-start | bytes 393224 | tf_op jit(solution)/shard_map/ppermute | solution.py:20
  22.7 13.3 %collective-permute-done.refs_0_.refs_1_ = bf16[1,2,4,32,256]{4,3,2,1,0:T(8,128)(2,1)S(1)} collective-permute-done((bf16[1,2,4,32,256]{4,3,2,1,0:T(8,128)(2,1)S(1)}, bf16[1,2,4,32,256]{4,3,2,1,0:T(8,128)(2,1)S(1)}, u32[]{:S(2)}, u32[]{:S(2)}) %collective-permute-start) | collective-permute-done | bytes 131104 | tf_op jit(solution)/shard_map/ppermute | solution.py:20
  36.1 2.5 %collective-permute-done.1.refs_2_ = bf16[1,2,4,32,256]{4,3,2,1,0:T(8,128)(2,1)S(1)} collective-permute-done((bf16[1,2,4,32,256]{4,3,2,1,0:T(8,128)(2,1)S(1)}, bf16[1,2,4,32,256]{4,3,2,1,0:T(8,128)(2,1)S(1)}, u32[]{:S(2)}, u32[]{:S(2)}) %collective-permute-start.1) | collective-permute-done | bytes 131104 | tf_op jit(solution)/shard_map/ppermute | solution.py:20
  38.6 7.3 %collective-permute-done.2.refs_1_ = bf16[4,256,128]{2,1,0:T(8,128)(2,1)S(1)} collective-permute-done((bf16[4,256,128]{2,1,0:T(8,128)(2,1)S(1)}, bf16[4,256,128]{2,1,0:T(8,128)(2,1)S(1)}, u32[]{:S(2)}, u32[]{:S(2)}) %collective-permute-start.2) | collective-permute-done | bytes 262176 | tf_op jit(solution)/shard_map/ppermute | solution.py:36
  45.9 3.2 %shard_map.71.refs_2_.refs_6_ = bf16[14,256,256]{2,1,0:T(8,128)(2,1)S(1)} custom-call(bf16[64,112,128]{2,1,0:T(8,128)(2,1)} %all-to-all-done.refs_0_), custom_call_target="tpu_custom_call" | custom-call | tf_op jit(solution)/shard_map/pallas_call | solution.py:96
  49.7 2.2 %collective-permute-start.3 = (bf16[6,2,1,32,256]{4,3,2,1,0:T(8,128)(2,1)S(1)}, bf16[6,2,1,32,256]{4,3,2,1,0:T(8,128)(2,1)S(1)}, u32[]{:S(2)}, u32[]{:S(2)}) collective-permute-start(bf16[6,2,1,32,256]{4,3,2,1,0:T(8,128)(2,1)S(1)} %get-tuple-element.40), channel_id=1, source_target_pairs={{0,1},{1,2},{2,3},{3,4},{4,5},{5,6},{6,7},{8,9},{9,10},{10,11},{11... | collective-permute-start | bytes 589832 | tf_op jit(solution)/shard_map/ppermute | solution.py:28
  51.9 4.0 %collective-permute-start.4 = (bf16[6,2,1,32,256]{4,3,2,1,0:T(8,128)(2,1)S(1)}, bf16[6,2,1,32,256]{4,3,2,1,0:T(8,128)(2,1)S(1)}, u32[]{:S(2)}, u32[]{:S(2)}) collective-permute-start(bf16[6,2,1,32,256]{4,3,2,1,0:T(8,128)(2,1)S(1)} %get-tuple-element.41), channel_id=1, source_target_pairs={{1,0},{2,1},{3,2},{4,3},{5,4},{6,5},{7,6},{9,8},{10,9},{11,10},{12... | collective-permute-start | bytes 589832 | tf_op jit(solution)/shard_map/ppermute | solution.py:28
  59.9 3.7 %collective-permute-done.4.refs_4_ = bf16[6,2,1,32,256]{4,3,2,1,0:T(8,128)(2,1)S(1)} collective-permute-done((bf16[6,2,1,32,256]{4,3,2,1,0:T(8,128)(2,1)S(1)}, bf16[6,2,1,32,256]{4,3,2,1,0:T(8,128)(2,1)S(1)}, u32[]{:S(2)}, u32[]{:S(2)}) %collective-permute-start.4) | collective-permute-done | bytes 196640 | tf_op jit(solution)/shard_map/ppermute | solution.py:28
  64.4 2.5 %shard_map.72.refs_4_ = f32[4,256,256]{2,1,0:T(8,128)S(1)} custom-call(s32[1]{0:T(128)} %bitcast.1.refs_0_, bf16[6,2,192,768]{3,2,1,0:T(8,128)(2,1)S(1)} %shard_map.70.refs_1_.refs_2_, bf16[14,256,256]{2,1,0:T(8,128)(2,1)S(1)} %shard_map.71.refs_2_.refs_6_), custom_call_target="tpu_custom_call" | custom-call | tf_op jit(solution)/shard_map/pallas_call | solution.py:96
  67.2 3.8 %shard_map.74 = (bf16[4,2,4,32,256]{4,3,2,1,0:T(8,128)(2,1)S(1)}, bf16[4,256,128]{2,1,0:T(8,128)(2,1)S(1)}, bf16[4,256,128]{2,1,0:T(8,128)(2,1)S(1)}) custom-call(s32[1]{0:T(128)} %bitcast.1.refs_0_, s32[1]{0:T(128)} %bitcast.refs_0_.refs_1_, bf16[6,2,192,768]{3,2,1,0:T(8,128)(2,1)S(1)} %shard_map.70.refs_1_.refs_2_, ...), custom_call_target="tpu_custom_call" | custom-call | tf_op jit(solution)/shard_map/pallas_call | solution.py:96
  73.7 2.3 %shard_map.75 = (bf16[14,256,256]{2,1,0:T(8,128)(2,1)S(1)}, bf16[256,1024]{1,0:T(8,128)(2,1)S(1)}) custom-call(s32[1]{0:T(128)} %bitcast.1.refs_0_, bf16[6,2,192,768]{3,2,1,0:T(8,128)(2,1)S(1)} %shard_map.70.refs_1_.refs_2_, bf16[4,2,4,32,256]{4,3,2,1,0:T(8,128)(2,1)S(1)} %get-tuple-element.49.refs_2_.refs_1_), custom_call_target="tpu_custom_call" | custom-call | tf_op jit(solution)/shard_map/pallas_call | solution.py:96
  76.1 2.3 %collective-permute-done.10.refs_2_.refs_3_ = bf16[1,2,4,32,256]{4,3,2,1,0:T(8,128)(2,1)S(1)} collective-permute-done((bf16[1,2,4,32,256]{4,3,2,1,0:T(8,128)(2,1)S(1)}, bf16[1,2,4,32,256]{4,3,2,1,0:T(8,128)(2,1)S(1)}, u32[]{:S(2)}, u32[]{:S(2)}) %collective-permute-start.10) | collective-permute-done | bytes 131104 | tf_op jit(solution)/shard_map/ppermute | solution.py:20
  78.4 2.2 %collective-permute-done.11.refs_1_ = bf16[4,256,128]{2,1,0:T(8,128)(2,1)S(1)} collective-permute-done((bf16[4,256,128]{2,1,0:T(8,128)(2,1)S(1)}, bf16[4,256,128]{2,1,0:T(8,128)(2,1)S(1)}, u32[]{:S(2)}, u32[]{:S(2)}) %collective-permute-start.11) | collective-permute-done | bytes 262176 | tf_op jit(solution)/shard_map/ppermute | solution.py:36
  80.7 2.3 %collective-permute-start.12 = (bf16[14,256,256]{2,1,0:T(8,128)(2,1)S(1)}, bf16[14,256,256]{2,1,0:T(8,128)(2,1)S(1)}, u32[]{:S(2)}, u32[]{:S(2)}) collective-permute-start(bf16[14,256,256]{2,1,0:T(8,128)(2,1)S(1)} %get-tuple-element.53), channel_id=1, source_target_pairs={{0,64},{64,0},{1,65},{65,1},{2,66},{66,2},{3,67},{67,3},{4,68},{68... | collective-permute-start | bytes 5505032 | tf_op jit(solution)/shard_map/ppermute | solution.py:32
  84.9 4.3 %collective-permute-start.14 = (bf16[6,2,1,32,256]{4,3,2,1,0:T(8,128)(2,1)S(1)}, bf16[6,2,1,32,256]{4,3,2,1,0:T(8,128)(2,1)S(1)}, u32[]{:S(2)}, u32[]{:S(2)}) collective-permute-start(bf16[6,2,1,32,256]{4,3,2,1,0:T(8,128)(2,1)S(1)} %get-tuple-element.57), channel_id=1, source_target_pairs={{1,0},{2,1},{3,2},{4,3},{5,4},{6,5},{7,6},{9,8},{10,9},{11,10},{12... | collective-permute-start | bytes 589832 | tf_op jit(solution)/shard_map/ppermute | solution.py:28
  89.2 2.3 %shard_map.76.refs_0_ = bf16[14,256,256]{2,1,0:T(8,128)(2,1)S(1)} custom-call(s32[1]{0:T(128)} %bitcast.1.refs_0_, bf16[6,2,192,768]{3,2,1,0:T(8,128)(2,1)S(1)} %shard_map.70.refs_1_.refs_2_, bf16[256,1024]{1,0:T(8,128)(2,1)S(1)} %get-tuple-element.50.refs_2_), custom_call_target="tpu_custom_call" | custom-call | tf_op jit(solution)/shard_map/pallas_call | solution.py:96
  91.5 3.2 %shard_map.77 = bf16[64,112,128]{2,1,0:T(8,128)(2,1)} custom-call(bf16[14,256,256]{2,1,0:T(8,128)(2,1)S(1)} %shard_map.76.refs_0_, bf16[14,256,256]{2,1,0:T(8,128)(2,1)S(1)} %collective-permute-done.12.refs_1_), custom_call_target="tpu_custom_call" | custom-call | tf_op jit(solution)/shard_map/pallas_call | solution.py:96
  94.8 2.1 %collective-permute-done.14.refs_5_ = bf16[6,2,1,32,256]{4,3,2,1,0:T(8,128)(2,1)S(1)} collective-permute-done((bf16[6,2,1,32,256]{4,3,2,1,0:T(8,128)(2,1)S(1)}, bf16[6,2,1,32,256]{4,3,2,1,0:T(8,128)(2,1)S(1)}, u32[]{:S(2)}, u32[]{:S(2)}) %collective-permute-start.14) | collective-permute-done | bytes 196640 | tf_op jit(solution)/shard_map/ppermute | solution.py:28
  97.6 8.7 %all-to-all-start.1 = ((bf16[64,112,128]{2,1,0:T(8,128)(2,1)}), bf16[64,112,128]{2,1,0:T(8,128)(2,1)S(1)}, u32[]{:S(2)}, u32[]{:S(2)}) async-start(bf16[64,112,128]{2,1,0:T(8,128)(2,1)} %shard_map.77), calls=%async_computation.1 | async-start | bytes 3670016 | tf_op jit(solution)/shard_map/all_to_all | solution.py:418
  110.2 8.5 %shard_map.81 = bf16[4,2,128,256]{3,2,1,0:T(8,128)(2,1)} custom-call(s32[1]{0:T(128)} %bitcast.1.refs_0_, bf16[4,2,4,32,256]{4,3,2,1,0:T(8,128)(2,1)} %copy-done.2, bf16[1,2,4,32,256]{4,3,2,1,0:T(8,128)(2,1)} %copy-done.5, bf16[1,2,4,32,256]{4,3,2,1,0:T(8,128)(2,1)} %copy-done.6, bf16[6,2,1,32,256]{4,3,2,1,0:T(8,128)(2,1)} %copy-done.7, ...), custom_call_target="tpu_custom_call" | custom-call | tf_op jit(solution)/shard_map/pallas_call | solution.py:96
  118.8 12.1 %all-to-all-done.1.refs_0_ = bf16[64,112,128]{2,1,0:T(8,128)(2,1)S(1)} async-done(((bf16[64,112,128]{2,1,0:T(8,128)(2,1)}), bf16[64,112,128]{2,1,0:T(8,128)(2,1)S(1)}, u32[]{:S(2)}, u32[]{:S(2)}) %all-to-all-start.1) | async-done | bytes 1835040 | tf_op jit(solution)/shard_map/all_to_all | solution.py:418
  131.2 5.6 %collective-permute-start.18 = (f32[112,128]{1,0:T(8,128)S(1)}, f32[112,128]{1,0:T(8,128)S(1)}, u32[]{:S(2)}, u32[]{:S(2)}) collective-permute-start(f32[112,128]{1,0:T(8,128)S(1)} %shard_map.82.refs_1_), channel_id=1, source_target_pairs={{0,64},{64,0},{1,65},{65,1},{2,66},{66,2},{3,67},{67,3},{4,68},{68... | collective-permute-start | bytes 172040 | tf_op jit(solution)/shard_map/ppermute | solution.py:32
  136.8 2.2 %shard_map.80 = bf16[4,2,32,32,32]{4,3,2,1,0:T(8,128)(2,1)} custom-call(s32[1]{0:T(128)} %bitcast.refs_0_.refs_1_, bf16[2,256,128]{2,1,0:T(8,128)(2,1)S(1)} %get-tuple-element.62.refs_1_, bf16[2,256,128]{2,1,0:T(8,128)(2,1)S(1)} %collective-permute-done.15.refs_2_, bf16[2,256,128]{2,1,0:T(8,128)(2,1)S(1)} %collective-permute-done.16.refs_3_, ...), custom_call_target="tpu_custom_call" | custom-call | tf_op jit(solution)/shard_map/pallas_call | solution.py:96
  (57 shorter events, 24.8 us)
Async XLA Ops:
  3.7 42.2 %all-to-all-start = ((bf16[64,112,128]{2,1,0:T(8,128)(2,1)}), bf16[64,112,128]{2,1,0:T(8,128)(2,1)}, u32[]{:S(2)}, u32[]{:S(2)}) async-start(bf16[64,112,128]{2,1,0:T(8,128)(2,1)} %shard_map.67), calls=%async_computation | async-start | bytes 3670016 | tf_op jit(solution)/shard_map/all_to_all | solution.py:393
  17.0 28.9 %collective-permute-start.2 = (bf16[4,256,128]{2,1,0:T(8,128)(2,1)S(1)}, bf16[4,256,128]{2,1,0:T(8,128)(2,1)S(1)}, u32[]{:S(2)}, u32[]{:S(2)}) collective-permute-start(bf16[4,256,128]{2,1,0:T(8,128)(2,1)S(1)} %get-tuple-element.37), channel_id=1, source_target_pairs={{0,1},{1,0},{2,3},{3,2},{4,5},{5,4},{6,7},{7,6},{8,9},{9,8},{10,11... | collective-permute-start | bytes 786440 | tf_op jit(solution)/shard_map/ppermute | solution.py:36
  18.3 17.8 %collective-permute-start = (bf16[1,2,4,32,256]{4,3,2,1,0:T(8,128)(2,1)S(1)}, bf16[1,2,4,32,256]{4,3,2,1,0:T(8,128)(2,1)S(1)}, u32[]{:S(2)}, u32[]{:S(2)}) collective-permute-start(bf16[1,2,4,32,256]{4,3,2,1,0:T(8,128)(2,1)S(1)} %get-tuple-element.74), channel_id=1, source_target_pairs={{0,8},{8,16},{16,24},{24,32},{32,40},{40,48},{48,56},{1,9},{9,17},... | collective-permute-start | bytes 393224 | tf_op jit(solution)/shard_map/ppermute | solution.py:20
  21.4 17.2 %collective-permute-start.1 = (bf16[1,2,4,32,256]{4,3,2,1,0:T(8,128)(2,1)S(1)}, bf16[1,2,4,32,256]{4,3,2,1,0:T(8,128)(2,1)S(1)}, u32[]{:S(2)}, u32[]{:S(2)}) collective-permute-start(bf16[1,2,4,32,256]{4,3,2,1,0:T(8,128)(2,1)S(1)} %get-tuple-element.73), channel_id=1, source_target_pairs={{8,0},{16,8},{24,16},{32,24},{40,32},{48,40},{56,48},{9,1},{17,9},... | collective-permute-start | bytes 393224 | tf_op jit(solution)/shard_map/ppermute | solution.py:20
  49.1 15.3 %copy-start = (bf16[14,256,256]{2,1,0:T(8,128)(2,1)}, bf16[14,256,256]{2,1,0:T(8,128)(2,1)S(1)}, u32[]{:S(2)}) copy-start(bf16[14,256,256]{2,1,0:T(8,128)(2,1)S(1)} %shard_map.71.refs_2_.refs_6_) | copy-start | bytes 5505028
  49.1 18.1 %collective-permute-start.5 = (bf16[14,256,256]{2,1,0:T(8,128)(2,1)S(1)}, bf16[14,256,256]{2,1,0:T(8,128)(2,1)S(1)}, u32[]{:S(2)}, u32[]{:S(2)}) collective-permute-start(bf16[14,256,256]{2,1,0:T(8,128)(2,1)S(1)} %shard_map.71.refs_2_.refs_6_), channel_id=1, source_target_pairs={{0,64},{64,0},{1,65},{65,1},{2,66},{66,2},{3,67},{67,3},{4,68},{68... | collective-permute-start | bytes 5505032 | tf_op jit(solution)/shard_map/ppermute | solution.py:32
  49.7 9.4 %collective-permute-start.3 = (bf16[6,2,1,32,256]{4,3,2,1,0:T(8,128)(2,1)S(1)}, bf16[6,2,1,32,256]{4,3,2,1,0:T(8,128)(2,1)S(1)}, u32[]{:S(2)}, u32[]{:S(2)}) collective-permute-start(bf16[6,2,1,32,256]{4,3,2,1,0:T(8,128)(2,1)S(1)} %get-tuple-element.40), channel_id=1, source_target_pairs={{0,1},{1,2},{2,3},{3,4},{4,5},{5,6},{6,7},{8,9},{9,10},{10,11},{11... | collective-permute-start | bytes 589832 | tf_op jit(solution)/shard_map/ppermute | solution.py:28
  51.9 11.7 %collective-permute-start.4 = (bf16[6,2,1,32,256]{4,3,2,1,0:T(8,128)(2,1)S(1)}, bf16[6,2,1,32,256]{4,3,2,1,0:T(8,128)(2,1)S(1)}, u32[]{:S(2)}, u32[]{:S(2)}) collective-permute-start(bf16[6,2,1,32,256]{4,3,2,1,0:T(8,128)(2,1)S(1)} %get-tuple-element.41), channel_id=1, source_target_pairs={{1,0},{2,1},{3,2},{4,3},{5,4},{6,5},{7,6},{9,8},{10,9},{11,10},{12... | collective-permute-start | bytes 589832 | tf_op jit(solution)/shard_map/ppermute | solution.py:28
  55.9 10.9 %collective-permute-start.6 = (bf16[2,256,128]{2,1,0:T(8,128)(2,1)S(1)}, bf16[2,256,128]{2,1,0:T(8,128)(2,1)S(1)}, u32[]{:S(2)}, u32[]{:S(2)}) collective-permute-start(bf16[2,256,128]{2,1,0:T(8,128)(2,1)S(1)} %get-tuple-element.46), channel_id=1, source_target_pairs={{0,2},{1,3},{2,4},{3,5},{4,6},{5,7},{6,0},{7,1},{8,10},{9,11},{10,... | collective-permute-start | bytes 393224 | tf_op jit(solution)/shard_map/ppermute | solution.py:42
  56.9 9.9 %collective-permute-start.7 = (bf16[2,256,128]{2,1,0:T(8,128)(2,1)S(1)}, bf16[2,256,128]{2,1,0:T(8,128)(2,1)S(1)}, u32[]{:S(2)}, u32[]{:S(2)}) collective-permute-start(bf16[2,256,128]{2,1,0:T(8,128)(2,1)S(1)} %get-tuple-element.47), channel_id=1, source_target_pairs={{0,4},{1,5},{2,6},{3,7},{4,0},{5,1},{6,2},{7,3},{8,12},{9,13},{10,... | collective-permute-start | bytes 393224 | tf_op jit(solution)/shard_map/ppermute | solution.py:42
  59.1 8.1 %collective-permute-start.8 = (bf16[2,256,128]{2,1,0:T(8,128)(2,1)S(1)}, bf16[2,256,128]{2,1,0:T(8,128)(2,1)S(1)}, u32[]{:S(2)}, u32[]{:S(2)}) collective-permute-start(bf16[2,256,128]{2,1,0:T(8,128)(2,1)S(1)} %get-tuple-element.48), channel_id=1, source_target_pairs={{0,6},{1,7},{2,0},{3,1},{4,2},{5,3},{6,4},{7,5},{8,14},{9,15},{10,... | collective-permute-start | bytes 393224 | tf_op jit(solution)/shard_map/ppermute | solution.py:42
  71.0 9.7 %collective-permute-start.11 = (bf16[4,256,128]{2,1,0:T(8,128)(2,1)S(1)}, bf16[4,256,128]{2,1,0:T(8,128)(2,1)S(1)}, u32[]{:S(2)}, u32[]{:S(2)}) collective-permute-start(bf16[4,256,128]{2,1,0:T(8,128)(2,1)S(1)} %get-tuple-element.52), channel_id=1, source_target_pairs={{0,1},{1,0},{2,3},{3,2},{4,5},{5,4},{6,7},{7,6},{8,9},{9,8},{10,11... | collective-permute-start | bytes 786440 | tf_op jit(solution)/shard_map/ppermute | solution.py:36
  71.1 5.0 %collective-permute-start.9 = (bf16[1,2,4,32,256]{4,3,2,1,0:T(8,128)(2,1)S(1)}, bf16[1,2,4,32,256]{4,3,2,1,0:T(8,128)(2,1)S(1)}, u32[]{:S(2)}, u32[]{:S(2)}) collective-permute-start(bf16[1,2,4,32,256]{4,3,2,1,0:T(8,128)(2,1)S(1)} %get-tuple-element.72), channel_id=1, source_target_pairs={{0,8},{8,16},{16,24},{24,32},{32,40},{40,48},{48,56},{1,9},{9,17},... | collective-permute-start | bytes 393224 | tf_op jit(solution)/shard_map/ppermute | solution.py:20
  72.4 6.0 %collective-permute-start.10 = (bf16[1,2,4,32,256]{4,3,2,1,0:T(8,128)(2,1)S(1)}, bf16[1,2,4,32,256]{4,3,2,1,0:T(8,128)(2,1)S(1)}, u32[]{:S(2)}, u32[]{:S(2)}) collective-permute-start(bf16[1,2,4,32,256]{4,3,2,1,0:T(8,128)(2,1)S(1)} %get-tuple-element.71), channel_id=1, source_target_pairs={{8,0},{16,8},{24,16},{32,24},{40,32},{48,40},{56,48},{9,1},{17,9},... | collective-permute-start | bytes 393224 | tf_op jit(solution)/shard_map/ppermute | solution.py:20
  76.1 15.4 %copy-start.5 = (bf16[1,2,4,32,256]{4,3,2,1,0:T(8,128)(2,1)}, bf16[1,2,4,32,256]{4,3,2,1,0:T(8,128)(2,1)S(1)}, u32[]{:S(2)}) copy-start(bf16[1,2,4,32,256]{4,3,2,1,0:T(8,128)(2,1)S(1)} %collective-permute-done.9.refs_0_.refs_2_) | copy-start | bytes 393220
  78.4 13.1 %copy-start.6 = (bf16[1,2,4,32,256]{4,3,2,1,0:T(8,128)(2,1)}, bf16[1,2,4,32,256]{4,3,2,1,0:T(8,128)(2,1)S(1)}, u32[]{:S(2)}) copy-start(bf16[1,2,4,32,256]{4,3,2,1,0:T(8,128)(2,1)S(1)} %collective-permute-done.10.refs_2_.refs_3_) | copy-start | bytes 393220
  80.7 10.9 %collective-permute-start.12 = (bf16[14,256,256]{2,1,0:T(8,128)(2,1)S(1)}, bf16[14,256,256]{2,1,0:T(8,128)(2,1)S(1)}, u32[]{:S(2)}, u32[]{:S(2)}) collective-permute-start(bf16[14,256,256]{2,1,0:T(8,128)(2,1)S(1)} %get-tuple-element.53), channel_id=1, source_target_pairs={{0,64},{64,0},{1,65},{65,1},{2,66},{66,2},{3,67},{67,3},{4,68},{68... | collective-permute-start | bytes 5505032 | tf_op jit(solution)/shard_map/ppermute | solution.py:32
  83.0 11.8 %collective-permute-start.13 = (bf16[6,2,1,32,256]{4,3,2,1,0:T(8,128)(2,1)S(1)}, bf16[6,2,1,32,256]{4,3,2,1,0:T(8,128)(2,1)S(1)}, u32[]{:S(2)}, u32[]{:S(2)}) collective-permute-start(bf16[6,2,1,32,256]{4,3,2,1,0:T(8,128)(2,1)S(1)} %get-tuple-element.56), channel_id=1, source_target_pairs={{0,1},{1,2},{2,3},{3,4},{4,5},{5,6},{6,7},{8,9},{9,10},{10,11},{11... | collective-permute-start | bytes 589832 | tf_op jit(solution)/shard_map/ppermute | solution.py:28
  84.9 12.0 %collective-permute-start.14 = (bf16[6,2,1,32,256]{4,3,2,1,0:T(8,128)(2,1)S(1)}, bf16[6,2,1,32,256]{4,3,2,1,0:T(8,128)(2,1)S(1)}, u32[]{:S(2)}, u32[]{:S(2)}) collective-permute-start(bf16[6,2,1,32,256]{4,3,2,1,0:T(8,128)(2,1)S(1)} %get-tuple-element.57), channel_id=1, source_target_pairs={{1,0},{2,1},{3,2},{4,3},{5,4},{6,5},{7,6},{9,8},{10,9},{11,10},{12... | collective-permute-start | bytes 589832 | tf_op jit(solution)/shard_map/ppermute | solution.py:28
  97.6 33.3 %all-to-all-start.1 = ((bf16[64,112,128]{2,1,0:T(8,128)(2,1)}), bf16[64,112,128]{2,1,0:T(8,128)(2,1)S(1)}, u32[]{:S(2)}, u32[]{:S(2)}) async-start(bf16[64,112,128]{2,1,0:T(8,128)(2,1)} %shard_map.77), calls=%async_computation.1 | async-start | bytes 3670016 | tf_op jit(solution)/shard_map/all_to_all | solution.py:418
  106.3 30.5 %collective-permute-start.15 = (bf16[2,256,128]{2,1,0:T(8,128)(2,1)S(1)}, bf16[2,256,128]{2,1,0:T(8,128)(2,1)S(1)}, u32[]{:S(2)}, u32[]{:S(2)}) collective-permute-start(bf16[2,256,128]{2,1,0:T(8,128)(2,1)S(1)} %get-tuple-element.63), channel_id=1, source_target_pairs={{0,2},{1,3},{2,4},{3,5},{4,6},{5,7},{6,0},{7,1},{8,10},{9,11},{10,... | collective-permute-start | bytes 393224 | tf_op jit(solution)/shard_map/ppermute | solution.py:42
  107.6 29.3 %collective-permute-start.16 = (bf16[2,256,128]{2,1,0:T(8,128)(2,1)S(1)}, bf16[2,256,128]{2,1,0:T(8,128)(2,1)S(1)}, u32[]{:S(2)}, u32[]{:S(2)}) collective-permute-start(bf16[2,256,128]{2,1,0:T(8,128)(2,1)S(1)} %get-tuple-element.64), channel_id=1, source_target_pairs={{0,4},{1,5},{2,6},{3,7},{4,0},{5,1},{6,2},{7,3},{8,12},{9,13},{10,... | collective-permute-start | bytes 393224 | tf_op jit(solution)/shard_map/ppermute | solution.py:42
  108.6 28.2 %collective-permute-start.17 = (bf16[2,256,128]{2,1,0:T(8,128)(2,1)S(1)}, bf16[2,256,128]{2,1,0:T(8,128)(2,1)S(1)}, u32[]{:S(2)}, u32[]{:S(2)}) collective-permute-start(bf16[2,256,128]{2,1,0:T(8,128)(2,1)S(1)} %get-tuple-element.65), channel_id=1, source_target_pairs={{0,6},{1,7},{2,0},{3,1},{4,2},{5,3},{6,4},{7,5},{8,14},{9,15},{10,... | collective-permute-start | bytes 393224 | tf_op jit(solution)/shard_map/ppermute | solution.py:42
  131.2 7.9 %collective-permute-start.18 = (f32[112,128]{1,0:T(8,128)S(1)}, f32[112,128]{1,0:T(8,128)S(1)}, u32[]{:S(2)}, u32[]{:S(2)}) collective-permute-start(f32[112,128]{1,0:T(8,128)S(1)} %shard_map.82.refs_1_), channel_id=1, source_target_pairs={{0,64},{64,0},{1,65},{65,1},{2,66},{66,2},{3,67},{67,3},{4,68},{68... | collective-permute-start | bytes 172040 | tf_op jit(solution)/shard_map/ppermute | solution.py:32
  (6 other events, 23.6 us)

commit v3 on v2

--- a/solution.py
+++ b/solution.py
@@ -218,12 +218,13 @@
 
 
 def fill_shifts(pieces, target, window):
-    middle, before, after, left, right = pieces
+    middle, before, after = pieces[:3]
     window[0, :, 32:160, :] = before[0].reshape(2, 128, 256)
     window[1:5, :, 32:160, :] = middle[...].reshape(4, 2, 128, 256)
     window[5, :, 32:160, :] = after[0].reshape(2, 128, 256)
-    window[:, :, 0:32, :] = left[...].reshape(6, 2, 32, 256)
-    window[:, :, 160:192, :] = right[...].reshape(6, 2, 32, 256)
+    for at, side in zip((0, 160), pieces[3:]):
+        rows = jnp.zeros((6, 2, 32, 256), BF16) if side is None else side[...].reshape(6, 2, 32, 256)
+        window[:, :, at : at + 32, :] = rows
     row = lax.broadcasted_iota(jnp.int32, (192, 256), 0) % 32
 
     def plane(n, carry):
@@ -255,10 +256,6 @@
         out[0, :, 0] = before[0, :, at]
         out[1:5, :, 0] = array[:, :, at]
         out[5, :, 0] = after[0, :, at]
-
-
-def prepare_body(middle, before, after, left, right, shifts, window):
-    fill_shifts((middle, before, after, left, right), shifts, window)
 
 
 def groups_of(half):
@@ -285,7 +282,9 @@
     return total
 
 
-def forward_first_body(core, shifts, mine, partial):
+def forward_first_body(core, middle, before, after, left, right, mine, shifts, partial, window):
+    fill_shifts((middle, before, after, left, right), shifts, window)
+
     def run(half):
         def plane(p, carry):
             partial[p] = conv_rows(shifts, mine, p, half)
@@ -296,8 +295,9 @@
     by_core(core, run)
 
 
-def forward_second_body(core, place, shifts, other, partial, r0, r1, r2, r3, grad_pre, keep, send, blocks, cots, outs):
-    for d, block in enumerate((r0, r1, r2, r3)):
+def forward_second_body(core, place, shifts, other, partial, *refs):
+    grad_pre, keep, send, given, turned, blocks, cots, outs = refs[4:]
+    for d, block in enumerate(refs[:4]):
         for n, at in enumerate(blocks_of(place, -1, d)):
             blocks[at] = block[n]
     for high in range(2):
@@ -324,6 +324,9 @@
     for d in range(4):
         for out, at in zip((keep, send), blocks_of(place, 1, d)):
             out[d] = blocks[at]
+    for p in range(4):
+        turned[:, 256 * p : 256 * p + 256] = grad_pre[p].reshape(256, 256).astype(F32).T.astype(BF16)
+    by_core(core, lambda half: tap_grads(shifts, turned, given, half), 1)
 
 
 def tap_grads(shifts, turned, out, half):
@@ -338,38 +341,61 @@
                     out[9 * i + 3 * j + k - 13 * half] = res[:, 256 * n : 256 * n + 256]
 
 
-def give_grads_body(core, shifts, grad_pre, out, turned):
-    for p in range(4):
-        turned[:, 256 * p : 256 * p + 256] = grad_pre[p].reshape(256, 256).astype(F32).T.astype(BF16)
-    by_core(core, lambda half: tap_grads(shifts, turned, out, half), 1)
-
-
-def keep_grads_body(core, shifts, turned, out):
-    by_core(core, lambda half: tap_grads(shifts, turned, out, half))
-
-
-def input_grad_body(core, middle, before, after, left, right, mine, other, out, shifts, window):
-    fill_shifts((middle, before, after, left, right), shifts, window)
+def keep_grads_body(core, shifts, turned, received, out, kept):
+    by_core(core, lambda half: tap_grads(shifts, turned, kept, half))
+    pack_grad_body(kept, received, out)
+
+
+def weight_of(mine, other, half, tap):
+    first, second = (other, mine) if half else (mine, other)
+    return first[tap] if tap < HALF else second[tap - HALF]
+
+
+def back_dot(rows, weight):
+    return lax.dot_general(rows, weight, (((1,), (1,)), ((), ())), preferred_element_type=F32)
+
+
+def input_grad_body(core, middle, before, after, mine, other, inner, edges, shifts, window):
+    fill_shifts((middle, before, after, None, None), shifts, window)
 
     def run(half):
-        first, second = (other, mine) if half else (mine, other)
-
         def plane(p, carry):
             total = jnp.zeros((256, 256), F32)
             for i in range(3):
                 for j in range(3):
                     for k in range(3):
-                        tap = 9 * i + 3 * j + k
-                        rhs = first[tap] if tap < HALF else second[tap - HALF]
                         lanes = pl.ds(256 * (2 - k), 256)
                         lhs = shifts[p + 2 - i, :, 32 * (2 - j) : 32 * (2 - j) + 128, lanes].reshape(256, 256)
-                        total = total + lax.dot_general(
-                            lhs, rhs, (((1,), (1,)), ((), ())), preferred_element_type=F32
-                        )
-            out[p] = total.astype(BF16).reshape(2, 128, 256)
+                        total = total + back_dot(lhs, weight_of(mine, other, half, 9 * i + 3 * j + k))
+            rows = total.reshape(2, 4, 32, 256)
+            inner[p] = rows[:, 1:3].astype(BF16)
+            edges[p, :, 0] = rows[:, 0]
+            edges[p, :, 1] = rows[:, 3]
             return carry
 
         lax.fori_loop(0, 4, plane, 0)
+
+    by_core(core, run)
+
+
+def edge_grad_body(core, left, right, mine, other, inner, edges, out, shifts):
+    row = lax.broadcasted_iota(jnp.int32, (384, 256), 0) % 32
+    for n, side in enumerate((left, right)):
+        wide = side[...].reshape(384, 256).astype(F32)
+        up = jnp.where(row == 0, 0.0, pltpu.roll(wide, 1, 0))
+        down = jnp.where(row == 31, 0.0, pltpu.roll(wide, 383, 0))
+        for k, part in enumerate((up, wide, down)):
+            shifts[n, k] = part.astype(BF16).reshape(6, 64, 256)
+    out[:, :, 1:3] = inner[...]
+
+    def run(half):
+        for n, (at, j) in enumerate(((0, 2), (3, 0))):
+            total = edges[:, :, n].reshape(256, 256)
+            for i in range(3):
+                for k in range(3):
+                    lhs = shifts[n, 2 - k, 2 - i : 6 - i].reshape(256, 256)
+                    total = total + back_dot(lhs, weight_of(mine, other, half, 9 * i + 3 * j + k))
+            out[:, :, at] = total.astype(BF16).reshape(4, 2, 32, 256)
 
     by_core(core, run)
 
@@ -390,44 +416,56 @@
     keep, send = call(pack_cotangent_body, (four, four))(place, cotangent)
     before, after = halo(features, "sx", 0)
     got = swap_sides(send)
+    blocks, before, after, keep, got = lax.optimization_barrier((blocks, before, after, keep, got))
     blocks = lax.all_to_all(blocks, GRID, 0, 0, tiled=True)
-    before, after, blocks, got = lax.optimization_barrier((before, after, blocks, got))
     left, right = corners(before, features, after)
     cot = spread(keep, got)
     mine = call(unpack_kernel_body, shape((HALF, 256, 256)), far=(0,))(blocks)
+    mine, left, right, *cot = lax.optimization_barrier((mine, left, right, *cot))
     other = swap_cores(mine)
-    shifts = call(prepare_body, shape((6, 2, 192, 768)), [pltpu.VMEM((6, 2, 192, 256), BF16)])(
-        features, before, after, left, right
-    )
-    planes = shape((4, 256, 256), F32)
-    partial = call(forward_first_body, planes)(index, shifts, mine)
-    grad_pre, keep, send = call(
+    shifts, partial = call(
+        forward_first_body,
+        (shape((6, 2, 192, 768)), shape((4, 256, 256), F32)),
+        [pltpu.VMEM((6, 2, 192, 256), BF16)],
+    )(index, features, before, after, left, right, mine)
+    grad_pre, keep, send, given, turned = call(
         forward_second_body,
-        (shape((4, 2, 4, 32, 256)), four, four),
+        (shape((4, 2, 4, 32, 256)), four, four, shape((HALF, 256, 256)), shape((256, 1024))),
         [pltpu.VMEM((8, 256, 128), BF16), pltpu.VMEM((4, 256, 256), BF16), pltpu.VMEM((4, 256, 256), BF16)],
     )(index, place, shifts, other, partial, *cot)
     before, after = halo(grad_pre, "sx", 0)
     got = swap_sides(send)
-    given, turned = call(give_grads_body, (shape((HALF, 256, 256)), shape((256, 1024))))(index, shifts, grad_pre)
-    given, before, after, got = lax.optimization_barrier((given, before, after, got))
     received = swap_cores(given)
+    turned, before, after, got = lax.optimization_barrier((turned, before, after, got))
+    blocks = call(
+        keep_grads_body, shape((64, 112, 128)), [pltpu.VMEM((HALF, 256, 256), BF16)], far_out=(0,)
+    )(index, shifts, turned, received)
+    blocks, before, after, keep, got = lax.optimization_barrier((blocks, before, after, keep, got))
     left, right = corners(before, grad_pre, after)
-    kept = call(keep_grads_body, shape((HALF, 256, 256)))(index, shifts, turned)
-    blocks = call(pack_grad_body, shape((64, 112, 128)), far_out=(0,))(kept, received)
-    blocks, left, right, keep, got = lax.optimization_barrier((blocks, left, right, keep, got))
     blocks = lax.all_to_all(blocks, GRID, 0, 0, tiled=True)
     pieces = spread(keep, got)
+    half = shape((4, 2, 2, 32, 256))
+    inner, edges = call(
+        input_grad_body,
+        (half, shape((4, 2, 2, 32, 256), F32)),
+        [pltpu.VMEM((6, 2, 192, 768), BF16), pltpu.VMEM((6, 2, 192, 256), BF16)],
+        far=(1, 2, 3, 4, 5),
+        far_out=(0, 1),
+    )(index, grad_pre, before, after, mine, other)
+    blocks, inner, edges = lax.optimization_barrier((blocks, inner, edges))
+    rows = call(sum_grad_body, shape((112, 128), F32))(blocks)
+    rows, left, right = lax.optimization_barrier((rows, left, right))
+    turned_rows = swap_cores(rows)
     input_grad = call(
-        input_grad_body,
-        shape((4, 2, 128, 256)),
-        [pltpu.VMEM((6, 2, 192, 768), BF16), pltpu.VMEM((6, 2, 192, 256), BF16)],
-        far=(1, 2, 3, 4, 5, 6, 7),
-    )(index, grad_pre, before, after, left, right, mine, other)
-    blocks, input_grad = lax.optimization_barrier((blocks, input_grad))
-    rows = call(sum_grad_body, shape((112, 128), F32))(blocks)
-    kernel_grad = call(unpack_grad_body, shape((27, 32, 32), F32))(index, rows, swap_cores(rows))
+        edge_grad_body,
+        shape((4, 2, 4, 32, 256)),
+        [pltpu.VMEM((2, 3, 6, 64, 256), BF16)],
+        far=(3, 4, 5, 6),
+    )(index, left, right, mine, other, inner, edges)
+    input_grad, *pieces = lax.optimization_barrier((input_grad, *pieces))
     output = call(unpack_output_body, shape((4, 2, 32, 32, 32)))(place, *pieces)
-    return (output, input_grad.reshape(4, 2, 4, 32, 256), kernel_grad.reshape(3, 3, 3, 32, 32))
+    kernel_grad = call(unpack_grad_body, shape((27, 32, 32), F32))(index, rows, turned_rows)
+    return (output, input_grad, kernel_grad.reshape(3, 3, 3, 32, 32))
 
 
 def solution(mesh):

time: 142 us -> 137 us (0.965)
  waiting for transfers between devices: 47.2 us -> 32.9 us
  Pallas kernels: 32.9 us -> 38.9 us
  starting transfers between devices: 55.6 us -> 61.2 us
    ppermute x4, waiting for transfers between devices: 18.2 us -> 4.78 us  [halo(): return (lax.ppermute(last, axis, up), lax.ppermute(leading, axis, down))]
    ppermute x2, waiting for transfers between devices: 9.54 us -> 0.01 us  [swap_sides(): lax.ppermute(array, 'sy', [(i, i + 1 - 2 * (i % 2)) for i in range(8)])]
    all_to_all x2, starting transfers between devices: 19.8 us -> 26.3 us  [local(): blocks = lax.all_to_all(blocks, GRID, 0, 0, tiled=True)]
    ppermute x3, starting transfers between devices: 8.47 us -> 2.34 us  [swap_cores(): return lax.ppermute(array, 'sample', [(0, 1), (1, 0)])]
    pallas_call x17 -> x15, Pallas kernels: 32.9 us -> 38.9 us  [run(): pl.pallas_call(kernel, out_shape=[pltpu.HBM(x.shape, x.dtype) if n in far...]
    all_to_all x2, waiting for transfers between devices: 12.1 us -> 15.5 us  [local(): blocks = lax.all_to_all(blocks, GRID, 0, 0, tiled=True)]
    ppermute x4, waiting for transfers between devices: 6.99 us -> 10.3 us  [corners(): return (lax.ppermute(last, 'sy', up), lax.ppermute(leading, 'sy', down))]
    ppermute x4, starting transfers between devices: 6.98 us -> 9.79 us  [halo(): return (lax.ppermute(last, axis, up), lax.ppermute(leading, axis, down))]
  transfers between devices with their start and end apart: 21 -> 21, of which waited for: 10 -> 12; matrix products, arithmetic and copies ran while one was open for 0% -> 0% of each run, Pallas kernels for 16% -> 19%
where the time goes in v3:
time: 137 us; the launch traced here: 136 us
  starting transfers between devices  61.2 us (45%)
  Pallas kernels  38.9 us (28%)
  waiting for transfers between devices  32.9 us (24%)
  local copies, waits for them, and re-layouts  1.72 us (1%)
    pallas_call x15, Pallas kernels, run(): pl.pallas_call(kernel, out_shape=[pltpu.HBM(x.shape, x.dtype) if n in far...  38.9 us
    all_to_all x2, starting transfers between devices, local(): blocks = lax.all_to_all(blocks, GRID, 0, 0, tiled=True)  26.3 us
    all_to_all x2, waiting for transfers between devices, local(): blocks = lax.all_to_all(blocks, GRID, 0, 0, tiled=True)  15.5 us
    ppermute x4, starting transfers between devices, corners(): return (lax.ppermute(last, 'sy', up), lax.ppermute(leading, 'sy', down))  12.4 us
    ppermute x4, waiting for transfers between devices, corners(): return (lax.ppermute(last, 'sy', up), lax.ppermute(leading, 'sy', down))  10.3 us
    ppermute x4, starting transfers between devices, halo(): return (lax.ppermute(last, axis, up), lax.ppermute(leading, axis, down))  9.79 us
    ppermute x6, starting transfers between devices, spread(): lax.ppermute(pieces[d], 'sy', [(i, (i // 2 + d) % 4 * 2 + i % 2) for i in...  7.86 us
    ppermute x4, waiting for transfers between devices, halo(): return (lax.ppermute(last, axis, up), lax.ppermute(leading, axis, down))  4.78 us
  transfers between devices with their start and end apart: 21, of which 12 were waited for; matrix products, arithmetic and copies ran while one was open for 0% of the time, Pallas kernels for 19%

profile of v3, /device:TPU:3, one launch (start us, length us, event | category | flops | bytes accessed | tf_op | source)
XLA Modules:
  0.0 135.9 jit_solution(10628918607053133913)
XLA Ops:
  2.8 1.7 %collective-permute-start.2 = (bf16[4,256,128]{2,1,0:T(8,128)(2,1)S(1)}, bf16[4,256,128]{2,1,0:T(8,128)(2,1)S(1)}, u32[]{:S(2)}, u32[]{:S(2)}) collective-permute-start(bf16[4,256,128]{2,1,0:T(8,128)(2,1)S(1)} %get-tuple-element.59), channel_id=1, source_target_pairs={{0,1},{1,0},{2,3},{3,2},{4,5},{5,4},{6,7},{7,6},{8,9},{9,8},{10,11... | collective-permute-start | bytes 786440 | tf_op jit(solution)/shard_map/ppermute | solution.py:36
  4.5 3.2 %collective-permute-start = (bf16[1,2,4,32,256]{4,3,2,1,0:T(8,128)(2,1)S(1)}, bf16[1,2,4,32,256]{4,3,2,1,0:T(8,128)(2,1)S(1)}, u32[]{:S(2)}, u32[]{:S(2)}) collective-permute-start(bf16[1,2,4,32,256]{4,3,2,1,0:T(8,128)(2,1)S(1)} %get-tuple-element.116), channel_id=1, source_target_pairs={{0,8},{8,16},{16,24},{24,32},{32,40},{40,48},{48,56},{1,9},{9,17},... | collective-permute-start | bytes 393224 | tf_op jit(solution)/shard_map/ppermute | solution.py:20
  10.6 2.9 %collective-permute-done.1.refs_2_.refs_3_ = bf16[1,2,4,32,256]{4,3,2,1,0:T(8,128)(2,1)S(1)} collective-permute-done((bf16[1,2,4,32,256]{4,3,2,1,0:T(8,128)(2,1)S(1)}, bf16[1,2,4,32,256]{4,3,2,1,0:T(8,128)(2,1)S(1)}, u32[]{:S(2)}, u32[]{:S(2)}) %collective-permute-start.1) | collective-permute-done | bytes 131104 | tf_op jit(solution)/shard_map/ppermute | solution.py:20
  13.5 12.7 %all-to-all-start = ((bf16[64,112,128]{2,1,0:T(8,128)(2,1)}), bf16[64,112,128]{2,1,0:T(8,128)(2,1)}, u32[]{:S(2)}, u32[]{:S(2)}) async-start(bf16[64,112,128]{2,1,0:T(8,128)(2,1)} %shard_map.67), calls=%async_computation | async-start | bytes 3670016 | tf_op jit(solution)/shard_map/all_to_all | solution.py:420
  27.0 3.1 %collective-permute-start.3 = (bf16[6,2,1,32,256]{4,3,2,1,0:T(8,128)(2,1)}, bf16[6,2,1,32,256]{4,3,2,1,0:T(8,128)(2,1)S(1)}, u32[]{:S(2)}, u32[]{:S(2)}) collective-permute-start(bf16[6,2,1,32,256]{4,3,2,1,0:T(8,128)(2,1)} %get-tuple-element.63), channel_id=1, source_target_pairs={{0,1},{1,2},{2,3},{3,4},{4,5},{5,6},{6,7},{8,9},{9,10},{10,11},{11... | collective-permute-start | bytes 589832 | tf_op jit(solution)/shard_map/ppermute | solution.py:28
  30.1 3.1 %collective-permute-start.4 = (bf16[6,2,1,32,256]{4,3,2,1,0:T(8,128)(2,1)}, bf16[6,2,1,32,256]{4,3,2,1,0:T(8,128)(2,1)S(1)}, u32[]{:S(2)}, u32[]{:S(2)}) collective-permute-start(bf16[6,2,1,32,256]{4,3,2,1,0:T(8,128)(2,1)} %get-tuple-element.64), channel_id=1, source_target_pairs={{1,0},{2,1},{3,2},{4,3},{5,4},{6,5},{7,6},{9,8},{10,9},{11,10},{12... | collective-permute-start | bytes 589832 | tf_op jit(solution)/shard_map/ppermute | solution.py:28
  35.9 2.0 %collective-permute-start.7 = (bf16[2,256,128]{2,1,0:T(8,128)(2,1)}, bf16[2,256,128]{2,1,0:T(8,128)(2,1)S(1)}, u32[]{:S(2)}, u32[]{:S(2)}) collective-permute-start(bf16[2,256,128]{2,1,0:T(8,128)(2,1)} %get-tuple-element.70), channel_id=1, source_target_pairs={{0,6},{1,7},{2,0},{3,1},{4,2},{5,3},{6,4},{7,5},{8,14},{9,15},{10,... | collective-permute-start | bytes 393224 | tf_op jit(solution)/shard_map/ppermute | solution.py:42
  37.9 11.2 %all-to-all-done.refs_0_ = bf16[64,112,128]{2,1,0:T(8,128)(2,1)} async-done(((bf16[64,112,128]{2,1,0:T(8,128)(2,1)}), bf16[64,112,128]{2,1,0:T(8,128)(2,1)}, u32[]{:S(2)}, u32[]{:S(2)}) %all-to-all-start) | async-done | bytes 1835040 | tf_op jit(solution)/shard_map/all_to_all | solution.py:420
  49.1 3.2 %shard_map.69.refs_6_.refs_4_.refs_3_ = bf16[14,256,256]{2,1,0:T(8,128)(2,1)S(1)} custom-call(bf16[64,112,128]{2,1,0:T(8,128)(2,1)} %all-to-all-done.refs_0_), custom_call_target="tpu_custom_call" | custom-call | tf_op jit(solution)/shard_map/pallas_call | solution.py:96
  55.5 2.0 %collective-permute-done.4.refs_5_ = bf16[6,2,1,32,256]{4,3,2,1,0:T(8,128)(2,1)S(1)} collective-permute-done((bf16[6,2,1,32,256]{4,3,2,1,0:T(8,128)(2,1)}, bf16[6,2,1,32,256]{4,3,2,1,0:T(8,128)(2,1)S(1)}, u32[]{:S(2)}, u32[]{:S(2)}) %collective-permute-start.4) | collective-permute-done | bytes 196640 | tf_op jit(solution)/shard_map/ppermute | solution.py:28
  58.6 3.3 %shard_map.72 = (bf16[6,2,192,768]{3,2,1,0:T(8,128)(2,1)S(1)}, f32[4,256,256]{2,1,0:T(8,128)S(1)}) custom-call(s32[1]{0:T(128)} %bitcast.1.refs_0_, bf16[4,2,4,32,256]{4,3,2,1,0:T(8,128)(2,1)S(1)} %copy-done.3, bf16[1,2,4,32,256]{4,3,2,1,0:T(8,128)(2,1)S(1)} %collective-permute-done.refs_0_.refs_2_, ...), custom_call_target="tpu_custom_call" | custom-call | tf_op jit(solution)/shard_map/pallas_call | solution.py:96
  62.0 6.0 %shard_map.73 = (bf16[4,2,4,32,256]{4,3,2,1,0:T(8,128)(2,1)S(1)}, bf16[4,256,128]{2,1,0:T(8,128)(2,1)S(1)}, bf16[4,256,128]{2,1,0:T(8,128)(2,1)S(1)}, bf16[14,25...) custom-call(s32[1]{0:T(128)} %bitcast.1.refs_0_, s32[1]{0:T(128)} %bitcast.refs_0_.refs_1_, ...), custom_call_target="tpu_custom_call" | custom-call | tf_op jit(solution)/shard_map/pallas_call | solution.py:96
  70.5 4.0 %collective-permute-start.9 = (bf16[1,2,4,32,256]{4,3,2,1,0:T(8,128)(2,1)S(1)}, bf16[1,2,4,32,256]{4,3,2,1,0:T(8,128)(2,1)S(1)}, u32[]{:S(2)}, u32[]{:S(2)}) collective-permute-start(bf16[1,2,4,32,256]{4,3,2,1,0:T(8,128)(2,1)S(1)} %get-tuple-element.114), channel_id=1, source_target_pairs={{0,8},{8,16},{16,24},{24,32},{32,40},{40,48},{48,56},{1,9},{9,17},... | collective-permute-start | bytes 393224 | tf_op jit(solution)/shard_map/ppermute | solution.py:20
  76.5 5.4 %shard_map.74 = bf16[64,112,128]{2,1,0:T(8,128)(2,1)} custom-call(s32[1]{0:T(128)} %bitcast.1.refs_0_, bf16[6,2,192,768]{3,2,1,0:T(8,128)(2,1)S(1)} %get-tuple-element.74.refs_2_.refs_1_, bf16[256,1024]{1,0:T(8,128)(2,1)S(1)} %get-tuple-element.83.refs_2_, bf16[14,256,256]{2,1,0:T(8,128)(2,1)S(1)} %collective-permute-done.12.refs_3_), custom_call_target="tpu_custom_call" | custom-call | tf_op jit(solution)/shard_map/pallas_call | solution.py:96
  81.9 13.5 %all-to-all-start.1 = ((bf16[64,112,128]{2,1,0:T(8,128)(2,1)}), bf16[64,112,128]{2,1,0:T(8,128)(2,1)S(1)}, u32[]{:S(2)}, u32[]{:S(2)}) async-start(bf16[64,112,128]{2,1,0:T(8,128)(2,1)} %shard_map.74), calls=%async_computation.1 | async-start | bytes 3670016 | tf_op jit(solution)/shard_map/all_to_all | solution.py:445
  95.5 3.1 %collective-permute-start.13 = (bf16[6,2,1,32,256]{4,3,2,1,0:T(8,128)(2,1)S(1)}, bf16[6,2,1,32,256]{4,3,2,1,0:T(8,128)(2,1)S(1)}, u32[]{:S(2)}, u32[]{:S(2)}) collective-permute-start(bf16[6,2,1,32,256]{4,3,2,1,0:T(8,128)(2,1)S(1)} %get-tuple-element.95), channel_id=1, source_target_pairs={{0,1},{1,2},{2,3},{3,4},{4,5},{5,6},{6,7},{8,9},{9,10},{10,11},{11... | collective-permute-start | bytes 589832 | tf_op jit(solution)/shard_map/ppermute | solution.py:28
  98.6 3.1 %collective-permute-start.14 = (bf16[6,2,1,32,256]{4,3,2,1,0:T(8,128)(2,1)S(1)}, bf16[6,2,1,32,256]{4,3,2,1,0:T(8,128)(2,1)S(1)}, u32[]{:S(2)}, u32[]{:S(2)}) collective-permute-start(bf16[6,2,1,32,256]{4,3,2,1,0:T(8,128)(2,1)S(1)} %get-tuple-element.96), channel_id=1, source_target_pairs={{1,0},{2,1},{3,2},{4,3},{5,4},{6,5},{7,6},{9,8},{10,9},{11,10},{12... | collective-permute-start | bytes 589832 | tf_op jit(solution)/shard_map/ppermute | solution.py:28
  104.5 2.0 %collective-permute-start.17 = (bf16[2,256,128]{2,1,0:T(8,128)(2,1)}, bf16[2,256,128]{2,1,0:T(8,128)(2,1)S(1)}, u32[]{:S(2)}, u32[]{:S(2)}) collective-permute-start(bf16[2,256,128]{2,1,0:T(8,128)(2,1)} %get-tuple-element.106), channel_id=1, source_target_pairs={{0,6},{1,7},{2,0},{3,1},{4,2},{5,3},{6,4},{7,5},{8,14},{9,15},{10,... | collective-permute-start | bytes 393224 | tf_op jit(solution)/shard_map/ppermute | solution.py:42
  106.5 8.5 %shard_map.75 = (bf16[4,2,2,32,256]{4,3,2,1,0:T(8,128)(2,1)}, f32[4,2,2,32,256]{4,3,2,1,0:T(8,128)}) custom-call(s32[1]{0:T(128)} %bitcast.1.refs_0_, bf16[4,2,4,32,256]{4,3,2,1,0:T(8,128)(2,1)} %copy-done.2, bf16[1,2,4,32,256]{4,3,2,1,0:T(8,128)(2,1)} %copy-done.6, bf16[1,2,4,32,256]{4,3,2,1,0:T(8,128)(2,1)} %copy-done.5, bf16[14,256,256]{2,1,0:T(8,128)(2,1)} %copy-done, ...), custom_call_target="tpu_custom_call" | custom-call | tf_op jit(solution)/shard_map/pallas_call | solution.py:96
  115.0 4.3 %all-to-all-done.1.refs_0_ = bf16[64,112,128]{2,1,0:T(8,128)(2,1)S(1)} async-done(((bf16[64,112,128]{2,1,0:T(8,128)(2,1)}), bf16[64,112,128]{2,1,0:T(8,128)(2,1)S(1)}, u32[]{:S(2)}, u32[]{:S(2)}) %all-to-all-start.1) | async-done | bytes 1835040 | tf_op jit(solution)/shard_map/all_to_all | solution.py:445
  119.6 5.0 %collective-permute-done.13.refs_1_ = bf16[6,2,1,32,256]{4,3,2,1,0:T(8,128)(2,1)S(1)} collective-permute-done((bf16[6,2,1,32,256]{4,3,2,1,0:T(8,128)(2,1)S(1)}, bf16[6,2,1,32,256]{4,3,2,1,0:T(8,128)(2,1)S(1)}, u32[]{:S(2)}, u32[]{:S(2)}) %collective-permute-start.13) | collective-permute-done | bytes 196640 | tf_op jit(solution)/shard_map/ppermute | solution.py:28
  124.6 2.2 %collective-permute-done.14.refs_2_ = bf16[6,2,1,32,256]{4,3,2,1,0:T(8,128)(2,1)S(1)} collective-permute-done((bf16[6,2,1,32,256]{4,3,2,1,0:T(8,128)(2,1)S(1)}, bf16[6,2,1,32,256]{4,3,2,1,0:T(8,128)(2,1)S(1)}, u32[]{:S(2)}, u32[]{:S(2)}) %collective-permute-start.14) | collective-permute-done | bytes 196640 | tf_op jit(solution)/shard_map/ppermute | solution.py:28
  127.7 4.1 %shard_map.78 = bf16[4,2,4,32,256]{4,3,2,1,0:T(8,128)(2,1)} custom-call(s32[1]{0:T(128)} %bitcast.1.refs_0_, bf16[6,2,1,32,256]{4,3,2,1,0:T(8,128)(2,1)S(1)} %collective-permute-done.13.refs_1_, bf16[6,2,1,32,256]{4,3,2,1,0:T(8,128)(2,1)S(1)} %collective-permute-done.14.refs_2_, bf16[14,256,256]{2,1,0:T(8,128)(2,1)} %copy-done, ...), custom_call_target="tpu_custom_call" | custom-call | tf_op jit(solution)/shard_map/pallas_call | solution.py:96
  131.8 2.2 %shard_map.80 = bf16[4,2,32,32,32]{4,3,2,1,0:T(8,128)(2,1)} custom-call(s32[1]{0:T(128)} %bitcast.refs_0_.refs_1_, bf16[2,256,128]{2,1,0:T(8,128)(2,1)S(1)} %get-tuple-element.107.refs_1_, bf16[2,256,128]{2,1,0:T(8,128)(2,1)S(1)} %collective-permute-done.15.refs_2_, bf16[2,256,128]{2,1,0:T(8,128)(2,1)S(1)} %collective-permute-done.16.refs_3_, ...), custom_call_target="tpu_custom_call" | custom-call | tf_op jit(solution)/shard_map/pallas_call | solution.py:96
  (55 shorter events, 23.1 us)
Async XLA Ops:
  2.8 10.7 %collective-permute-start.2 = (bf16[4,256,128]{2,1,0:T(8,128)(2,1)S(1)}, bf16[4,256,128]{2,1,0:T(8,128)(2,1)S(1)}, u32[]{:S(2)}, u32[]{:S(2)}) collective-permute-start(bf16[4,256,128]{2,1,0:T(8,128)(2,1)S(1)} %get-tuple-element.59), channel_id=1, source_target_pairs={{0,1},{1,0},{2,3},{3,2},{4,5},{5,4},{6,7},{7,6},{8,9},{9,8},{10,11... | collective-permute-start | bytes 786440 | tf_op jit(solution)/shard_map/ppermute | solution.py:36
  4.5 6.1 %collective-permute-start = (bf16[1,2,4,32,256]{4,3,2,1,0:T(8,128)(2,1)S(1)}, bf16[1,2,4,32,256]{4,3,2,1,0:T(8,128)(2,1)S(1)}, u32[]{:S(2)}, u32[]{:S(2)}) collective-permute-start(bf16[1,2,4,32,256]{4,3,2,1,0:T(8,128)(2,1)S(1)} %get-tuple-element.116), channel_id=1, source_target_pairs={{0,8},{8,16},{16,24},{24,32},{32,40},{40,48},{48,56},{1,9},{9,17},... | collective-permute-start | bytes 393224 | tf_op jit(solution)/shard_map/ppermute | solution.py:20
  7.7 5.7 %collective-permute-start.1 = (bf16[1,2,4,32,256]{4,3,2,1,0:T(8,128)(2,1)S(1)}, bf16[1,2,4,32,256]{4,3,2,1,0:T(8,128)(2,1)S(1)}, u32[]{:S(2)}, u32[]{:S(2)}) collective-permute-start(bf16[1,2,4,32,256]{4,3,2,1,0:T(8,128)(2,1)S(1)} %get-tuple-element.115), channel_id=1, source_target_pairs={{8,0},{16,8},{24,16},{32,24},{40,32},{48,40},{56,48},{9,1},{17,9},... | collective-permute-start | bytes 393224 | tf_op jit(solution)/shard_map/ppermute | solution.py:20
  13.5 35.7 %all-to-all-start = ((bf16[64,112,128]{2,1,0:T(8,128)(2,1)}), bf16[64,112,128]{2,1,0:T(8,128)(2,1)}, u32[]{:S(2)}, u32[]{:S(2)}) async-start(bf16[64,112,128]{2,1,0:T(8,128)(2,1)} %shard_map.67), calls=%async_computation | async-start | bytes 3670016 | tf_op jit(solution)/shard_map/all_to_all | solution.py:420
  27.0 28.6 %collective-permute-start.3 = (bf16[6,2,1,32,256]{4,3,2,1,0:T(8,128)(2,1)}, bf16[6,2,1,32,256]{4,3,2,1,0:T(8,128)(2,1)S(1)}, u32[]{:S(2)}, u32[]{:S(2)}) collective-permute-start(bf16[6,2,1,32,256]{4,3,2,1,0:T(8,128)(2,1)} %get-tuple-element.63), channel_id=1, source_target_pairs={{0,1},{1,2},{2,3},{3,4},{4,5},{5,6},{6,7},{8,9},{9,10},{10,11},{11... | collective-permute-start | bytes 589832 | tf_op jit(solution)/shard_map/ppermute | solution.py:28
  30.1 27.5 %collective-permute-start.4 = (bf16[6,2,1,32,256]{4,3,2,1,0:T(8,128)(2,1)}, bf16[6,2,1,32,256]{4,3,2,1,0:T(8,128)(2,1)S(1)}, u32[]{:S(2)}, u32[]{:S(2)}) collective-permute-start(bf16[6,2,1,32,256]{4,3,2,1,0:T(8,128)(2,1)} %get-tuple-element.64), channel_id=1, source_target_pairs={{1,0},{2,1},{3,2},{4,3},{5,4},{6,5},{7,6},{9,8},{10,9},{11,10},{12... | collective-permute-start | bytes 589832 | tf_op jit(solution)/shard_map/ppermute | solution.py:28
  34.0 18.3 %collective-permute-start.5 = (bf16[2,256,128]{2,1,0:T(8,128)(2,1)}, bf16[2,256,128]{2,1,0:T(8,128)(2,1)S(1)}, u32[]{:S(2)}, u32[]{:S(2)}) collective-permute-start(bf16[2,256,128]{2,1,0:T(8,128)(2,1)} %get-tuple-element.68), channel_id=1, source_target_pairs={{0,2},{1,3},{2,4},{3,5},{4,6},{5,7},{6,0},{7,1},{8,10},{9,11},{10,... | collective-permute-start | bytes 393224 | tf_op jit(solution)/shard_map/ppermute | solution.py:42
  35.2 18.3 %collective-permute-start.6 = (bf16[2,256,128]{2,1,0:T(8,128)(2,1)}, bf16[2,256,128]{2,1,0:T(8,128)(2,1)S(1)}, u32[]{:S(2)}, u32[]{:S(2)}) collective-permute-start(bf16[2,256,128]{2,1,0:T(8,128)(2,1)} %get-tuple-element.69), channel_id=1, source_target_pairs={{0,4},{1,5},{2,6},{3,7},{4,0},{5,1},{6,2},{7,3},{8,12},{9,13},{10,... | collective-permute-start | bytes 393224 | tf_op jit(solution)/shard_map/ppermute | solution.py:42
  35.9 18.6 %collective-permute-start.7 = (bf16[2,256,128]{2,1,0:T(8,128)(2,1)}, bf16[2,256,128]{2,1,0:T(8,128)(2,1)S(1)}, u32[]{:S(2)}, u32[]{:S(2)}) collective-permute-start(bf16[2,256,128]{2,1,0:T(8,128)(2,1)} %get-tuple-element.70), channel_id=1, source_target_pairs={{0,6},{1,7},{2,0},{3,1},{4,2},{5,3},{6,4},{7,5},{8,14},{9,15},{10,... | collective-permute-start | bytes 393224 | tf_op jit(solution)/shard_map/ppermute | solution.py:42
  57.5 4.5 %collective-permute-start.8 = (bf16[14,256,256]{2,1,0:T(8,128)(2,1)S(1)}, bf16[14,256,256]{2,1,0:T(8,128)(2,1)S(1)}, u32[]{:S(2)}, u32[]{:S(2)}) collective-permute-start(bf16[14,256,256]{2,1,0:T(8,128)(2,1)S(1)} %shard_map.69.refs_6_.refs_4_.refs_3_), channel_id=1, source_target_pairs={{0,64},{64,0},{1,65},{65,1},{2,66},{66,2},{3,67},{67,3},{4,68},{68... | collective-permute-start | bytes 5505032 | tf_op jit(solution)/shard_map/ppermute | solution.py:32
  68.0 27.4 %copy-start.2 = (bf16[4,2,4,32,256]{4,3,2,1,0:T(8,128)(2,1)}, bf16[4,2,4,32,256]{4,3,2,1,0:T(8,128)(2,1)S(1)}, u32[]{:S(2)}) copy-start(bf16[4,2,4,32,256]{4,3,2,1,0:T(8,128)(2,1)S(1)} %get-tuple-element.81.refs_1_) | copy-start | bytes 1572868
  68.0 8.4 %collective-permute-start.12 = (bf16[14,256,256]{2,1,0:T(8,128)(2,1)S(1)}, bf16[14,256,256]{2,1,0:T(8,128)(2,1)S(1)}, u32[]{:S(2)}, u32[]{:S(2)}) collective-permute-start(bf16[14,256,256]{2,1,0:T(8,128)(2,1)S(1)} %get-tuple-element.84), channel_id=1, source_target_pairs={{0,64},{64,0},{1,65},{65,1},{2,66},{66,2},{3,67},{67,3},{4,68},{68... | collective-permute-start | bytes 5505032 | tf_op jit(solution)/shard_map/ppermute | solution.py:32
  68.4 8.1 %collective-permute-start.11 = (bf16[4,256,128]{2,1,0:T(8,128)(2,1)S(1)}, bf16[4,256,128]{2,1,0:T(8,128)(2,1)S(1)}, u32[]{:S(2)}, u32[]{:S(2)}) collective-permute-start(bf16[4,256,128]{2,1,0:T(8,128)(2,1)S(1)} %get-tuple-element.82), channel_id=1, source_target_pairs={{0,1},{1,0},{2,3},{3,2},{4,5},{5,4},{6,7},{7,6},{8,9},{9,8},{10,11... | collective-permute-start | bytes 786440 | tf_op jit(solution)/shard_map/ppermute | solution.py:36
  69.2 6.4 %collective-permute-start.10 = (bf16[1,2,4,32,256]{4,3,2,1,0:T(8,128)(2,1)S(1)}, bf16[1,2,4,32,256]{4,3,2,1,0:T(8,128)(2,1)S(1)}, u32[]{:S(2)}, u32[]{:S(2)}) collective-permute-start(bf16[1,2,4,32,256]{4,3,2,1,0:T(8,128)(2,1)S(1)} %get-tuple-element.113), channel_id=1, source_target_pairs={{8,0},{16,8},{24,16},{32,24},{40,32},{48,40},{56,48},{9,1},{17,9},... | collective-permute-start | bytes 393224 | tf_op jit(solution)/shard_map/ppermute | solution.py:20
  70.5 5.9 %collective-permute-start.9 = (bf16[1,2,4,32,256]{4,3,2,1,0:T(8,128)(2,1)S(1)}, bf16[1,2,4,32,256]{4,3,2,1,0:T(8,128)(2,1)S(1)}, u32[]{:S(2)}, u32[]{:S(2)}) collective-permute-start(bf16[1,2,4,32,256]{4,3,2,1,0:T(8,128)(2,1)S(1)} %get-tuple-element.114), channel_id=1, source_target_pairs={{0,8},{8,16},{16,24},{24,32},{32,40},{40,48},{48,56},{1,9},{9,17},... | collective-permute-start | bytes 393224 | tf_op jit(solution)/shard_map/ppermute | solution.py:20
  75.7 19.8 %copy-start.5 = (bf16[1,2,4,32,256]{4,3,2,1,0:T(8,128)(2,1)}, bf16[1,2,4,32,256]{4,3,2,1,0:T(8,128)(2,1)S(1)}, u32[]{:S(2)}) copy-start(bf16[1,2,4,32,256]{4,3,2,1,0:T(8,128)(2,1)S(1)} %collective-permute-done.10.refs_3_.refs_2_) | copy-start | bytes 393220
  76.5 19.0 %copy-start.6 = (bf16[1,2,4,32,256]{4,3,2,1,0:T(8,128)(2,1)}, bf16[1,2,4,32,256]{4,3,2,1,0:T(8,128)(2,1)S(1)}, u32[]{:S(2)}) copy-start(bf16[1,2,4,32,256]{4,3,2,1,0:T(8,128)(2,1)S(1)} %collective-permute-done.9.refs_2_.refs_0_) | copy-start | bytes 393220
  81.9 37.4 %all-to-all-start.1 = ((bf16[64,112,128]{2,1,0:T(8,128)(2,1)}), bf16[64,112,128]{2,1,0:T(8,128)(2,1)S(1)}, u32[]{:S(2)}, u32[]{:S(2)}) async-start(bf16[64,112,128]{2,1,0:T(8,128)(2,1)} %shard_map.74), calls=%async_computation.1 | async-start | bytes 3670016 | tf_op jit(solution)/shard_map/all_to_all | solution.py:445
  95.5 29.1 %collective-permute-start.13 = (bf16[6,2,1,32,256]{4,3,2,1,0:T(8,128)(2,1)S(1)}, bf16[6,2,1,32,256]{4,3,2,1,0:T(8,128)(2,1)S(1)}, u32[]{:S(2)}, u32[]{:S(2)}) collective-permute-start(bf16[6,2,1,32,256]{4,3,2,1,0:T(8,128)(2,1)S(1)} %get-tuple-element.95), channel_id=1, source_target_pairs={{0,1},{1,2},{2,3},{3,4},{4,5},{5,6},{6,7},{8,9},{9,10},{10,11},{11... | collective-permute-start | bytes 589832 | tf_op jit(solution)/shard_map/ppermute | solution.py:28
  98.6 28.2 %collective-permute-start.14 = (bf16[6,2,1,32,256]{4,3,2,1,0:T(8,128)(2,1)S(1)}, bf16[6,2,1,32,256]{4,3,2,1,0:T(8,128)(2,1)S(1)}, u32[]{:S(2)}, u32[]{:S(2)}) collective-permute-start(bf16[6,2,1,32,256]{4,3,2,1,0:T(8,128)(2,1)S(1)} %get-tuple-element.96), channel_id=1, source_target_pairs={{1,0},{2,1},{3,2},{4,3},{5,4},{6,5},{7,6},{9,8},{10,9},{11,10},{12... | collective-permute-start | bytes 589832 | tf_op jit(solution)/shard_map/ppermute | solution.py:28
  102.5 29.3 %collective-permute-start.15 = (bf16[2,256,128]{2,1,0:T(8,128)(2,1)}, bf16[2,256,128]{2,1,0:T(8,128)(2,1)S(1)}, u32[]{:S(2)}, u32[]{:S(2)}) collective-permute-start(bf16[2,256,128]{2,1,0:T(8,128)(2,1)} %get-tuple-element.104), channel_id=1, source_target_pairs={{0,2},{1,3},{2,4},{3,5},{4,6},{5,7},{6,0},{7,1},{8,10},{9,11},{10,... | collective-permute-start | bytes 393224 | tf_op jit(solution)/shard_map/ppermute | solution.py:42
  103.8 28.0 %collective-permute-start.16 = (bf16[2,256,128]{2,1,0:T(8,128)(2,1)}, bf16[2,256,128]{2,1,0:T(8,128)(2,1)S(1)}, u32[]{:S(2)}, u32[]{:S(2)}) collective-permute-start(bf16[2,256,128]{2,1,0:T(8,128)(2,1)} %get-tuple-element.105), channel_id=1, source_target_pairs={{0,4},{1,5},{2,6},{3,7},{4,0},{5,1},{6,2},{7,3},{8,12},{9,13},{10,... | collective-permute-start | bytes 393224 | tf_op jit(solution)/shard_map/ppermute | solution.py:42
  104.5 27.3 %collective-permute-start.17 = (bf16[2,256,128]{2,1,0:T(8,128)(2,1)}, bf16[2,256,128]{2,1,0:T(8,128)(2,1)S(1)}, u32[]{:S(2)}, u32[]{:S(2)}) collective-permute-start(bf16[2,256,128]{2,1,0:T(8,128)(2,1)} %get-tuple-element.106), channel_id=1, source_target_pairs={{0,6},{1,7},{2,0},{3,1},{4,2},{5,3},{6,4},{7,5},{8,14},{9,15},{10,... | collective-permute-start | bytes 393224 | tf_op jit(solution)/shard_map/ppermute | solution.py:42
  126.8 7.2 %collective-permute-start.18 = (f32[112,128]{1,0:T(8,128)S(1)}, f32[112,128]{1,0:T(8,128)S(1)}, u32[]{:S(2)}, u32[]{:S(2)}) collective-permute-start(f32[112,128]{1,0:T(8,128)S(1)} %shard_map.76.refs_1_), channel_id=1, source_target_pairs={{0,64},{64,0},{1,65},{65,1},{2,66},{66,2},{3,67},{67,3},{4,68},{68... | collective-permute-start | bytes 172040 | tf_op jit(solution)/shard_map/ppermute | solution.py:32
  (6 other events, 40.8 us)

commit v4 on v3

--- a/solution.py
+++ b/solution.py
@@ -53,7 +53,7 @@
     return size
 
 
-def call(body, out, scratch=(), far=(), far_out=()):
+def call(body, out, scratch=(), far=(), far_out=(), parts=0):
     outs = list(out) if isinstance(out, tuple) else [out]
 
     def run(*args):
@@ -66,21 +66,34 @@
             near = list(refs[:count])
             extra = refs[count:]
             sems = extra[-1]
-            copies = []
+            pieces = max(parts, 1)
+
+            def copy_in(at, piece):
+                size = args[held[at]].shape[0] // pieces
+                rows = pl.ds(piece * size, size)
+                return pltpu.make_async_copy(
+                    refs[held[at]].at[rows], extra[at].at[rows], sems.at[at * pieces + piece]
+                )
+
+            def wait(piece):
+                for at in range(len(held)):
+                    copy_in(at, piece).wait()
+
             for at, n in enumerate(held):
                 near[n] = extra[at]
-                copies.append(pltpu.make_async_copy(refs[n], near[n], sems.at[at]))
-            for copy in copies:
-                copy.start()
+            for piece in range(pieces):
+                for at in range(len(held)):
+                    copy_in(at, piece).start()
             for at, n in enumerate(written):
                 near[len(args) + n] = extra[len(held) + at]
-            for copy in copies:
-                copy.wait()
-            body(*near, *extra[len(held) + len(written) : -1])
+            if not parts:
+                wait(0)
+            given = (wait,) if parts else ()
+            body(*near, *extra[len(held) + len(written) : -1], *given)
             copies = []
             for at, n in enumerate(written):
                 to = refs[len(args) + n]
-                copies.append(pltpu.make_async_copy(near[len(args) + n], to, sems.at[len(held) + at]))
+                copies.append(pltpu.make_async_copy(near[len(args) + n], to, sems.at[len(held) * pieces + at]))
             for copy in copies:
                 copy.start()
             for copy in copies:
@@ -98,7 +111,7 @@
             out_shape=[pltpu.HBM(x.shape, x.dtype) if n in far_out else x for n, x in enumerate(outs)],
             in_specs=specs,
             out_specs=[FAR if n in far_out else FULL for n in range(len(outs))],
-            scratch_shapes=[*rooms, pltpu.SemaphoreType.DMA((len(held) + len(written) + 1,))],
+            scratch_shapes=[*rooms, pltpu.SemaphoreType.DMA((len(held) * max(parts, 1) + len(written) + 1,))],
             compiler_params=pltpu.CompilerParams(vmem_limit_bytes=total + (3 << 20)),
         )(*[pltpu.with_memory_space_constraint(x, pltpu.HBM) if n in held else x for n, x in enumerate(args)])
         return result if isinstance(out, tuple) else result[0]
@@ -138,8 +151,9 @@
     out[...] = jnp.broadcast_to(block[None], out.shape)
 
 
-def unpack_kernel_body(mine, out):
+def unpack_kernel_body(mine, out, wait):
     def step(n, carry):
+        wait(n)
         for t in range(HALF // 2):
             for high in range(2):
                 parts = [mine[8 * n + high * 4 + s, 16 * t : 16 * t + 16, :] for s in range(4)]
@@ -378,7 +392,7 @@
     by_core(core, run)
 
 
-def edge_grad_body(core, left, right, mine, other, inner, edges, out, shifts):
+def edge_grad_body(core, left, right, mine, other, inner, edges, out, shifts, wait):
     row = lax.broadcasted_iota(jnp.int32, (384, 256), 0) % 32
     for n, side in enumerate((left, right)):
         wide = side[...].reshape(384, 256).astype(F32)
@@ -386,6 +400,7 @@
         down = jnp.where(row == 31, 0.0, pltpu.roll(wide, 383, 0))
         for k, part in enumerate((up, wide, down)):
             shifts[n, k] = part.astype(BF16).reshape(6, 64, 256)
+    wait(0)
     out[:, :, 1:3] = inner[...]
 
     def run(half):
@@ -420,7 +435,7 @@
     blocks = lax.all_to_all(blocks, GRID, 0, 0, tiled=True)
     left, right = corners(before, features, after)
     cot = spread(keep, got)
-    mine = call(unpack_kernel_body, shape((HALF, 256, 256)), far=(0,))(blocks)
+    mine = call(unpack_kernel_body, shape((HALF, 256, 256)), far=(0,), parts=8)(blocks)
     mine, left, right, *cot = lax.optimization_barrier((mine, left, right, *cot))
     other = swap_cores(mine)
     shifts, partial = call(
@@ -436,7 +451,6 @@
     before, after = halo(grad_pre, "sx", 0)
     got = swap_sides(send)
     received = swap_cores(given)
-    turned, before, after, got = lax.optimization_barrier((turned, before, after, got))
     blocks = call(
         keep_grads_body, shape((64, 112, 128)), [pltpu.VMEM((HALF, 256, 256), BF16)], far_out=(0,)
     )(index, shifts, turned, received)
@@ -461,6 +475,7 @@
         shape((4, 2, 4, 32, 256)),
         [pltpu.VMEM((2, 3, 6, 64, 256), BF16)],
         far=(3, 4, 5, 6),
+        parts=1,
     )(index, left, right, mine, other, inner, edges)
     input_grad, *pieces = lax.optimization_barrier((input_grad, *pieces))
     output = call(unpack_output_body, shape((4, 2, 32, 32, 32)))(place, *pieces)

time: 137 us -> 132 us (0.964)
  starting transfers between devices: 61.2 us -> 58.3 us
  waiting for transfers between devices: 32.9 us -> 31.5 us
    ppermute x4, waiting for transfers between devices: 4.78 us -> 2.87 us  [halo(): return (lax.ppermute(last, axis, up), lax.ppermute(leading, axis, down))]
    ppermute x4, starting transfers between devices: 9.79 us -> 8.27 us  [halo(): return (lax.ppermute(last, axis, up), lax.ppermute(leading, axis, down))]
  transfers between devices with their start and end apart: 21 -> 21, of which waited for: 12 -> 10; matrix products, arithmetic and copies ran while one was open for 0% -> 0% of each run, Pallas kernels for 19% -> 23%
where the time goes in v4:
time: 132 us; the launch traced here: 131 us
  starting transfers between devices  58.3 us (44%)
  Pallas kernels  38.3 us (29%)
  waiting for transfers between devices  31.5 us (24%)
  local copies, waits for them, and re-layouts  1.72 us (1%)
    pallas_call x15, Pallas kernels, run(): pl.pallas_call(kernel, out_shape=[pltpu.HBM(x.shape, x.dtype) if n in far...  38.3 us
    all_to_all x2, starting transfers between devices, local(): blocks = lax.all_to_all(blocks, GRID, 0, 0, tiled=True)  25.4 us
    all_to_all x2, waiting for transfers between devices, local(): blocks = lax.all_to_all(blocks, GRID, 0, 0, tiled=True)  15.5 us
    ppermute x4, starting transfers between devices, corners(): return (lax.ppermute(last, 'sy', up), lax.ppermute(leading, 'sy', down))  12.4 us
    ppermute x4, waiting for transfers between devices, corners(): return (lax.ppermute(last, 'sy', up), lax.ppermute(leading, 'sy', down))  10.3 us
    ppermute x4, starting transfers between devices, halo(): return (lax.ppermute(last, axis, up), lax.ppermute(leading, axis, down))  8.27 us
    ppermute x6, starting transfers between devices, spread(): lax.ppermute(pieces[d], 'sy', [(i, (i // 2 + d) % 4 * 2 + i % 2) for i in...  7.86 us
    ppermute x4, waiting for transfers between devices, halo(): return (lax.ppermute(last, axis, up), lax.ppermute(leading, axis, down))  2.87 us
  transfers between devices with their start and end apart: 21, of which 10 were waited for; matrix products, arithmetic and copies ran while one was open for 0% of the time, Pallas kernels for 23%

profile of v4, /device:TPU:3, one launch (start us, length us, event | category | flops | bytes accessed | tf_op | source)
XLA Modules:
  0.0 131.1 jit_solution(14549585917325591875)
XLA Ops:
  4.5 3.2 %collective-permute-start = (bf16[1,2,4,32,256]{4,3,2,1,0:T(8,128)(2,1)S(1)}, bf16[1,2,4,32,256]{4,3,2,1,0:T(8,128)(2,1)S(1)}, u32[]{:S(2)}, u32[]{:S(2)}) collective-permute-start(bf16[1,2,4,32,256]{4,3,2,1,0:T(8,128)(2,1)S(1)} %get-tuple-element.108), channel_id=1, source_target_pairs={{0,8},{8,16},{16,24},{24,32},{32,40},{40,48},{48,56},{1,9},{9,17},... | collective-permute-start | bytes 393224 | tf_op jit(solution)/shard_map/ppermute | solution.py:20
  10.6 2.9 %collective-permute-done.1.refs_2_.refs_3_ = bf16[1,2,4,32,256]{4,3,2,1,0:T(8,128)(2,1)S(1)} collective-permute-done((bf16[1,2,4,32,256]{4,3,2,1,0:T(8,128)(2,1)S(1)}, bf16[1,2,4,32,256]{4,3,2,1,0:T(8,128)(2,1)S(1)}, u32[]{:S(2)}, u32[]{:S(2)}) %collective-permute-start.1) | collective-permute-done | bytes 131104 | tf_op jit(solution)/shard_map/ppermute | solution.py:20
  13.5 12.7 %all-to-all-start = ((bf16[64,112,128]{2,1,0:T(8,128)(2,1)}), bf16[64,112,128]{2,1,0:T(8,128)(2,1)}, u32[]{:S(2)}, u32[]{:S(2)}) async-start(bf16[64,112,128]{2,1,0:T(8,128)(2,1)} %shard_map.67), calls=%async_computation | async-start | bytes 3670016 | tf_op jit(solution)/shard_map/all_to_all | solution.py:435
  27.0 3.1 %collective-permute-start.3 = (bf16[6,2,1,32,256]{4,3,2,1,0:T(8,128)(2,1)}, bf16[6,2,1,32,256]{4,3,2,1,0:T(8,128)(2,1)S(1)}, u32[]{:S(2)}, u32[]{:S(2)}) collective-permute-start(bf16[6,2,1,32,256]{4,3,2,1,0:T(8,128)(2,1)} %get-tuple-element.59), channel_id=1, source_target_pairs={{0,1},{1,2},{2,3},{3,4},{4,5},{5,6},{6,7},{8,9},{9,10},{10,11},{11... | collective-permute-start | bytes 589832 | tf_op jit(solution)/shard_map/ppermute | solution.py:28
  30.1 3.1 %collective-permute-start.4 = (bf16[6,2,1,32,256]{4,3,2,1,0:T(8,128)(2,1)}, bf16[6,2,1,32,256]{4,3,2,1,0:T(8,128)(2,1)S(1)}, u32[]{:S(2)}, u32[]{:S(2)}) collective-permute-start(bf16[6,2,1,32,256]{4,3,2,1,0:T(8,128)(2,1)} %get-tuple-element.60), channel_id=1, source_target_pairs={{1,0},{2,1},{3,2},{4,3},{5,4},{6,5},{7,6},{9,8},{10,9},{11,10},{12... | collective-permute-start | bytes 589832 | tf_op jit(solution)/shard_map/ppermute | solution.py:28
  35.9 2.0 %collective-permute-start.7 = (bf16[2,256,128]{2,1,0:T(8,128)(2,1)}, bf16[2,256,128]{2,1,0:T(8,128)(2,1)S(1)}, u32[]{:S(2)}, u32[]{:S(2)}) collective-permute-start(bf16[2,256,128]{2,1,0:T(8,128)(2,1)} %get-tuple-element.66), channel_id=1, source_target_pairs={{0,6},{1,7},{2,0},{3,1},{4,2},{5,3},{6,4},{7,5},{8,14},{9,15},{10,... | collective-permute-start | bytes 393224 | tf_op jit(solution)/shard_map/ppermute | solution.py:42
  37.9 11.2 %all-to-all-done.refs_0_ = bf16[64,112,128]{2,1,0:T(8,128)(2,1)} async-done(((bf16[64,112,128]{2,1,0:T(8,128)(2,1)}), bf16[64,112,128]{2,1,0:T(8,128)(2,1)}, u32[]{:S(2)}, u32[]{:S(2)}) %all-to-all-start) | async-done | bytes 1835040 | tf_op jit(solution)/shard_map/all_to_all | solution.py:435
  49.1 2.7 %shard_map.69.refs_6_.refs_4_.refs_3_ = bf16[14,256,256]{2,1,0:T(8,128)(2,1)S(1)} custom-call(bf16[64,112,128]{2,1,0:T(8,128)(2,1)} %all-to-all-done.refs_0_), custom_call_target="tpu_custom_call" | custom-call | tf_op jit(solution)/shard_map/pallas_call | solution.py:109
  51.8 1.7 %collective-permute-done.6.refs_7_ = bf16[2,256,128]{2,1,0:T(8,128)(2,1)S(1)} collective-permute-done((bf16[2,256,128]{2,1,0:T(8,128)(2,1)}, bf16[2,256,128]{2,1,0:T(8,128)(2,1)S(1)}, u32[]{:S(2)}, u32[]{:S(2)}) %collective-permute-start.6) | collective-permute-done | bytes 131104 | tf_op jit(solution)/shard_map/ppermute | solution.py:42
  55.5 2.0 %collective-permute-done.4.refs_5_ = bf16[6,2,1,32,256]{4,3,2,1,0:T(8,128)(2,1)S(1)} collective-permute-done((bf16[6,2,1,32,256]{4,3,2,1,0:T(8,128)(2,1)}, bf16[6,2,1,32,256]{4,3,2,1,0:T(8,128)(2,1)S(1)}, u32[]{:S(2)}, u32[]{:S(2)}) %collective-permute-start.4) | collective-permute-done | bytes 196640 | tf_op jit(solution)/shard_map/ppermute | solution.py:28
  58.6 3.3 %shard_map.72 = (bf16[6,2,192,768]{3,2,1,0:T(8,128)(2,1)S(1)}, f32[4,256,256]{2,1,0:T(8,128)S(1)}) custom-call(s32[1]{0:T(128)} %bitcast.1.refs_0_, bf16[4,2,4,32,256]{4,3,2,1,0:T(8,128)(2,1)S(1)} %copy-done.3, bf16[1,2,4,32,256]{4,3,2,1,0:T(8,128)(2,1)S(1)} %collective-permute-done.refs_0_.refs_2_, ...), custom_call_target="tpu_custom_call" | custom-call | tf_op jit(solution)/shard_map/pallas_call | solution.py:109
  62.0 6.0 %shard_map.73 = (bf16[4,2,4,32,256]{4,3,2,1,0:T(8,128)(2,1)S(1)}, bf16[4,256,128]{2,1,0:T(8,128)(2,1)S(1)}, bf16[4,256,128]{2,1,0:T(8,128)(2,1)S(1)}, bf16[14,25...) custom-call(s32[1]{0:T(128)} %bitcast.1.refs_0_, s32[1]{0:T(128)} %bitcast.refs_0_.refs_1_, ...), custom_call_target="tpu_custom_call" | custom-call | tf_op jit(solution)/shard_map/pallas_call | solution.py:109
  68.8 2.5 %collective-permute-start.10 = (bf16[1,2,4,32,256]{4,3,2,1,0:T(8,128)(2,1)S(1)}, bf16[1,2,4,32,256]{4,3,2,1,0:T(8,128)(2,1)S(1)}, u32[]{:S(2)}, u32[]{:S(2)}) collective-permute-start(bf16[1,2,4,32,256]{4,3,2,1,0:T(8,128)(2,1)S(1)} %get-tuple-element.106), channel_id=1, source_target_pairs={{0,8},{8,16},{16,24},{24,32},{32,40},{40,48},{48,56},{1,9},{9,17},... | collective-permute-start | bytes 393224 | tf_op jit(solution)/shard_map/ppermute | solution.py:20
  72.6 5.4 %shard_map.74 = bf16[64,112,128]{2,1,0:T(8,128)(2,1)} custom-call(s32[1]{0:T(128)} %bitcast.1.refs_0_, bf16[6,2,192,768]{3,2,1,0:T(8,128)(2,1)S(1)} %get-tuple-element.70.refs_2_.refs_1_, bf16[256,1024]{1,0:T(8,128)(2,1)S(1)} %get-tuple-element.76.refs_2_, bf16[14,256,256]{2,1,0:T(8,128)(2,1)S(1)} %collective-permute-done.9.refs_3_), custom_call_target="tpu_custom_call" | custom-call | tf_op jit(solution)/shard_map/pallas_call | solution.py:109
  78.1 12.7 %all-to-all-start.1 = ((bf16[64,112,128]{2,1,0:T(8,128)(2,1)}), bf16[64,112,128]{2,1,0:T(8,128)(2,1)S(1)}, u32[]{:S(2)}, u32[]{:S(2)}) async-start(bf16[64,112,128]{2,1,0:T(8,128)(2,1)} %shard_map.74), calls=%async_computation.1 | async-start | bytes 3670016 | tf_op jit(solution)/shard_map/all_to_all | solution.py:459
  90.8 3.1 %collective-permute-start.13 = (bf16[6,2,1,32,256]{4,3,2,1,0:T(8,128)(2,1)S(1)}, bf16[6,2,1,32,256]{4,3,2,1,0:T(8,128)(2,1)S(1)}, u32[]{:S(2)}, u32[]{:S(2)}) collective-permute-start(bf16[6,2,1,32,256]{4,3,2,1,0:T(8,128)(2,1)S(1)} %get-tuple-element.87), channel_id=1, source_target_pairs={{0,1},{1,2},{2,3},{3,4},{4,5},{5,6},{6,7},{8,9},{9,10},{10,11},{11... | collective-permute-start | bytes 589832 | tf_op jit(solution)/shard_map/ppermute | solution.py:28
  93.9 3.1 %collective-permute-start.14 = (bf16[6,2,1,32,256]{4,3,2,1,0:T(8,128)(2,1)S(1)}, bf16[6,2,1,32,256]{4,3,2,1,0:T(8,128)(2,1)S(1)}, u32[]{:S(2)}, u32[]{:S(2)}) collective-permute-start(bf16[6,2,1,32,256]{4,3,2,1,0:T(8,128)(2,1)S(1)} %get-tuple-element.88), channel_id=1, source_target_pairs={{1,0},{2,1},{3,2},{4,3},{5,4},{6,5},{7,6},{9,8},{10,9},{11,10},{12... | collective-permute-start | bytes 589832 | tf_op jit(solution)/shard_map/ppermute | solution.py:28
  99.8 2.0 %collective-permute-start.17 = (bf16[2,256,128]{2,1,0:T(8,128)(2,1)}, bf16[2,256,128]{2,1,0:T(8,128)(2,1)S(1)}, u32[]{:S(2)}, u32[]{:S(2)}) collective-permute-start(bf16[2,256,128]{2,1,0:T(8,128)(2,1)} %get-tuple-element.98), channel_id=1, source_target_pairs={{0,6},{1,7},{2,0},{3,1},{4,2},{5,3},{6,4},{7,5},{8,14},{9,15},{10,... | collective-permute-start | bytes 393224 | tf_op jit(solution)/shard_map/ppermute | solution.py:42
  101.8 8.5 %shard_map.75 = (bf16[4,2,2,32,256]{4,3,2,1,0:T(8,128)(2,1)}, f32[4,2,2,32,256]{4,3,2,1,0:T(8,128)}) custom-call(s32[1]{0:T(128)} %bitcast.1.refs_0_, bf16[4,2,4,32,256]{4,3,2,1,0:T(8,128)(2,1)} %copy-done.2, bf16[1,2,4,32,256]{4,3,2,1,0:T(8,128)(2,1)} %copy-done.5, bf16[1,2,4,32,256]{4,3,2,1,0:T(8,128)(2,1)} %copy-done.6, bf16[14,256,256]{2,1,0:T(8,128)(2,1)} %copy-done, ...), custom_call_target="tpu_custom_call" | custom-call | tf_op jit(solution)/shard_map/pallas_call | solution.py:109
  110.3 4.3 %all-to-all-done.1.refs_0_ = bf16[64,112,128]{2,1,0:T(8,128)(2,1)S(1)} async-done(((bf16[64,112,128]{2,1,0:T(8,128)(2,1)}), bf16[64,112,128]{2,1,0:T(8,128)(2,1)S(1)}, u32[]{:S(2)}, u32[]{:S(2)}) %all-to-all-start.1) | async-done | bytes 1835040 | tf_op jit(solution)/shard_map/all_to_all | solution.py:459
  114.9 5.1 %collective-permute-done.13.refs_1_ = bf16[6,2,1,32,256]{4,3,2,1,0:T(8,128)(2,1)S(1)} collective-permute-done((bf16[6,2,1,32,256]{4,3,2,1,0:T(8,128)(2,1)S(1)}, bf16[6,2,1,32,256]{4,3,2,1,0:T(8,128)(2,1)S(1)}, u32[]{:S(2)}, u32[]{:S(2)}) %collective-permute-start.13) | collective-permute-done | bytes 196640 | tf_op jit(solution)/shard_map/ppermute | solution.py:28
  119.9 2.2 %collective-permute-done.14.refs_2_ = bf16[6,2,1,32,256]{4,3,2,1,0:T(8,128)(2,1)S(1)} collective-permute-done((bf16[6,2,1,32,256]{4,3,2,1,0:T(8,128)(2,1)S(1)}, bf16[6,2,1,32,256]{4,3,2,1,0:T(8,128)(2,1)S(1)}, u32[]{:S(2)}, u32[]{:S(2)}) %collective-permute-start.14) | collective-permute-done | bytes 196640 | tf_op jit(solution)/shard_map/ppermute | solution.py:28
  123.0 3.9 %shard_map.78 = bf16[4,2,4,32,256]{4,3,2,1,0:T(8,128)(2,1)} custom-call(s32[1]{0:T(128)} %bitcast.1.refs_0_, bf16[6,2,1,32,256]{4,3,2,1,0:T(8,128)(2,1)S(1)} %collective-permute-done.13.refs_1_, bf16[6,2,1,32,256]{4,3,2,1,0:T(8,128)(2,1)S(1)} %collective-permute-done.14.refs_2_, bf16[14,256,256]{2,1,0:T(8,128)(2,1)} %copy-done, ...), custom_call_target="tpu_custom_call" | custom-call | tf_op jit(solution)/shard_map/pallas_call | solution.py:109
  127.0 2.2 %shard_map.80 = bf16[4,2,32,32,32]{4,3,2,1,0:T(8,128)(2,1)} custom-call(s32[1]{0:T(128)} %bitcast.refs_0_.refs_1_, bf16[2,256,128]{2,1,0:T(8,128)(2,1)S(1)} %get-tuple-element.99.refs_1_, bf16[2,256,128]{2,1,0:T(8,128)(2,1)S(1)} %collective-permute-done.15.refs_2_, bf16[2,256,128]{2,1,0:T(8,128)(2,1)S(1)} %collective-permute-done.16.refs_3_, ...), custom_call_target="tpu_custom_call" | custom-call | tf_op jit(solution)/shard_map/pallas_call | solution.py:109
  (55 shorter events, 21.1 us)
Async XLA Ops:
  2.8 10.7 %collective-permute-start.2 = (bf16[4,256,128]{2,1,0:T(8,128)(2,1)S(1)}, bf16[4,256,128]{2,1,0:T(8,128)(2,1)S(1)}, u32[]{:S(2)}, u32[]{:S(2)}) collective-permute-start(bf16[4,256,128]{2,1,0:T(8,128)(2,1)S(1)} %get-tuple-element.55), channel_id=1, source_target_pairs={{0,1},{1,0},{2,3},{3,2},{4,5},{5,4},{6,7},{7,6},{8,9},{9,8},{10,11... | collective-permute-start | bytes 786440 | tf_op jit(solution)/shard_map/ppermute | solution.py:36
  4.5 6.1 %collective-permute-start = (bf16[1,2,4,32,256]{4,3,2,1,0:T(8,128)(2,1)S(1)}, bf16[1,2,4,32,256]{4,3,2,1,0:T(8,128)(2,1)S(1)}, u32[]{:S(2)}, u32[]{:S(2)}) collective-permute-start(bf16[1,2,4,32,256]{4,3,2,1,0:T(8,128)(2,1)S(1)} %get-tuple-element.108), channel_id=1, source_target_pairs={{0,8},{8,16},{16,24},{24,32},{32,40},{40,48},{48,56},{1,9},{9,17},... | collective-permute-start | bytes 393224 | tf_op jit(solution)/shard_map/ppermute | solution.py:20
  7.7 5.7 %collective-permute-start.1 = (bf16[1,2,4,32,256]{4,3,2,1,0:T(8,128)(2,1)S(1)}, bf16[1,2,4,32,256]{4,3,2,1,0:T(8,128)(2,1)S(1)}, u32[]{:S(2)}, u32[]{:S(2)}) collective-permute-start(bf16[1,2,4,32,256]{4,3,2,1,0:T(8,128)(2,1)S(1)} %get-tuple-element.107), channel_id=1, source_target_pairs={{8,0},{16,8},{24,16},{32,24},{40,32},{48,40},{56,48},{9,1},{17,9},... | collective-permute-start | bytes 393224 | tf_op jit(solution)/shard_map/ppermute | solution.py:20
  13.5 35.7 %all-to-all-start = ((bf16[64,112,128]{2,1,0:T(8,128)(2,1)}), bf16[64,112,128]{2,1,0:T(8,128)(2,1)}, u32[]{:S(2)}, u32[]{:S(2)}) async-start(bf16[64,112,128]{2,1,0:T(8,128)(2,1)} %shard_map.67), calls=%async_computation | async-start | bytes 3670016 | tf_op jit(solution)/shard_map/all_to_all | solution.py:435
  27.0 28.6 %collective-permute-start.3 = (bf16[6,2,1,32,256]{4,3,2,1,0:T(8,128)(2,1)}, bf16[6,2,1,32,256]{4,3,2,1,0:T(8,128)(2,1)S(1)}, u32[]{:S(2)}, u32[]{:S(2)}) collective-permute-start(bf16[6,2,1,32,256]{4,3,2,1,0:T(8,128)(2,1)} %get-tuple-element.59), channel_id=1, source_target_pairs={{0,1},{1,2},{2,3},{3,4},{4,5},{5,6},{6,7},{8,9},{9,10},{10,11},{11... | collective-permute-start | bytes 589832 | tf_op jit(solution)/shard_map/ppermute | solution.py:28
  30.1 27.5 %collective-permute-start.4 = (bf16[6,2,1,32,256]{4,3,2,1,0:T(8,128)(2,1)}, bf16[6,2,1,32,256]{4,3,2,1,0:T(8,128)(2,1)S(1)}, u32[]{:S(2)}, u32[]{:S(2)}) collective-permute-start(bf16[6,2,1,32,256]{4,3,2,1,0:T(8,128)(2,1)} %get-tuple-element.60), channel_id=1, source_target_pairs={{1,0},{2,1},{3,2},{4,3},{5,4},{6,5},{7,6},{9,8},{10,9},{11,10},{12... | collective-permute-start | bytes 589832 | tf_op jit(solution)/shard_map/ppermute | solution.py:28
  34.0 17.8 %collective-permute-start.5 = (bf16[2,256,128]{2,1,0:T(8,128)(2,1)}, bf16[2,256,128]{2,1,0:T(8,128)(2,1)S(1)}, u32[]{:S(2)}, u32[]{:S(2)}) collective-permute-start(bf16[2,256,128]{2,1,0:T(8,128)(2,1)} %get-tuple-element.64), channel_id=1, source_target_pairs={{0,2},{1,3},{2,4},{3,5},{4,6},{5,7},{6,0},{7,1},{8,10},{9,11},{10,... | collective-permute-start | bytes 393224 | tf_op jit(solution)/shard_map/ppermute | solution.py:42
  35.2 18.3 %collective-permute-start.6 = (bf16[2,256,128]{2,1,0:T(8,128)(2,1)}, bf16[2,256,128]{2,1,0:T(8,128)(2,1)S(1)}, u32[]{:S(2)}, u32[]{:S(2)}) collective-permute-start(bf16[2,256,128]{2,1,0:T(8,128)(2,1)} %get-tuple-element.65), channel_id=1, source_target_pairs={{0,4},{1,5},{2,6},{3,7},{4,0},{5,1},{6,2},{7,3},{8,12},{9,13},{10,... | collective-permute-start | bytes 393224 | tf_op jit(solution)/shard_map/ppermute | solution.py:42
  35.9 18.6 %collective-permute-start.7 = (bf16[2,256,128]{2,1,0:T(8,128)(2,1)}, bf16[2,256,128]{2,1,0:T(8,128)(2,1)S(1)}, u32[]{:S(2)}, u32[]{:S(2)}) collective-permute-start(bf16[2,256,128]{2,1,0:T(8,128)(2,1)} %get-tuple-element.66), channel_id=1, source_target_pairs={{0,6},{1,7},{2,0},{3,1},{4,2},{5,3},{6,4},{7,5},{8,14},{9,15},{10,... | collective-permute-start | bytes 393224 | tf_op jit(solution)/shard_map/ppermute | solution.py:42
  51.8 16.2 %copy-start = (bf16[14,256,256]{2,1,0:T(8,128)(2,1)}, bf16[14,256,256]{2,1,0:T(8,128)(2,1)S(1)}, u32[]{:S(2)}) copy-start(bf16[14,256,256]{2,1,0:T(8,128)(2,1)S(1)} %shard_map.69.refs_6_.refs_4_.refs_3_) | copy-start | bytes 5505028
  57.5 4.4 %collective-permute-start.8 = (bf16[14,256,256]{2,1,0:T(8,128)(2,1)S(1)}, bf16[14,256,256]{2,1,0:T(8,128)(2,1)S(1)}, u32[]{:S(2)}, u32[]{:S(2)}) collective-permute-start(bf16[14,256,256]{2,1,0:T(8,128)(2,1)S(1)} %shard_map.69.refs_6_.refs_4_.refs_3_), channel_id=1, source_target_pairs={{0,64},{64,0},{1,65},{65,1},{2,66},{66,2},{3,67},{67,3},{4,68},{68... | collective-permute-start | bytes 5505032 | tf_op jit(solution)/shard_map/ppermute | solution.py:32
  68.0 22.8 %copy-start.2 = (bf16[4,2,4,32,256]{4,3,2,1,0:T(8,128)(2,1)}, bf16[4,2,4,32,256]{4,3,2,1,0:T(8,128)(2,1)S(1)}, u32[]{:S(2)}) copy-start(bf16[4,2,4,32,256]{4,3,2,1,0:T(8,128)(2,1)S(1)} %get-tuple-element.78.refs_1_) | copy-start | bytes 1572868
  68.0 4.6 %collective-permute-start.9 = (bf16[14,256,256]{2,1,0:T(8,128)(2,1)S(1)}, bf16[14,256,256]{2,1,0:T(8,128)(2,1)S(1)}, u32[]{:S(2)}, u32[]{:S(2)}) collective-permute-start(bf16[14,256,256]{2,1,0:T(8,128)(2,1)S(1)} %get-tuple-element.77), channel_id=1, source_target_pairs={{0,64},{64,0},{1,65},{65,1},{2,66},{66,2},{3,67},{67,3},{4,68},{68... | collective-permute-start | bytes 5505032 | tf_op jit(solution)/shard_map/ppermute | solution.py:32
  68.3 9.7 %collective-permute-start.12 = (bf16[4,256,128]{2,1,0:T(8,128)(2,1)S(1)}, bf16[4,256,128]{2,1,0:T(8,128)(2,1)S(1)}, u32[]{:S(2)}, u32[]{:S(2)}) collective-permute-start(bf16[4,256,128]{2,1,0:T(8,128)(2,1)S(1)} %get-tuple-element.80), channel_id=1, source_target_pairs={{0,1},{1,0},{2,3},{3,2},{4,5},{5,4},{6,7},{7,6},{8,9},{9,8},{10,11... | collective-permute-start | bytes 786440 | tf_op jit(solution)/shard_map/ppermute | solution.py:36
  68.8 9.2 %collective-permute-start.10 = (bf16[1,2,4,32,256]{4,3,2,1,0:T(8,128)(2,1)S(1)}, bf16[1,2,4,32,256]{4,3,2,1,0:T(8,128)(2,1)S(1)}, u32[]{:S(2)}, u32[]{:S(2)}) collective-permute-start(bf16[1,2,4,32,256]{4,3,2,1,0:T(8,128)(2,1)S(1)} %get-tuple-element.106), channel_id=1, source_target_pairs={{0,8},{8,16},{16,24},{24,32},{32,40},{40,48},{48,56},{1,9},{9,17},... | collective-permute-start | bytes 393224 | tf_op jit(solution)/shard_map/ppermute | solution.py:20
  71.3 6.8 %collective-permute-start.11 = (bf16[1,2,4,32,256]{4,3,2,1,0:T(8,128)(2,1)S(1)}, bf16[1,2,4,32,256]{4,3,2,1,0:T(8,128)(2,1)S(1)}, u32[]{:S(2)}, u32[]{:S(2)}) collective-permute-start(bf16[1,2,4,32,256]{4,3,2,1,0:T(8,128)(2,1)S(1)} %get-tuple-element.105), channel_id=1, source_target_pairs={{8,0},{16,8},{24,16},{32,24},{40,32},{48,40},{56,48},{9,1},{17,9},... | collective-permute-start | bytes 393224 | tf_op jit(solution)/shard_map/ppermute | solution.py:20
  78.0 12.8 %copy-start.5 = (bf16[1,2,4,32,256]{4,3,2,1,0:T(8,128)(2,1)}, bf16[1,2,4,32,256]{4,3,2,1,0:T(8,128)(2,1)S(1)}, u32[]{:S(2)}) copy-start(bf16[1,2,4,32,256]{4,3,2,1,0:T(8,128)(2,1)S(1)} %collective-permute-done.10.refs_2_.refs_0_) | copy-start | bytes 393220
  78.1 36.5 %all-to-all-start.1 = ((bf16[64,112,128]{2,1,0:T(8,128)(2,1)}), bf16[64,112,128]{2,1,0:T(8,128)(2,1)S(1)}, u32[]{:S(2)}, u32[]{:S(2)}) async-start(bf16[64,112,128]{2,1,0:T(8,128)(2,1)} %shard_map.74), calls=%async_computation.1 | async-start | bytes 3670016 | tf_op jit(solution)/shard_map/all_to_all | solution.py:459
  90.8 29.1 %collective-permute-start.13 = (bf16[6,2,1,32,256]{4,3,2,1,0:T(8,128)(2,1)S(1)}, bf16[6,2,1,32,256]{4,3,2,1,0:T(8,128)(2,1)S(1)}, u32[]{:S(2)}, u32[]{:S(2)}) collective-permute-start(bf16[6,2,1,32,256]{4,3,2,1,0:T(8,128)(2,1)S(1)} %get-tuple-element.87), channel_id=1, source_target_pairs={{0,1},{1,2},{2,3},{3,4},{4,5},{5,6},{6,7},{8,9},{9,10},{10,11},{11... | collective-permute-start | bytes 589832 | tf_op jit(solution)/shard_map/ppermute | solution.py:28
  93.9 28.2 %collective-permute-start.14 = (bf16[6,2,1,32,256]{4,3,2,1,0:T(8,128)(2,1)S(1)}, bf16[6,2,1,32,256]{4,3,2,1,0:T(8,128)(2,1)S(1)}, u32[]{:S(2)}, u32[]{:S(2)}) collective-permute-start(bf16[6,2,1,32,256]{4,3,2,1,0:T(8,128)(2,1)S(1)} %get-tuple-element.88), channel_id=1, source_target_pairs={{1,0},{2,1},{3,2},{4,3},{5,4},{6,5},{7,6},{9,8},{10,9},{11,10},{12... | collective-permute-start | bytes 589832 | tf_op jit(solution)/shard_map/ppermute | solution.py:28
  97.8 29.1 %collective-permute-start.15 = (bf16[2,256,128]{2,1,0:T(8,128)(2,1)}, bf16[2,256,128]{2,1,0:T(8,128)(2,1)S(1)}, u32[]{:S(2)}, u32[]{:S(2)}) collective-permute-start(bf16[2,256,128]{2,1,0:T(8,128)(2,1)} %get-tuple-element.96), channel_id=1, source_target_pairs={{0,2},{1,3},{2,4},{3,5},{4,6},{5,7},{6,0},{7,1},{8,10},{9,11},{10,... | collective-permute-start | bytes 393224 | tf_op jit(solution)/shard_map/ppermute | solution.py:42
  99.1 27.8 %collective-permute-start.16 = (bf16[2,256,128]{2,1,0:T(8,128)(2,1)}, bf16[2,256,128]{2,1,0:T(8,128)(2,1)S(1)}, u32[]{:S(2)}, u32[]{:S(2)}) collective-permute-start(bf16[2,256,128]{2,1,0:T(8,128)(2,1)} %get-tuple-element.97), channel_id=1, source_target_pairs={{0,4},{1,5},{2,6},{3,7},{4,0},{5,1},{6,2},{7,3},{8,12},{9,13},{10,... | collective-permute-start | bytes 393224 | tf_op jit(solution)/shard_map/ppermute | solution.py:42
  99.8 27.2 %collective-permute-start.17 = (bf16[2,256,128]{2,1,0:T(8,128)(2,1)}, bf16[2,256,128]{2,1,0:T(8,128)(2,1)S(1)}, u32[]{:S(2)}, u32[]{:S(2)}) collective-permute-start(bf16[2,256,128]{2,1,0:T(8,128)(2,1)} %get-tuple-element.98), channel_id=1, source_target_pairs={{0,6},{1,7},{2,0},{3,1},{4,2},{5,3},{6,4},{7,5},{8,14},{9,15},{10,... | collective-permute-start | bytes 393224 | tf_op jit(solution)/shard_map/ppermute | solution.py:42
  122.1 7.1 %collective-permute-start.18 = (f32[112,128]{1,0:T(8,128)S(1)}, f32[112,128]{1,0:T(8,128)S(1)}, u32[]{:S(2)}, u32[]{:S(2)}) collective-permute-start(f32[112,128]{1,0:T(8,128)S(1)} %shard_map.76.refs_1_), channel_id=1, source_target_pairs={{0,64},{64,0},{1,65},{65,1},{2,66},{66,2},{3,67},{67,3},{4,68},{68... | collective-permute-start | bytes 172040 | tf_op jit(solution)/shard_map/ppermute | solution.py:32
  (6 other events, 37.8 us)

commit v5 on v4

--- a/solution.py
+++ b/solution.py
@@ -53,7 +53,7 @@
     return size
 
 
-def call(body, out, scratch=(), far=(), far_out=(), parts=0):
+def call(body, out, scratch=(), far=(), far_out=(), parts=0, parts_out=0):
     outs = list(out) if isinstance(out, tuple) else [out]
 
     def run(*args):
@@ -88,16 +88,26 @@
                 near[len(args) + n] = extra[len(held) + at]
             if not parts:
                 wait(0)
-            given = (wait,) if parts else ()
+            out_pieces = max(parts_out, 1)
+
+            def copy_out(at, piece):
+                n = written[at]
+                size = outs[n].shape[0] // out_pieces
+                rows = pl.ds(piece * size, size)
+                sem = sems.at[len(held) * pieces + at * out_pieces + piece]
+                return pltpu.make_async_copy(near[len(args) + n].at[rows], refs[len(args) + n].at[rows], sem)
+
+            def send(piece):
+                for at in range(len(written)):
+                    copy_out(at, piece).start()
+
+            given = ((wait,) if parts else ()) + ((send,) if parts_out else ())
             body(*near, *extra[len(held) + len(written) : -1], *given)
-            copies = []
-            for at, n in enumerate(written):
-                to = refs[len(args) + n]
-                copies.append(pltpu.make_async_copy(near[len(args) + n], to, sems.at[len(held) * pieces + at]))
-            for copy in copies:
-                copy.start()
-            for copy in copies:
-                copy.wait()
+            if not parts_out:
+                send(0)
+            for piece in range(out_pieces):
+                for at in range(len(written)):
+                    copy_out(at, piece).wait()
 
         rooms = [pltpu.VMEM(args[n].shape, args[n].dtype) for n in held]
         rooms += [pltpu.VMEM(outs[n].shape, outs[n].dtype) for n in written]
@@ -111,7 +121,7 @@
             out_shape=[pltpu.HBM(x.shape, x.dtype) if n in far_out else x for n, x in enumerate(outs)],
             in_specs=specs,
             out_specs=[FAR if n in far_out else FULL for n in range(len(outs))],
-            scratch_shapes=[*rooms, pltpu.SemaphoreType.DMA((len(held) * max(parts, 1) + len(written) + 1,))],
+            scratch_shapes=[*rooms, pltpu.SemaphoreType.DMA((len(held) * max(parts, 1) + len(written) * max(parts_out, 1) + 1,))],
             compiler_params=pltpu.CompilerParams(vmem_limit_bytes=total + (3 << 20)),
         )(*[pltpu.with_memory_space_constraint(x, pltpu.HBM) if n in held else x for n, x in enumerate(args)])
         return result if isinstance(out, tuple) else result[0]
@@ -221,14 +231,16 @@
         outs[d][1] = got[d]
 
 
-def unpack_output_body(place, *refs):
-    out = refs[4]
-    for d in range(4):
-        for n, at in enumerate(blocks_of(place, -1, d)):
-            for s in range(2):
-                rows = refs[d][n, 128 * s : 128 * s + 128, :].astype(F32)
-                for p in range(4):
+def finish_body(core, place, mine, other, *refs):
+    out, grad, send = refs[4:]
+    for p in range(4):
+        for d in range(4):
+            for n, at in enumerate(blocks_of(place, -1, d)):
+                for s in range(2):
+                    rows = refs[d][n, 128 * s : 128 * s + 128, :].astype(F32)
                     out[p, s, pl.ds(at * 4, 4)] = rows[:, 32 * p : 32 * p + 32].reshape(4, 32, 32).astype(BF16)
+        send(p)
+    unpack_grad_body(core, mine, other, grad)
 
 
 def fill_shifts(pieces, target, window):
@@ -478,8 +490,9 @@
         parts=1,
     )(index, left, right, mine, other, inner, edges)
     input_grad, *pieces = lax.optimization_barrier((input_grad, *pieces))
-    output = call(unpack_output_body, shape((4, 2, 32, 32, 32)))(place, *pieces)
-    kernel_grad = call(unpack_grad_body, shape((27, 32, 32), F32))(index, rows, turned_rows)
+    output, kernel_grad = call(
+        finish_body, (shape((4, 2, 32, 32, 32)), shape((27, 32, 32), F32)), far_out=(0,), parts_out=4
+    )(index, place, rows, turned_rows, *pieces)
     return (output, input_grad, kernel_grad.reshape(3, 3, 3, 32, 32))
 
 

time: 132 us -> 130 us (0.985)
    pallas_call x15 -> x14, Pallas kernels: 38.3 us -> 37 us  [run(): pl.pallas_call(kernel, out_shape=[pltpu.HBM(x.shape, x.dtype) if n in far...]
  transfers between devices with their start and end apart: 21 -> 21, of which waited for: 10 -> 10; matrix products, arithmetic and copies ran while one was open for 0% -> 0% of each run, Pallas kernels for 23% -> 21%
where the time goes in v5:
time: 130 us
  starting transfers between devices  58.3 us (45%)
  Pallas kernels  37 us (28%)
  waiting for transfers between devices  31.5 us (24%)
  local copies, waits for them, and re-layouts  1.71 us (1%)
    pallas_call x14, Pallas kernels, run(): pl.pallas_call(kernel, out_shape=[pltpu.HBM(x.shape, x.dtype) if n in far...  37 us
    all_to_all x2, starting transfers between devices, local(): blocks = lax.all_to_all(blocks, GRID, 0, 0, tiled=True)  25.4 us
    all_to_all x2, waiting for transfers between devices, local(): blocks = lax.all_to_all(blocks, GRID, 0, 0, tiled=True)  15.5 us
    ppermute x4, starting transfers between devices, corners(): return (lax.ppermute(last, 'sy', up), lax.ppermute(leading, 'sy', down))  12.4 us
    ppermute x4, waiting for transfers between devices, corners(): return (lax.ppermute(last, 'sy', up), lax.ppermute(leading, 'sy', down))  10.3 us
    ppermute x4, starting transfers between devices, halo(): return (lax.ppermute(last, axis, up), lax.ppermute(leading, axis, down))  8.28 us
    ppermute x6, starting transfers between devices, spread(): lax.ppermute(pieces[d], 'sy', [(i, (i // 2 + d) % 4 * 2 + i % 2) for i in...  7.86 us
    ppermute x4, waiting for transfers between devices, halo(): return (lax.ppermute(last, axis, up), lax.ppermute(leading, axis, down))  2.87 us
  transfers between devices with their start and end apart: 21, of which 10 were waited for; matrix products, arithmetic and copies ran while one was open for 0% of the time, Pallas kernels for 21%

profile of v5, /device:TPU:3, one launch (start us, length us, event | category | flops | bytes accessed | tf_op | source)
XLA Modules:
  0.0 129.8 jit_solution(13500525574312878547)
XLA Ops:
  4.5 3.2 %collective-permute-start = (bf16[1,2,4,32,256]{4,3,2,1,0:T(8,128)(2,1)S(1)}, bf16[1,2,4,32,256]{4,3,2,1,0:T(8,128)(2,1)S(1)}, u32[]{:S(2)}, u32[]{:S(2)}) collective-permute-start(bf16[1,2,4,32,256]{4,3,2,1,0:T(8,128)(2,1)S(1)} %get-tuple-element.112), channel_id=1, source_target_pairs={{0,8},{8,16},{16,24},{24,32},{32,40},{40,48},{48,56},{1,9},{9,17},... | collective-permute-start | bytes 393224 | tf_op jit(solution)/shard_map/ppermute | solution.py:20
  10.6 2.9 %collective-permute-done.1.refs_2_.refs_3_ = bf16[1,2,4,32,256]{4,3,2,1,0:T(8,128)(2,1)S(1)} collective-permute-done((bf16[1,2,4,32,256]{4,3,2,1,0:T(8,128)(2,1)S(1)}, bf16[1,2,4,32,256]{4,3,2,1,0:T(8,128)(2,1)S(1)}, u32[]{:S(2)}, u32[]{:S(2)}) %collective-permute-start.1) | collective-permute-done | bytes 131104 | tf_op jit(solution)/shard_map/ppermute | solution.py:20
  13.5 12.7 %all-to-all-start = ((bf16[64,112,128]{2,1,0:T(8,128)(2,1)}), bf16[64,112,128]{2,1,0:T(8,128)(2,1)}, u32[]{:S(2)}, u32[]{:S(2)}) async-start(bf16[64,112,128]{2,1,0:T(8,128)(2,1)} %shard_map.67), calls=%async_computation | async-start | bytes 3670016 | tf_op jit(solution)/shard_map/all_to_all | solution.py:447
  27.0 3.1 %collective-permute-start.3 = (bf16[6,2,1,32,256]{4,3,2,1,0:T(8,128)(2,1)}, bf16[6,2,1,32,256]{4,3,2,1,0:T(8,128)(2,1)S(1)}, u32[]{:S(2)}, u32[]{:S(2)}) collective-permute-start(bf16[6,2,1,32,256]{4,3,2,1,0:T(8,128)(2,1)} %get-tuple-element.61), channel_id=1, source_target_pairs={{0,1},{1,2},{2,3},{3,4},{4,5},{5,6},{6,7},{8,9},{9,10},{10,11},{11... | collective-permute-start | bytes 589832 | tf_op jit(solution)/shard_map/ppermute | solution.py:28
  30.1 3.1 %collective-permute-start.4 = (bf16[6,2,1,32,256]{4,3,2,1,0:T(8,128)(2,1)}, bf16[6,2,1,32,256]{4,3,2,1,0:T(8,128)(2,1)S(1)}, u32[]{:S(2)}, u32[]{:S(2)}) collective-permute-start(bf16[6,2,1,32,256]{4,3,2,1,0:T(8,128)(2,1)} %get-tuple-element.62), channel_id=1, source_target_pairs={{1,0},{2,1},{3,2},{4,3},{5,4},{6,5},{7,6},{9,8},{10,9},{11,10},{12... | collective-permute-start | bytes 589832 | tf_op jit(solution)/shard_map/ppermute | solution.py:28
  35.9 2.0 %collective-permute-start.7 = (bf16[2,256,128]{2,1,0:T(8,128)(2,1)}, bf16[2,256,128]{2,1,0:T(8,128)(2,1)S(1)}, u32[]{:S(2)}, u32[]{:S(2)}) collective-permute-start(bf16[2,256,128]{2,1,0:T(8,128)(2,1)} %get-tuple-element.68), channel_id=1, source_target_pairs={{0,6},{1,7},{2,0},{3,1},{4,2},{5,3},{6,4},{7,5},{8,14},{9,15},{10,... | collective-permute-start | bytes 393224 | tf_op jit(solution)/shard_map/ppermute | solution.py:42
  37.9 11.2 %all-to-all-done.refs_0_ = bf16[64,112,128]{2,1,0:T(8,128)(2,1)} async-done(((bf16[64,112,128]{2,1,0:T(8,128)(2,1)}), bf16[64,112,128]{2,1,0:T(8,128)(2,1)}, u32[]{:S(2)}, u32[]{:S(2)}) %all-to-all-start) | async-done | bytes 1835040 | tf_op jit(solution)/shard_map/all_to_all | solution.py:447
  49.1 2.7 %shard_map.69.refs_6_.refs_4_.refs_3_ = bf16[14,256,256]{2,1,0:T(8,128)(2,1)S(1)} custom-call(bf16[64,112,128]{2,1,0:T(8,128)(2,1)} %all-to-all-done.refs_0_), custom_call_target="tpu_custom_call" | custom-call | tf_op jit(solution)/shard_map/pallas_call | solution.py:119
  51.8 1.7 %collective-permute-done.6.refs_7_ = bf16[2,256,128]{2,1,0:T(8,128)(2,1)S(1)} collective-permute-done((bf16[2,256,128]{2,1,0:T(8,128)(2,1)}, bf16[2,256,128]{2,1,0:T(8,128)(2,1)S(1)}, u32[]{:S(2)}, u32[]{:S(2)}) %collective-permute-start.6) | collective-permute-done | bytes 131104 | tf_op jit(solution)/shard_map/ppermute | solution.py:42
  55.5 2.0 %collective-permute-done.4.refs_5_ = bf16[6,2,1,32,256]{4,3,2,1,0:T(8,128)(2,1)S(1)} collective-permute-done((bf16[6,2,1,32,256]{4,3,2,1,0:T(8,128)(2,1)}, bf16[6,2,1,32,256]{4,3,2,1,0:T(8,128)(2,1)S(1)}, u32[]{:S(2)}, u32[]{:S(2)}) %collective-permute-start.4) | collective-permute-done | bytes 196640 | tf_op jit(solution)/shard_map/ppermute | solution.py:28
  58.6 3.3 %shard_map.72 = (bf16[6,2,192,768]{3,2,1,0:T(8,128)(2,1)S(1)}, f32[4,256,256]{2,1,0:T(8,128)S(1)}) custom-call(s32[1]{0:T(128)} %bitcast.refs_0_, bf16[4,2,4,32,256]{4,3,2,1,0:T(8,128)(2,1)S(1)} %copy-done.3, bf16[1,2,4,32,256]{4,3,2,1,0:T(8,128)(2,1)S(1)} %collective-permute-done.refs_0_.refs_2_, ...), custom_call_target="tpu_custom_call" | custom-call | tf_op jit(solution)/shard_map/pallas_call | solution.py:119
  62.0 6.0 %shard_map.73 = (bf16[4,2,4,32,256]{4,3,2,1,0:T(8,128)(2,1)S(1)}, bf16[4,256,128]{2,1,0:T(8,128)(2,1)S(1)}, bf16[4,256,128]{2,1,0:T(8,128)(2,1)S(1)}, bf16[14,25...) custom-call(s32[1]{0:T(128)} %bitcast.refs_0_, s32[1]{0:T(128)} %bitcast.1.refs_0_.refs_1_, ...), custom_call_target="tpu_custom_call" | custom-call | tf_op jit(solution)/shard_map/pallas_call | solution.py:119
  68.8 2.5 %collective-permute-start.10 = (bf16[1,2,4,32,256]{4,3,2,1,0:T(8,128)(2,1)S(1)}, bf16[1,2,4,32,256]{4,3,2,1,0:T(8,128)(2,1)S(1)}, u32[]{:S(2)}, u32[]{:S(2)}) collective-permute-start(bf16[1,2,4,32,256]{4,3,2,1,0:T(8,128)(2,1)S(1)} %get-tuple-element.110), channel_id=1, source_target_pairs={{0,8},{8,16},{16,24},{24,32},{32,40},{40,48},{48,56},{1,9},{9,17},... | collective-permute-start | bytes 393224 | tf_op jit(solution)/shard_map/ppermute | solution.py:20
  72.6 5.4 %shard_map.74 = bf16[64,112,128]{2,1,0:T(8,128)(2,1)} custom-call(s32[1]{0:T(128)} %bitcast.refs_0_, bf16[6,2,192,768]{3,2,1,0:T(8,128)(2,1)S(1)} %get-tuple-element.72.refs_2_.refs_1_, bf16[256,1024]{1,0:T(8,128)(2,1)S(1)} %get-tuple-element.78.refs_2_, bf16[14,256,256]{2,1,0:T(8,128)(2,1)S(1)} %collective-permute-done.9.refs_3_), custom_call_target="tpu_custom_call" | custom-call | tf_op jit(solution)/shard_map/pallas_call | solution.py:119
  78.0 12.7 %all-to-all-start.1 = ((bf16[64,112,128]{2,1,0:T(8,128)(2,1)}), bf16[64,112,128]{2,1,0:T(8,128)(2,1)S(1)}, u32[]{:S(2)}, u32[]{:S(2)}) async-start(bf16[64,112,128]{2,1,0:T(8,128)(2,1)} %shard_map.74), calls=%async_computation.1 | async-start | bytes 3670016 | tf_op jit(solution)/shard_map/all_to_all | solution.py:471
  90.8 3.1 %collective-permute-start.13 = (bf16[6,2,1,32,256]{4,3,2,1,0:T(8,128)(2,1)S(1)}, bf16[6,2,1,32,256]{4,3,2,1,0:T(8,128)(2,1)S(1)}, u32[]{:S(2)}, u32[]{:S(2)}) collective-permute-start(bf16[6,2,1,32,256]{4,3,2,1,0:T(8,128)(2,1)S(1)} %get-tuple-element.89), channel_id=1, source_target_pairs={{0,1},{1,2},{2,3},{3,4},{4,5},{5,6},{6,7},{8,9},{9,10},{10,11},{11... | collective-permute-start | bytes 589832 | tf_op jit(solution)/shard_map/ppermute | solution.py:28
  93.9 3.1 %collective-permute-start.14 = (bf16[6,2,1,32,256]{4,3,2,1,0:T(8,128)(2,1)S(1)}, bf16[6,2,1,32,256]{4,3,2,1,0:T(8,128)(2,1)S(1)}, u32[]{:S(2)}, u32[]{:S(2)}) collective-permute-start(bf16[6,2,1,32,256]{4,3,2,1,0:T(8,128)(2,1)S(1)} %get-tuple-element.90), channel_id=1, source_target_pairs={{1,0},{2,1},{3,2},{4,3},{5,4},{6,5},{7,6},{9,8},{10,9},{11,10},{12... | collective-permute-start | bytes 589832 | tf_op jit(solution)/shard_map/ppermute | solution.py:28
  99.8 2.0 %collective-permute-start.18 = (bf16[2,256,128]{2,1,0:T(8,128)(2,1)}, bf16[2,256,128]{2,1,0:T(8,128)(2,1)S(1)}, u32[]{:S(2)}, u32[]{:S(2)}) collective-permute-start(bf16[2,256,128]{2,1,0:T(8,128)(2,1)} %get-tuple-element.101), channel_id=1, source_target_pairs={{0,6},{1,7},{2,0},{3,1},{4,2},{5,3},{6,4},{7,5},{8,14},{9,15},{10,... | collective-permute-start | bytes 393224 | tf_op jit(solution)/shard_map/ppermute | solution.py:42
  101.8 8.5 %shard_map.75 = (bf16[4,2,2,32,256]{4,3,2,1,0:T(8,128)(2,1)}, f32[4,2,2,32,256]{4,3,2,1,0:T(8,128)}) custom-call(s32[1]{0:T(128)} %bitcast.refs_0_, bf16[4,2,4,32,256]{4,3,2,1,0:T(8,128)(2,1)} %copy-done.2, bf16[1,2,4,32,256]{4,3,2,1,0:T(8,128)(2,1)} %copy-done.5, bf16[1,2,4,32,256]{4,3,2,1,0:T(8,128)(2,1)} %copy-done.6, bf16[14,256,256]{2,1,0:T(8,128)(2,1)} %copy-done, ...), custom_call_target="tpu_custom_call" | custom-call | tf_op jit(solution)/shard_map/pallas_call | solution.py:119
  110.3 4.3 %all-to-all-done.1.refs_0_ = bf16[64,112,128]{2,1,0:T(8,128)(2,1)S(1)} async-done(((bf16[64,112,128]{2,1,0:T(8,128)(2,1)}), bf16[64,112,128]{2,1,0:T(8,128)(2,1)S(1)}, u32[]{:S(2)}, u32[]{:S(2)}) %all-to-all-start.1) | async-done | bytes 1835040 | tf_op jit(solution)/shard_map/all_to_all | solution.py:471
  114.8 5.1 %collective-permute-done.13.refs_1_ = bf16[6,2,1,32,256]{4,3,2,1,0:T(8,128)(2,1)S(1)} collective-permute-done((bf16[6,2,1,32,256]{4,3,2,1,0:T(8,128)(2,1)S(1)}, bf16[6,2,1,32,256]{4,3,2,1,0:T(8,128)(2,1)S(1)}, u32[]{:S(2)}, u32[]{:S(2)}) %collective-permute-start.13) | collective-permute-done | bytes 196640 | tf_op jit(solution)/shard_map/ppermute | solution.py:28
  119.9 2.2 %collective-permute-done.14.refs_2_ = bf16[6,2,1,32,256]{4,3,2,1,0:T(8,128)(2,1)S(1)} collective-permute-done((bf16[6,2,1,32,256]{4,3,2,1,0:T(8,128)(2,1)S(1)}, bf16[6,2,1,32,256]{4,3,2,1,0:T(8,128)(2,1)S(1)}, u32[]{:S(2)}, u32[]{:S(2)}) %collective-permute-start.14) | collective-permute-done | bytes 196640 | tf_op jit(solution)/shard_map/ppermute | solution.py:28
  123.0 3.9 %shard_map.78 = bf16[4,2,4,32,256]{4,3,2,1,0:T(8,128)(2,1)} custom-call(s32[1]{0:T(128)} %bitcast.refs_0_, bf16[6,2,1,32,256]{4,3,2,1,0:T(8,128)(2,1)S(1)} %collective-permute-done.13.refs_1_, bf16[6,2,1,32,256]{4,3,2,1,0:T(8,128)(2,1)S(1)} %collective-permute-done.14.refs_2_, bf16[14,256,256]{2,1,0:T(8,128)(2,1)} %copy-done, ...), custom_call_target="tpu_custom_call" | custom-call | tf_op jit(solution)/shard_map/pallas_call | solution.py:119
  127.0 2.7 %shard_map.80 = (bf16[4,2,32,32,32]{4,3,2,1,0:T(8,128)(2,1)}, f32[27,32,32]{2,1,0:T(8,128)}) custom-call(s32[1]{0:T(128)} %bitcast.refs_0_, s32[1]{0:T(128)} %bitcast.1.refs_0_.refs_1_, f32[112,128]{1,0:T(8,128)S(1)} %shard_map.76.refs_2_, f32[112,128]{1,0:T(8,128)S(1)} %collective-permute-done.15.refs_3_, ...), custom_call_target="tpu_custom_call" | custom-call | tf_op jit(solution)/shard_map/pallas_call | solution.py:119
  (54 shorter events, 19.4 us)
Async XLA Ops:
  2.8 10.7 %collective-permute-start.2 = (bf16[4,256,128]{2,1,0:T(8,128)(2,1)S(1)}, bf16[4,256,128]{2,1,0:T(8,128)(2,1)S(1)}, u32[]{:S(2)}, u32[]{:S(2)}) collective-permute-start(bf16[4,256,128]{2,1,0:T(8,128)(2,1)S(1)} %get-tuple-element.57), channel_id=1, source_target_pairs={{0,1},{1,0},{2,3},{3,2},{4,5},{5,4},{6,7},{7,6},{8,9},{9,8},{10,11... | collective-permute-start | bytes 786440 | tf_op jit(solution)/shard_map/ppermute | solution.py:36
  4.5 6.1 %collective-permute-start = (bf16[1,2,4,32,256]{4,3,2,1,0:T(8,128)(2,1)S(1)}, bf16[1,2,4,32,256]{4,3,2,1,0:T(8,128)(2,1)S(1)}, u32[]{:S(2)}, u32[]{:S(2)}) collective-permute-start(bf16[1,2,4,32,256]{4,3,2,1,0:T(8,128)(2,1)S(1)} %get-tuple-element.112), channel_id=1, source_target_pairs={{0,8},{8,16},{16,24},{24,32},{32,40},{40,48},{48,56},{1,9},{9,17},... | collective-permute-start | bytes 393224 | tf_op jit(solution)/shard_map/ppermute | solution.py:20
  7.7 5.7 %collective-permute-start.1 = (bf16[1,2,4,32,256]{4,3,2,1,0:T(8,128)(2,1)S(1)}, bf16[1,2,4,32,256]{4,3,2,1,0:T(8,128)(2,1)S(1)}, u32[]{:S(2)}, u32[]{:S(2)}) collective-permute-start(bf16[1,2,4,32,256]{4,3,2,1,0:T(8,128)(2,1)S(1)} %get-tuple-element.111), channel_id=1, source_target_pairs={{8,0},{16,8},{24,16},{32,24},{40,32},{48,40},{56,48},{9,1},{17,9},... | collective-permute-start | bytes 393224 | tf_op jit(solution)/shard_map/ppermute | solution.py:20
  13.5 35.7 %all-to-all-start = ((bf16[64,112,128]{2,1,0:T(8,128)(2,1)}), bf16[64,112,128]{2,1,0:T(8,128)(2,1)}, u32[]{:S(2)}, u32[]{:S(2)}) async-start(bf16[64,112,128]{2,1,0:T(8,128)(2,1)} %shard_map.67), calls=%async_computation | async-start | bytes 3670016 | tf_op jit(solution)/shard_map/all_to_all | solution.py:447
  27.0 28.6 %collective-permute-start.3 = (bf16[6,2,1,32,256]{4,3,2,1,0:T(8,128)(2,1)}, bf16[6,2,1,32,256]{4,3,2,1,0:T(8,128)(2,1)S(1)}, u32[]{:S(2)}, u32[]{:S(2)}) collective-permute-start(bf16[6,2,1,32,256]{4,3,2,1,0:T(8,128)(2,1)} %get-tuple-element.61), channel_id=1, source_target_pairs={{0,1},{1,2},{2,3},{3,4},{4,5},{5,6},{6,7},{8,9},{9,10},{10,11},{11... | collective-permute-start | bytes 589832 | tf_op jit(solution)/shard_map/ppermute | solution.py:28
  30.1 27.5 %collective-permute-start.4 = (bf16[6,2,1,32,256]{4,3,2,1,0:T(8,128)(2,1)}, bf16[6,2,1,32,256]{4,3,2,1,0:T(8,128)(2,1)S(1)}, u32[]{:S(2)}, u32[]{:S(2)}) collective-permute-start(bf16[6,2,1,32,256]{4,3,2,1,0:T(8,128)(2,1)} %get-tuple-element.62), channel_id=1, source_target_pairs={{1,0},{2,1},{3,2},{4,3},{5,4},{6,5},{7,6},{9,8},{10,9},{11,10},{12... | collective-permute-start | bytes 589832 | tf_op jit(solution)/shard_map/ppermute | solution.py:28
  34.0 17.8 %collective-permute-start.5 = (bf16[2,256,128]{2,1,0:T(8,128)(2,1)}, bf16[2,256,128]{2,1,0:T(8,128)(2,1)S(1)}, u32[]{:S(2)}, u32[]{:S(2)}) collective-permute-start(bf16[2,256,128]{2,1,0:T(8,128)(2,1)} %get-tuple-element.66), channel_id=1, source_target_pairs={{0,2},{1,3},{2,4},{3,5},{4,6},{5,7},{6,0},{7,1},{8,10},{9,11},{10,... | collective-permute-start | bytes 393224 | tf_op jit(solution)/shard_map/ppermute | solution.py:42
  35.2 18.3 %collective-permute-start.6 = (bf16[2,256,128]{2,1,0:T(8,128)(2,1)}, bf16[2,256,128]{2,1,0:T(8,128)(2,1)S(1)}, u32[]{:S(2)}, u32[]{:S(2)}) collective-permute-start(bf16[2,256,128]{2,1,0:T(8,128)(2,1)} %get-tuple-element.67), channel_id=1, source_target_pairs={{0,4},{1,5},{2,6},{3,7},{4,0},{5,1},{6,2},{7,3},{8,12},{9,13},{10,... | collective-permute-start | bytes 393224 | tf_op jit(solution)/shard_map/ppermute | solution.py:42
  35.9 18.6 %collective-permute-start.7 = (bf16[2,256,128]{2,1,0:T(8,128)(2,1)}, bf16[2,256,128]{2,1,0:T(8,128)(2,1)S(1)}, u32[]{:S(2)}, u32[]{:S(2)}) collective-permute-start(bf16[2,256,128]{2,1,0:T(8,128)(2,1)} %get-tuple-element.68), channel_id=1, source_target_pairs={{0,6},{1,7},{2,0},{3,1},{4,2},{5,3},{6,4},{7,5},{8,14},{9,15},{10,... | collective-permute-start | bytes 393224 | tf_op jit(solution)/shard_map/ppermute | solution.py:42
  51.8 16.2 %copy-start = (bf16[14,256,256]{2,1,0:T(8,128)(2,1)}, bf16[14,256,256]{2,1,0:T(8,128)(2,1)S(1)}, u32[]{:S(2)}) copy-start(bf16[14,256,256]{2,1,0:T(8,128)(2,1)S(1)} %shard_map.69.refs_6_.refs_4_.refs_3_) | copy-start | bytes 5505028
  57.5 4.4 %collective-permute-start.8 = (bf16[14,256,256]{2,1,0:T(8,128)(2,1)S(1)}, bf16[14,256,256]{2,1,0:T(8,128)(2,1)S(1)}, u32[]{:S(2)}, u32[]{:S(2)}) collective-permute-start(bf16[14,256,256]{2,1,0:T(8,128)(2,1)S(1)} %shard_map.69.refs_6_.refs_4_.refs_3_), channel_id=1, source_target_pairs={{0,64},{64,0},{1,65},{65,1},{2,66},{66,2},{3,67},{67,3},{4,68},{68... | collective-permute-start | bytes 5505032 | tf_op jit(solution)/shard_map/ppermute | solution.py:32
  68.0 22.8 %copy-start.2 = (bf16[4,2,4,32,256]{4,3,2,1,0:T(8,128)(2,1)}, bf16[4,2,4,32,256]{4,3,2,1,0:T(8,128)(2,1)S(1)}, u32[]{:S(2)}) copy-start(bf16[4,2,4,32,256]{4,3,2,1,0:T(8,128)(2,1)S(1)} %get-tuple-element.80.refs_1_) | copy-start | bytes 1572868
  68.0 4.6 %collective-permute-start.9 = (bf16[14,256,256]{2,1,0:T(8,128)(2,1)S(1)}, bf16[14,256,256]{2,1,0:T(8,128)(2,1)S(1)}, u32[]{:S(2)}, u32[]{:S(2)}) collective-permute-start(bf16[14,256,256]{2,1,0:T(8,128)(2,1)S(1)} %get-tuple-element.79), channel_id=1, source_target_pairs={{0,64},{64,0},{1,65},{65,1},{2,66},{66,2},{3,67},{67,3},{4,68},{68... | collective-permute-start | bytes 5505032 | tf_op jit(solution)/shard_map/ppermute | solution.py:32
  68.3 9.7 %collective-permute-start.12 = (bf16[4,256,128]{2,1,0:T(8,128)(2,1)S(1)}, bf16[4,256,128]{2,1,0:T(8,128)(2,1)S(1)}, u32[]{:S(2)}, u32[]{:S(2)}) collective-permute-start(bf16[4,256,128]{2,1,0:T(8,128)(2,1)S(1)} %get-tuple-element.82), channel_id=1, source_target_pairs={{0,1},{1,0},{2,3},{3,2},{4,5},{5,4},{6,7},{7,6},{8,9},{9,8},{10,11... | collective-permute-start | bytes 786440 | tf_op jit(solution)/shard_map/ppermute | solution.py:36
  68.8 9.2 %collective-permute-start.10 = (bf16[1,2,4,32,256]{4,3,2,1,0:T(8,128)(2,1)S(1)}, bf16[1,2,4,32,256]{4,3,2,1,0:T(8,128)(2,1)S(1)}, u32[]{:S(2)}, u32[]{:S(2)}) collective-permute-start(bf16[1,2,4,32,256]{4,3,2,1,0:T(8,128)(2,1)S(1)} %get-tuple-element.110), channel_id=1, source_target_pairs={{0,8},{8,16},{16,24},{24,32},{32,40},{40,48},{48,56},{1,9},{9,17},... | collective-permute-start | bytes 393224 | tf_op jit(solution)/shard_map/ppermute | solution.py:20
  71.3 6.8 %collective-permute-start.11 = (bf16[1,2,4,32,256]{4,3,2,1,0:T(8,128)(2,1)S(1)}, bf16[1,2,4,32,256]{4,3,2,1,0:T(8,128)(2,1)S(1)}, u32[]{:S(2)}, u32[]{:S(2)}) collective-permute-start(bf16[1,2,4,32,256]{4,3,2,1,0:T(8,128)(2,1)S(1)} %get-tuple-element.109), channel_id=1, source_target_pairs={{8,0},{16,8},{24,16},{32,24},{40,32},{48,40},{56,48},{9,1},{17,9},... | collective-permute-start | bytes 393224 | tf_op jit(solution)/shard_map/ppermute | solution.py:20
  78.0 12.8 %copy-start.5 = (bf16[1,2,4,32,256]{4,3,2,1,0:T(8,128)(2,1)}, bf16[1,2,4,32,256]{4,3,2,1,0:T(8,128)(2,1)S(1)}, u32[]{:S(2)}) copy-start(bf16[1,2,4,32,256]{4,3,2,1,0:T(8,128)(2,1)S(1)} %collective-permute-done.10.refs_2_.refs_0_) | copy-start | bytes 393220
  78.0 36.5 %all-to-all-start.1 = ((bf16[64,112,128]{2,1,0:T(8,128)(2,1)}), bf16[64,112,128]{2,1,0:T(8,128)(2,1)S(1)}, u32[]{:S(2)}, u32[]{:S(2)}) async-start(bf16[64,112,128]{2,1,0:T(8,128)(2,1)} %shard_map.74), calls=%async_computation.1 | async-start | bytes 3670016 | tf_op jit(solution)/shard_map/all_to_all | solution.py:471
  90.8 29.1 %collective-permute-start.13 = (bf16[6,2,1,32,256]{4,3,2,1,0:T(8,128)(2,1)S(1)}, bf16[6,2,1,32,256]{4,3,2,1,0:T(8,128)(2,1)S(1)}, u32[]{:S(2)}, u32[]{:S(2)}) collective-permute-start(bf16[6,2,1,32,256]{4,3,2,1,0:T(8,128)(2,1)S(1)} %get-tuple-element.89), channel_id=1, source_target_pairs={{0,1},{1,2},{2,3},{3,4},{4,5},{5,6},{6,7},{8,9},{9,10},{10,11},{11... | collective-permute-start | bytes 589832 | tf_op jit(solution)/shard_map/ppermute | solution.py:28
  93.9 28.2 %collective-permute-start.14 = (bf16[6,2,1,32,256]{4,3,2,1,0:T(8,128)(2,1)S(1)}, bf16[6,2,1,32,256]{4,3,2,1,0:T(8,128)(2,1)S(1)}, u32[]{:S(2)}, u32[]{:S(2)}) collective-permute-start(bf16[6,2,1,32,256]{4,3,2,1,0:T(8,128)(2,1)S(1)} %get-tuple-element.90), channel_id=1, source_target_pairs={{1,0},{2,1},{3,2},{4,3},{5,4},{6,5},{7,6},{9,8},{10,9},{11,10},{12... | collective-permute-start | bytes 589832 | tf_op jit(solution)/shard_map/ppermute | solution.py:28
  97.9 29.1 %collective-permute-start.16 = (bf16[2,256,128]{2,1,0:T(8,128)(2,1)}, bf16[2,256,128]{2,1,0:T(8,128)(2,1)S(1)}, u32[]{:S(2)}, u32[]{:S(2)}) collective-permute-start(bf16[2,256,128]{2,1,0:T(8,128)(2,1)} %get-tuple-element.99), channel_id=1, source_target_pairs={{0,2},{1,3},{2,4},{3,5},{4,6},{5,7},{6,0},{7,1},{8,10},{9,11},{10,... | collective-permute-start | bytes 393224 | tf_op jit(solution)/shard_map/ppermute | solution.py:42
  99.1 27.8 %collective-permute-start.17 = (bf16[2,256,128]{2,1,0:T(8,128)(2,1)}, bf16[2,256,128]{2,1,0:T(8,128)(2,1)S(1)}, u32[]{:S(2)}, u32[]{:S(2)}) collective-permute-start(bf16[2,256,128]{2,1,0:T(8,128)(2,1)} %get-tuple-element.100), channel_id=1, source_target_pairs={{0,4},{1,5},{2,6},{3,7},{4,0},{5,1},{6,2},{7,3},{8,12},{9,13},{10,... | collective-permute-start | bytes 393224 | tf_op jit(solution)/shard_map/ppermute | solution.py:42
  99.8 27.1 %collective-permute-start.18 = (bf16[2,256,128]{2,1,0:T(8,128)(2,1)}, bf16[2,256,128]{2,1,0:T(8,128)(2,1)S(1)}, u32[]{:S(2)}, u32[]{:S(2)}) collective-permute-start(bf16[2,256,128]{2,1,0:T(8,128)(2,1)} %get-tuple-element.101), channel_id=1, source_target_pairs={{0,6},{1,7},{2,0},{3,1},{4,2},{5,3},{6,4},{7,5},{8,14},{9,15},{10,... | collective-permute-start | bytes 393224 | tf_op jit(solution)/shard_map/ppermute | solution.py:42
  122.1 4.8 %collective-permute-start.15 = (f32[112,128]{1,0:T(8,128)S(1)}, f32[112,128]{1,0:T(8,128)S(1)}, u32[]{:S(2)}, u32[]{:S(2)}) collective-permute-start(f32[112,128]{1,0:T(8,128)S(1)} %shard_map.76.refs_2_), channel_id=1, source_target_pairs={{0,64},{64,0},{1,65},{65,1},{2,66},{66,2},{3,67},{67,3},{4,68},{68... | collective-permute-start | bytes 172040 | tf_op jit(solution)/shard_map/ppermute | solution.py:32
  (6 other events, 37.8 us)
